TPU v7x, 32 devices: a whole 2x2x4 slice. The times are simulated.
32 devices in a mesh: head: 4 (over y, x), vocab: 8 (over z, core).
Axes of the slice: x: 2, y: 2, z: 4, core: 2. Of those that a mesh axis runs over, the one named last changes fastest.
Arguments:
- hidden_rows: bfloat16 [512, 2048], P(('head', 'vocab')), may hold values from -240 to 240
- head_weight: bfloat16 [4, 2048, 16384], P('head', None, 'vocab'), may hold values from -0.125 to 0.125
- teacher_logits: bfloat16 [4, 512, 16384], P('head', 'vocab'), may hold values from -24 to 336
Outputs:
- weight_grad: bfloat16 [4, 2048, 16384], P('head', None, 'vocab')
- input_grad: float32 [512, 2048], P(('head', 'vocab'))
All inputs are finite; a program needn't handle non-finite values.
Results may differ from a plain program's by a relative error of at most 0.004.
Values may be sent and summed in bfloat16 or wider, within the bound.
No kernel may reach another device: no remote copies, remote signals or barrier semaphores. Data moves between devices by JAX's collectives and lax.ppermute only.
A program may use at most 128 MiB of HBM per device.

v0:
```python
import jax
import jax.numpy as jnp
from jax import lax
from jax.sharding import PartitionSpec as P


def merged(value, axis, join):
    pieces = jax.tree.map(lambda part: lax.all_gather(part, axis), value)
    head = jax.tree.map(lambda part: part[0], pieces)
    tail = jax.tree.map(lambda part: part[1:], pieces)
    running, _ = lax.scan(lambda running, section: (join(running, section), None), head, tail)
    return running


def combine_stats(former, latter):
    top_student = jnp.maximum(former[0], latter[0])
    top_teacher = jnp.maximum(former[2], latter[2])
    total_student = former[1] * jnp.exp(former[0] - top_student) + latter[1] * jnp.exp(
        latter[0] - top_student
    )
    total_teacher = former[3] * jnp.exp(former[2] - top_teacher) + latter[3] * jnp.exp(
        latter[2] - top_teacher
    )
    return (top_student, total_student, top_teacher, total_teacher)


def per_device(hidden_rows, head_weight, teacher_logits):
    trunk = lax.all_gather(hidden_rows, ("head", "vocab"), axis=0, tiled=True)
    weight = head_weight[0]
    teacher_tile = lax.all_to_all(teacher_logits, "vocab", split_axis=2, concat_axis=1, tiled=True)
    teacher = teacher_tile[0].astype(jnp.float32)
    student = jnp.dot(trunk, weight, preferred_element_type=jnp.float32)
    local_student = jnp.max(student, axis=1)
    local_teacher = jnp.max(teacher, axis=1)
    local_stats = (
        local_student,
        jnp.sum(jnp.exp(student - local_student[:, None]), axis=1),
        local_teacher,
        jnp.sum(jnp.exp(teacher - local_teacher[:, None]), axis=1),
    )
    top_student, total_student, top_teacher, total_teacher = merged(
        local_stats, "vocab", combine_stats
    )
    student_exp = jnp.exp(student - top_student[:, None])
    teacher_exp = jnp.exp(teacher - top_teacher[:, None])
    student_prob = student_exp / total_student[:, None]
    teacher_prob = teacher_exp / total_teacher[:, None]
    logit_grad = (student_prob - teacher_prob).astype(jnp.bfloat16)
    weight_grad = lax.dot_general(
        trunk, logit_grad, (((0,), (0,)), ((), ())), preferred_element_type=jnp.float32
    )
    weight_grad = weight_grad.astype(jnp.bfloat16)[None]
    input_grad = lax.psum_scatter(
        lax.dot_general(
            logit_grad, weight, (((1,), (1,)), ((), ())), preferred_element_type=jnp.float32
        ),
        ("head", "vocab"),
        scatter_dimension=0,
        tiled=True,
    )
    return (weight_grad, input_grad)


def solution(mesh):
    return jax.shard_map(
        per_device,
        mesh=mesh,
        in_specs=(P(("head", "vocab"), None), P("head", None, "vocab"), P("head", "vocab", None)),
        out_specs=(P("head", None, "vocab"), P(("head", "vocab"), None)),
        check_vma=False,
    )
```

profile of v0, /device:TPU:0, one launch (start us, length us, event | category | flops | bytes accessed | tf_op | source)
XLA Modules:
  0.0 438.3 jit_solution(13313546699832678379)
XLA Ops:
  7.2 17.1 %copy.20 = bf16[1,64,16384]{1,0,2:T(2,128)(2,1)} copy(bf16[1,64,16384]{2,1,0:T(8,128)(2,1)} %param.7) | data formatting | bytes 4194304 | tf_op args[2]
  24.3 0.5 broadcast.8
  24.8 90.7 %reduce.3 = bf16[16384,64]{1,0:T(8,128)(2,1)} reduce(bf16[16384,1,64]{2,1,0:T(2,128)(2,1)} %bitcast.79, bf16[]{:T(256)} %broadcast.8), dimensions={1}, to_apply=%bitcast.56.reduce_sub_computation | reduce | bytes 4194306
  115.6 7.6 %reshape.72 = bf16[8,2,65536]{2,1,0:T(2,128)(2,1)} reshape(bf16[16384,64]{1,0:T(8,128)(2,1)} %reduce.3) | data formatting | bytes 4194304
  123.1 6.4 %all-to-all-start = ((bf16[8,2,65536]{2,1,0:T(2,128)(2,1)}), bf16[8,2,65536]{2,1,0:T(2,128)(2,1)S(1)}, u32[]{:S(2)}, u32[]{:S(2)}) async-start(bf16[8,2,65536]{2,1,0:T(2,128)(2,1)} %reshape.72), calls=%async_computation | async-start | bytes 4194304 | tf_op jit(solution)/shard_map/all_to_all | solution.py:30
  129.5 0.0 all-gather.8.cloned.1.call-start
  129.5 0.7 all-gather.8.cloned.1.call-update
  130.2 0.0 reduce-scatter.2.cloned.1.call-start
  130.3 52.4 %all-to-all-done = bf16[8,2,65536]{2,1,0:T(2,128)(2,1)S(1)} async-done(((bf16[8,2,65536]{2,1,0:T(2,128)(2,1)}), bf16[8,2,65536]{2,1,0:T(2,128)(2,1)S(1)}, u32[]{:S(2)}, u32[]{:S(2)}) %all-to-all-start) | async-done | bytes 2097184 | tf_op jit(solution)/shard_map/all_to_all | solution.py:30
  182.7 5.7 %reshape.73 = bf16[16384,1,64]{2,1,0:T(2,128)(2,1)} reshape(bf16[8,2,65536]{2,1,0:T(2,128)(2,1)S(1)} %all-to-all-done) | data formatting | bytes 4194304
  188.4 16.7 %copy.21 = bf16[1,64,16384]{2,1,0:T(8,128)(2,1)} copy(bf16[1,64,16384]{1,0,2:T(2,128)(2,1)} %bitcast.80) | data formatting | bytes 4194304 | tf_op jit(solution)/shard_map/all_to_all | solution.py:30
  205.0 2.8 copy.30
  207.8 0.4 fusion.9
  208.2 0.1 copy.22
  208.3 0.1 reshape.54
  208.3 12.8 %all-gather.4 = f32[8,1,512]{2,1,0:T(1,128)S(1)} all-gather(f32[1,1,512]{2,1,0:T(1,128)S(1)} %reshape.54), channel_id=1, replica_groups=mesh['head'=4,'vocab'=8] {'vocab'}, dimensions={0}, use_global_device_ids=true | all-gather | bytes 18432 | tf_op jit(solution)/shard_map/all_gather | solution.py:8
  221.1 0.8 exponential_reduce_fusion
  221.9 0.1 copy.23
  222.0 0.1 reshape.56
  222.1 13.0 %all-gather.5 = f32[8,1,512]{2,1,0:T(1,128)S(1)} all-gather(f32[1,1,512]{2,1,0:T(1,128)S(1)} %reshape.56), channel_id=1, replica_groups=mesh['head'=4,'vocab'=8] {'vocab'}, dimensions={0}, use_global_device_ids=true | all-gather | bytes 18432 | tf_op jit(solution)/shard_map/all_gather | solution.py:8
  235.0 0.5 fusion.8
  235.6 4.4 %copy.24 = f32[1,8,64,2048]{3,2,1,0:T(8,128)} copy(f32[1,8,64,2048]{3,1,2,0:T(8,128)S(1)} %fusion.8) | data formatting | bytes 8388608 | tf_op jit(solution)/shard_map/convert_element_type | solution.py:31
  240.0 7.7 %fusion.10 = (f32[512]{0:T(512)S(1)}, f32[512,2048]{1,0:T(8,128)S(1)}) fusion(bf16[512,2048]{1,0:T(8,128)(2,1)} %all-gather.8.cloned.1.call-done, bf16[1,2048,2048]{2,1,0:T(8,128)(2,1)} %param.6), kind=kOutput, calls=%fused_computation.25 | convolution fusion | flops 4296015360 | bytes 14682112 | tf_op jit(solution)/shard_map/dot_general | solution.py:32
  247.8 12.9 %all-gather.2 = f32[8,1,512]{2,1,0:T(1,128)S(1)} all-gather(f32[1,1,512]{2,1,0:T(1,128)S(1)} %bitcast.97), channel_id=2, replica_groups=mesh['head'=4,'vocab'=8] {'vocab'}, dimensions={0}, use_global_device_ids=true | all-gather | bytes 18432 | tf_op jit(solution)/shard_map/all_gather | solution.py:8
  260.7 0.7 exponential_reduce_fusion.1
  261.4 12.8 %all-gather.3 = f32[8,1,512]{2,1,0:T(1,128)S(1)} all-gather(f32[1,1,512]{2,1,0:T(1,128)S(1)} %bitcast.98), channel_id=3, replica_groups=mesh['head'=4,'vocab'=8] {'vocab'}, dimensions={0}, use_global_device_ids=true | all-gather | bytes 18432 | tf_op jit(solution)/shard_map/all_gather | solution.py:8
  274.2 0.8 while.16
  275.0 4.3 fusion.7
  279.3 9.4 %fusion = f32[512,2048]{1,0:T(8,128)} fusion(bf16[512,2048]{1,0:T(8,128)(2,1)S(1)} %fusion.7, bf16[1,2048,2048]{2,1,0:T(8,128)(2,1)} %param.6), kind=kOutput, calls=%fused_computation.6 | convolution fusion | flops 4294967296 | bytes 14680064 | tf_op jit(solution)/shard_map/dot_general | solution.py:54
  288.8 8.4 %convert_bitcast_fusion = bf16[1,2048,2048]{1,2,0:T(8,128)(2,1)} fusion(bf16[512,2048]{1,0:T(8,128)(2,1)S(1)} %fusion.7, bf16[512,2048]{1,0:T(8,128)(2,1)} %all-gather.8.cloned.1.call-done), kind=kOutput, calls=%fused_computation.10 | convolution fusion | flops 4299161600 | bytes 12582912 | tf_op jit(solution)/shard_map/dot_general | solution.py:49
  297.2 12.2 %copy.25 = bf16[1,2048,2048]{2,1,0:T(8,128)(2,1)} copy(bf16[1,2048,2048]{1,2,0:T(8,128)(2,1)} %convert_bitcast_fusion) | data formatting | bytes 16777216
  309.4 122.1 %reduce-scatter.2.cloned.1.call-done = f32[16,2048]{1,0:T(8,128)} async-done(((f32[512,2048]{1,0:T(8,128)}), f32[16,2048]{1,0:T(8,128)}) %reduce-scatter.2.cloned.1.call-update) | async-done | bytes 131088 | tf_op jit(solution)/shard_map/reduce_scatter | solution.py:53
  (58 shorter events, 0.5 us)
Async XLA Ops:
  123.1 59.5 %all-to-all-start = ((bf16[8,2,65536]{2,1,0:T(2,128)(2,1)}), bf16[8,2,65536]{2,1,0:T(2,128)(2,1)S(1)}, u32[]{:S(2)}, u32[]{:S(2)}) async-start(bf16[8,2,65536]{2,1,0:T(2,128)(2,1)} %reshape.72), calls=%async_computation | async-start | bytes 4194304 | tf_op jit(solution)/shard_map/all_to_all | solution.py:30
  129.5 110.6 %all-gather.8.cloned.1.call-start = ((), (), s32[]{:S(2)}) async-start(), calls=%async_computation.2 | async-start | bytes 2162688 | tf_op jit(solution)/shard_map/all_gather | solution.py:28
  130.2 301.3 %reduce-scatter.2.cloned.1.call-start = ((), (), s32[]{:S(2)}) async-start(), calls=%async_computation.3 | async-start | bytes 4325376 | tf_op jit(solution)/shard_map/reduce_scatter | solution.py:53
  221.1 14.5 %copy-start.1 = (f32[8,1,512]{2,1,0:T(1,128)}, f32[8,1,512]{2,1,0:T(1,128)S(1)}, u32[]{:S(2)}) copy-start(f32[8,1,512]{2,1,0:T(1,128)S(1)} %all-gather.4) | copy-start | bytes 49156
  235.0 5.0 %copy-start.2 = (f32[8,1,512]{2,1,0:T(1,128)}, f32[8,1,512]{2,1,0:T(1,128)S(1)}, u32[]{:S(2)}) copy-start(f32[8,1,512]{2,1,0:T(1,128)S(1)} %all-gather.5) | copy-start | bytes 49156
  247.8 12.9 %copy-start = (f32[512,2048]{1,0:T(8,128)}, f32[512,2048]{1,0:T(8,128)S(1)}, u32[]{:S(2)}) copy-start(f32[512,2048]{1,0:T(8,128)S(1)} %get-tuple-element.91) | copy-start | bytes 12582916
  247.8 26.4 %slice-start = ((f32[8,1,512]{2,1,0:T(1,128)}), f32[1,1,512]{2,1,0:T(1,128)S(1)}, s32[]{:S(2)}) async-start(f32[8,1,512]{2,1,0:T(1,128)} %copy-done.1), calls=%async_computation.4 | async-start | bytes 4096 | tf_op jit(solution)/shard_map/slice | solution.py:9
  247.8 26.4 %slice-start.1 = ((f32[8,1,512]{2,1,0:T(1,128)}), f32[1,1,512]{2,1,0:T(1,128)S(1)}, s32[]{:S(2)}) async-start(f32[8,1,512]{2,1,0:T(1,128)} %copy-done.2), calls=%async_computation.5 | async-start | bytes 4096 | tf_op jit(solution)/shard_map/slice | solution.py:9
Sparse Core Ops, SparseCore 0:
  133.3 69.2 all-gather.7
  288.9 142.5 reduce-scatter.1
where the time goes:
time: 440 us; the launch traced here: 438 us
  waiting for transfers between devices  175 us (40%)
  other arithmetic  97.6 us (22%)
  local copies, waits for them, and re-layouts  67.7 us (15%)
  blocking collectives  51.4 us (12%)
  matrix products  25.5 us (6%)
  between operations  14.1 us (3%)
  starting transfers between devices  6.43 us (1%)
    reduce_scatter x1, waiting for transfers between devices, per_device(): lax.psum_scatter(lax.dot_general(logit_grad, weight, (((1,), (1,)), ((),...  122 us
    unnamed x1, other arithmetic  90.7 us
    all_to_all x1, waiting for transfers between devices, per_device(): lax.all_to_all(teacher_logits, 'vocab', split_axis=2, concat_axis=1, tile...  52.4 us
    all_gather x4, blocking collectives, merged(): pieces = jax.tree.map(lambda part: lax.all_gather(part, axis), value)  51.4 us
    unnamed x18, local copies, waits for them, and re-layouts  46.1 us
    all_to_all x1, local copies, waits for them, and re-layouts, per_device(): lax.all_to_all(teacher_logits, 'vocab', split_axis=2, concat_axis=1, tile...  16.7 us
    dot_general x1, matrix products, per_device(): lax.dot_general(logit_grad, weight, (((1,), (1,)), ((), ())), preferred_e...  9.45 us
  transfers between devices with their start and end apart: 3, of which 2 were waited for; matrix products, arithmetic and copies ran while one was open for 12% of the time, Pallas kernels for 0%

commit v1 on v0

v1 whole, which is shorter than its diff:
```python
import functools

import jax
import jax.numpy as jnp
from jax import lax
from jax.experimental import pallas as pl
from jax.experimental.pallas import tpu as pltpu
from jax.sharding import PartitionSpec as P


F32 = jnp.float32
BF16 = jnp.bfloat16
LANES = 128
NT = (((1,), (1,)), ((), ()))
TN = (((0,), (0,)), ((), ()))
MIB = 1024 * 1024


def params(nbytes):
    return pltpu.CompilerParams(vmem_limit_bytes=nbytes + 4 * MIB)


def cost(flops, nbytes):
    return pl.CostEstimate(flops=flops, bytes_accessed=nbytes, transcendentals=0)


WHOLE = pl.BlockSpec(memory_space=pltpu.VMEM)


def teacher_stats(teacher):
    x = teacher[0].astype(F32)
    top = jnp.max(x, axis=1)
    return jnp.stack([top, jnp.sum(jnp.exp(x - top[:, None]), axis=1)])


def stack_kernel(*refs):
    rows = refs[0].shape[0]
    for i, ref in enumerate(refs[:-1]):
        refs[-1][i * rows : (i + 1) * rows, :] = ref[...]


def stacked(parts):
    rows, cols = parts[0].shape
    shape = jax.ShapeDtypeStruct((rows * len(parts), cols), parts[0].dtype)
    nbytes = shape.size * shape.dtype.itemsize
    return pl.pallas_call(
        stack_kernel,
        in_specs=[WHOLE] * len(parts),
        out_specs=WHOLE,
        out_shape=shape,
        compiler_params=params(2 * nbytes),
        cost_estimate=cost(0, 2 * nbytes),
    )(*parts)


def student_kernel(pieces, tile, *refs):
    parts, (w_ref, t_ref, e_ref, h_ref, stat_ref, cols_sc) = refs[:pieces], refs[pieces:]
    rows = parts[0].shape[0]
    for i, part in enumerate(parts):
        h_ref[i * rows : (i + 1) * rows, :] = part[...]

    @pl.loop(0, w_ref.shape[1] // tile)
    def _(j):
        at = pl.ds(pl.multiple_of(j * tile, tile), tile)
        e_ref[:, at] = jnp.dot(h_ref[...], w_ref[:, at], preferred_element_type=F32)

    step = 8
    lane = lax.broadcasted_iota(jnp.int32, (step, LANES), 1)

    def body(i, _):
        at = pl.ds(pl.multiple_of(i * step, step), step)
        x = e_ref[at, :]
        top = jnp.max(x, axis=1, keepdims=True)
        e = jnp.exp(x - top)
        e_ref[at, :] = e
        total = jnp.sum(e, axis=1, keepdims=True)
        cols_sc[at, :] = jnp.where(lane == 0, top, jnp.where(lane == 1, total, 0.0))
        return _

    lax.fori_loop(0, e_ref.shape[0] // step, body, 0, unroll=4)
    stat_ref[...] = cols_sc[...].T[:8, :]
    stat_ref[2:4, : t_ref.shape[1]] = t_ref[...]


def student(parts, weight, tstat, tile):
    depth, cols = weight.shape
    rows = sum(p.shape[0] for p in parts)
    return pl.pallas_call(
        functools.partial(student_kernel, len(parts), tile),
        in_specs=[WHOLE] * (len(parts) + 2),
        out_specs=[WHOLE] * 3,
        out_shape=[
            jax.ShapeDtypeStruct((rows, cols), F32),
            jax.ShapeDtypeStruct((rows, depth), BF16),
            jax.ShapeDtypeStruct((8, rows), F32),
        ],
        scratch_shapes=[pltpu.VMEM((rows, LANES), F32)],
        compiler_params=params(2 * depth * cols + 8 * rows * cols + 4 * rows * depth),
        cost_estimate=cost(2 * rows * cols * depth, 2 * depth * cols + 4 * rows * cols),
        name="student",
    )(*parts, weight, tstat)


def swap_groups(x, size, lanes):
    lane = lax.broadcasted_iota(jnp.int32, x.shape, 1)
    return jnp.where((lane // size) % 2 == 0, pltpu.roll(x, lanes - size, 1), pltpu.roll(x, size, 1))


def logit_grad_kernel(place, n_stats, tile, ids, *refs):
    stats = refs[:n_stats]
    teachers = refs[n_stats : n_stats + place.nv]
    e_ref, g_ref, cols_sc = refs[n_stats + place.nv :]
    rows = g_ref.shape[0]
    half = rows // 2
    me = ids[0] * place.nv + ids[1]

    tops, totals, teacher = [], [], []
    for zk, ref in enumerate(stats):
        for ck in range(2):
            x = ref[8 * ck : 8 * ck + 8, :]
            teacher.append(x[2:4, : rows // place.nv])
            if ck:
                x = jnp.concatenate([x[:, half:], x[:, :half]], axis=1)
            bit = 1
            while bit < place.nz:
                if zk & bit:
                    x = swap_groups(x, bit * place.group, rows)
                bit *= 2
            tops.append(x[0:1])
            totals.append(x[1:2])
    top = functools.reduce(jnp.maximum, tops)
    total = sum(t * jnp.exp(m - top) for m, t in zip(tops, totals))
    scale = jnp.exp(tops[0] - top) / total
    teacher = jnp.concatenate(teacher, axis=1)
    packed = jnp.concatenate(
        [scale, teacher[0:1], 1.0 / teacher[1:2], jnp.zeros((LANES - 3, rows), F32)], axis=0
    )
    cols_sc[...] = packed.T

    @pl.loop(0, g_ref.shape[1] // tile)
    def _(j):
        across = pl.ds(pl.multiple_of(j * tile, tile), tile)
        for i, t_ref in enumerate(teachers):
            step, ck = divmod(i, 2)
            per = t_ref.shape[0] // place.group
            source = ids[2 + step] * 2 + jnp.bitwise_xor(jnp.bitwise_and(ids[1], 1), ck)
            vk = jnp.bitwise_xor(source, ids[1])
            for sub in range(per):
                can = source * per + sub
                to = place.position(jnp.bitwise_xor(me, can)) * place.group
                to = pl.ds(pl.multiple_of(to, place.group), place.group)
                c = cols_sc[to, :]
                at = pl.multiple_of((vk * per + sub) * place.group, place.group)
                d = cols_sc[pl.ds(at, place.group), :]
                t = t_ref[sub * place.group : (sub + 1) * place.group, across].astype(F32)
                q = jnp.exp(t - d[:, 1:2]) * d[:, 2:3]
                g_ref[to, across] = (e_ref[to, across] * c[:, 0:1] - q).astype(BF16)


def logit_grad(place, ids, stats, teachers, e, tile):
    rows, cols = e.shape
    return pl.pallas_call(
        functools.partial(logit_grad_kernel, place, len(stats), tile),
        in_specs=[pl.BlockSpec(memory_space=pltpu.SMEM)]
        + [WHOLE] * (len(stats) + len(teachers) + 1),
        out_specs=WHOLE,
        out_shape=jax.ShapeDtypeStruct((rows, cols), BF16),
        scratch_shapes=[pltpu.VMEM((rows, LANES), F32)],
        compiler_params=params(8 * rows * cols + 4 * LANES * rows),
        cost_estimate=cost(8 * rows * cols, 8 * rows * cols),
        name="logit_grad",
    )(ids, *stats, *teachers, e)


def input_grad_kernel(start, tile, g_ref, w_ref, keep_ref, send_ref):
    half = g_ref.shape[0] // 2

    @pl.loop(0, keep_ref.shape[1] // tile)
    def _(j):
        at = pl.ds(pl.multiple_of(j * tile, tile), tile)
        w = w_ref[pl.ds(pl.multiple_of(start + j * tile, tile), tile), :]
        out = lax.dot_general(g_ref[...], w, NT, preferred_element_type=F32)
        keep_ref[:, at] = out[:half]
        send_ref[:, at] = out[half:].astype(BF16)


def input_grad_part(g, weight, start, width, tile):
    rows, cols = g.shape
    return pl.pallas_call(
        functools.partial(input_grad_kernel, start, tile),
        in_specs=[WHOLE] * 2,
        out_specs=[WHOLE] * 2,
        out_shape=[
            jax.ShapeDtypeStruct((rows // 2, width), F32),
            jax.ShapeDtypeStruct((rows // 2, width), BF16),
        ],
        compiler_params=params(2 * rows * cols + 2 * weight.size + 3 * rows * width),
        cost_estimate=cost(2 * rows * cols * width, 2 * cols * (rows + width)),
        name="input_grad",
    )(g, weight)


def weight_grad_kernel(h_ref, g_ref, *refs):
    o_ref = refs[-1]
    o_ref[0] = lax.dot_general(h_ref[...], g_ref[...], TN, preferred_element_type=F32).astype(BF16)


def weight_grad_part(h, g, before, part, parts, tile):
    rows, depth = h.shape
    cols = g.shape[1]
    steps = cols // parts // tile
    start = part * steps
    extra = [] if before is None else [before]
    return pl.pallas_call(
        weight_grad_kernel,
        grid=(steps,),
        in_specs=[
            pl.BlockSpec((rows, depth), lambda j: (0, 0)),
            pl.BlockSpec((rows, tile), lambda j: (0, start + j)),
        ]
        + [pl.BlockSpec(memory_space=pl.ANY)] * len(extra),
        out_specs=pl.BlockSpec((1, depth, tile), lambda j: (0, 0, start + j)),
        out_shape=jax.ShapeDtypeStruct((1, depth, cols), BF16),
        input_output_aliases={2: 0} if extra else {},
        compiler_params=params(4 * depth * rows + 4 * rows * tile + 8 * depth * tile),
        cost_estimate=cost(2 * rows * cols * depth // parts, 2 * depth * cols // parts),
        name="weight_grad",
    )(h, g, *extra)


class Place:
    def __init__(self, nh, nv, group):
        self.nh, self.nv, self.nz, self.group = nh, nv, nv // 2, group

    def bits(self, r):
        ck, rest = divmod(r, self.nh * self.nz)
        hk, zk = divmod(rest, self.nz)
        return hk * self.nv + zk * 2 + ck

    def position(self, d):
        hk, vk = d // self.nv, d % self.nv
        zk, ck = vk // 2, vk % 2
        return (ck * self.nh + hk) * self.nz + zk


def swap(x, axis, size, k):
    return lax.ppermute(x, axis, [(i, i ^ k) for i in range(size)])


def coded(i):
    return i ^ (i >> 1)


def shifted(z, nz, step):
    place, rest = z, z >> 1
    bits = nz
    while bits > 2:
        place, rest, bits = place ^ rest, rest >> 1, bits // 2
    return coded((place + step) % nz)


def relative(nh, nv, hidden, weight, teacher):
    place = Place(nh, nv, hidden.shape[0])
    nz = place.nz
    v = lax.axis_index("vocab")
    z, core = v // 2, v % 2
    sources = [shifted(z, nz, nz - step) for step in range(nz)]
    ids = jnp.stack([lax.axis_index("head"), v] + sources).astype(jnp.int32)
    cols = weight.shape[2]

    near = [hidden] + [None] * (nz - 1)
    for k in range(nz - 1, 0, -1):
        near[k] = swap(hidden, "vocab", nv, 2 * k)

    def piece(step, ck):
        to = shifted(z, nz, step) * 2 + (core ^ ck)
        return lax.dynamic_slice(teacher, (0, 0, to * cols), (1, teacher.shape[1], cols))[0]

    def move(x, step):
        pairs = [(2 * i + c, 2 * shifted(i, nz, step) + c) for i in range(nz) for c in range(2)]
        return lax.ppermute(x, "vocab", pairs)

    blocks = []
    pieces = lax.optimization_barrier(
        tuple((piece(step, 0), piece(step, 1)) for step in range(nz))
    )
    for step in range(nz):
        mine, cross = pieces[step]
        cross = swap(cross, "vocab", nv, 1)
        if step:
            mine = move(mine, step)
            cross = move(cross, step)
        blocks += [mine, cross]

    block = stacked(near)
    own = [block]
    for k in range(1, nh):
        own.append(swap(block, "head", nh, k))
    other = []
    for k in range(nh):
        other.append(swap(own[k], "vocab", nv, 1))

    e, h, stat = student(own + other, weight[0], teacher_stats(teacher), 512)
    pair = swap(stat, "vocab", nv, 1)
    pair = stacked([stat, pair])
    stats = [pair]
    for k in range(1, nz):
        stats.append(swap(pair, "vocab", nv, 2 * k))
    g = logit_grad(place, ids, stats, blocks, e, 1024)

    depth = weight.shape[1]
    chunks = 2
    width = depth // chunks
    rows = place.group * nz
    sums = []
    for c in range(chunks):
        keep, send = input_grad_part(g, weight[0], c * width, width, 512)
        send = swap(send, "vocab", nv, 1)
        keep = keep + send.astype(F32)
        part = [keep[k * rows : (k + 1) * rows] for k in range(nh)]
        total = part[0]
        for k in range(1, nh):
            part[k] = swap(part[k].astype(BF16), "head", nh, k)
            total = total + part[k].astype(F32)
        part = [total[k * place.group : (k + 1) * place.group] for k in range(nz)]
        total = part[0]
        for k in range(1, nz):
            part[k] = swap(part[k].astype(BF16), "vocab", nv, 2 * k)
            total = total + part[k].astype(F32)
        sums.append(total)
    grad = None
    for part in range(PARTS):
        grad = weight_grad_part(h, g, grad, part, PARTS, 512)
    return (grad, jnp.concatenate(sums, axis=1))


PARTS = 4


def gathered(hidden, weight, teacher):
    trunk = lax.all_gather(hidden, ("head", "vocab"), axis=0, tiled=True)
    weight = weight[0]
    teacher = lax.all_to_all(teacher, "vocab", split_axis=2, concat_axis=1, tiled=True)[0]
    teacher = teacher.astype(F32)
    s = jnp.dot(trunk, weight, preferred_element_type=F32)
    tops = [jnp.max(x, axis=1) for x in (s, teacher)]
    totals = [jnp.sum(jnp.exp(x - m[:, None]), axis=1) for x, m in zip((s, teacher), tops)]
    stat = lax.all_gather(jnp.stack(tops + totals), "vocab")
    prob = []
    for i, x in enumerate((s, teacher)):
        top = jnp.max(stat[:, i], axis=0)
        total = jnp.sum(stat[:, i + 2] * jnp.exp(stat[:, i] - top), axis=0)
        prob.append(jnp.exp(x - top[:, None]) / total[:, None])
    g = (prob[0] - prob[1]).astype(BF16)
    grad = lax.dot_general(trunk, g, TN, preferred_element_type=F32).astype(BF16)[None]
    back = lax.dot_general(g, weight, NT, preferred_element_type=F32)
    return (grad, lax.psum_scatter(back, ("head", "vocab"), scatter_dimension=0, tiled=True))


def per_device(nh, nv, plain, hidden, weight, teacher):
    if plain:
        return gathered(hidden, weight, teacher)
    return relative(nh, nv, hidden, weight, teacher)


def solution(mesh):
    nh, nv = mesh.shape["head"], mesh.shape["vocab"]

    def step(hidden, weight, teacher):
        group = hidden.shape[0] // (nh * nv)
        plain = nh & (nh - 1) or nv & (nv - 1) or group % 16
        run = jax.shard_map(
            functools.partial(per_device, nh, nv, plain),
            mesh=mesh,
            in_specs=(P(("head", "vocab"), None), P("head", None, "vocab"), P("head", "vocab", None)),
            out_specs=(P("head", None, "vocab"), P(("head", "vocab"), None)),
            check_vma=False,
        )
        return run(hidden, weight, teacher)

    return step
```

time: 440 us -> 126 us (0.29)
  waiting for transfers between devices: 175 us -> 31.3 us
  other arithmetic: 97.6 us -> 5.63 us
  blocking collectives: 51.4 us -> 0 us
  local copies, waits for them, and re-layouts: 67.7 us -> 16.5 us
  starting transfers between devices: 6.43 us -> 39.9 us
  Pallas kernels: 0 us -> 31.5 us
  matrix products: 25.5 us -> 0 us
  between operations: 14.1 us -> 0.88 us
    reduce_scatter x1 -> x0, waiting for transfers between devices: 122 us -> none  [per_device(): lax.psum_scatter(lax.dot_general(logit_grad, weight, (((1,), (1,)), ((),...]
    unnamed x1 -> x0, other arithmetic: 90.7 us -> none
    all_to_all x1 -> x0, waiting for transfers between devices: 52.4 us -> none  [per_device(): lax.all_to_all(teacher_logits, 'vocab', split_axis=2, concat_axis=1, tile...]
    all_gather x4 -> x0, blocking collectives: 51.4 us -> none  [merged(): pieces = jax.tree.map(lambda part: lax.all_gather(part, axis), value)]
    ppermute x0 -> x38, starting transfers between devices: none -> 39.9 us  [the longest x32 30.7 us: swap(): return lax.ppermute(x, axis, [(i, i ^ k) for i in range(size)])]
    unnamed x18 -> x30, local copies, waits for them, and re-layouts: 46.1 us -> 13.8 us
    pallas_call x0 -> x10, Pallas kernels: none -> 31.5 us  [the longest x1 13.1 us: student(): pl.pallas_call(functools.partial(student_kernel, len(parts), tile), in_sp...]
    ppermute x0 -> x38, waiting for transfers between devices: none -> 31.3 us  [the longest x32 23.9 us: swap(): return lax.ppermute(x, axis, [(i, i ^ k) for i in range(size)])]
  transfers between devices with their start and end apart: 3 -> 38, of which waited for: 2 -> 15; matrix products, arithmetic and copies ran while one was open for 12% -> 6% of each run, Pallas kernels for 0% -> 21%
where the time goes in v1:
time: 126 us
  starting transfers between devices  39.9 us (32%)
  Pallas kernels  31.5 us (25%)
  waiting for transfers between devices  31.3 us (25%)
  local copies, waits for them, and re-layouts  16.5 us (13%)
  other arithmetic  5.63 us (4%)
    ppermute x32, starting transfers between devices, swap(): return lax.ppermute(x, axis, [(i, i ^ k) for i in range(size)])  30.7 us
    ppermute x32, waiting for transfers between devices, swap(): return lax.ppermute(x, axis, [(i, i ^ k) for i in range(size)])  23.9 us
    unnamed x30, local copies, waits for them, and re-layouts  13.8 us
    pallas_call x1, Pallas kernels, student(): pl.pallas_call(functools.partial(student_kernel, len(parts), tile), in_sp...  13.1 us
    pallas_call x4, Pallas kernels, weight_grad_part(): pl.pallas_call(weight_grad_kernel, grid=(steps,), in_specs=[pl.BlockSpec(...  10.4 us
    ppermute x6, starting transfers between devices, move(): return lax.ppermute(x, 'vocab', pairs)  9.21 us
    ppermute x6, waiting for transfers between devices, move(): return lax.ppermute(x, 'vocab', pairs)  7.47 us
    pallas_call x2, Pallas kernels, input_grad_part(): pl.pallas_call(functools.partial(input_grad_kernel, start, tile), in_spec...  5.13 us
  transfers between devices with their start and end apart: 38, of which 15 were waited for; matrix products, arithmetic and copies ran while one was open for 6% of the time, Pallas kernels for 21%

profile of v1, /device:TPU:0, one launch (start us, length us, event | category | flops | bytes accessed | tf_op | source)
XLA Modules:
  0.0 125.7 jit_solution(16749042109096996381)
XLA Ops:
  0.6 3.1 %collective-permute-start = (bf16[16,2048]{1,0:T(8,128)(2,1)}, bf16[16,2048]{1,0:T(8,128)(2,1)S(1)}, u32[]{:S(2)}, u32[]{:S(2)}) collective-permute-start(bf16[16,2048]{1,0:T(8,128)(2,1)} %refs_0_.1), channel_id=1, source_target_pairs={{0,2},{1,3},{2,0},{3,1},{4,6},{5,7},{6,4},{7,5},{8,10},{9,11},{10,... | collective-permute-start | bytes 196616 | tf_op jit(solution)/shard_map/ppermute | solution.py:247
  3.8 2.6 %collective-permute-start.1 = (bf16[16,2048]{1,0:T(8,128)(2,1)}, bf16[16,2048]{1,0:T(8,128)(2,1)S(1)}, u32[]{:S(2)}, u32[]{:S(2)}) collective-permute-start(bf16[16,2048]{1,0:T(8,128)(2,1)} %refs_0_.1), channel_id=1, source_target_pairs={{0,4},{1,5},{2,6},{3,7},{4,0},{5,1},{6,2},{7,3},{8,12},{9,13},{10,... | collective-permute-start | bytes 196616 | tf_op jit(solution)/shard_map/ppermute | solution.py:247
  6.3 2.6 %dynamic-slice_bitcast_fusion = (bf16[64,2048]{1,0:T(8,128)(2,1)}, bf16[64,2048]{1,0:T(8,128)(2,1)}, bf16[64,2048]{1,0:T(8,128)(2,1)}, bf16[64,2048]{1,0:T(8,128...) fusion(bf16[1,64,16384]{2,1,0:T(8,128)(2,1)} %param.5, ...), kind=kLoop, calls=%fused_computation.11 | loop fusion | bytes 4194336 | tf_op jit(solution)/shard_map/squeeze | solution.py:277
  16.2 2.0 %reduce_max.18 = bf16[64]{0:T(256)(128)(2,1)S(1)} reduce(bf16[1,64,16384]{2,1,0:T(8,128)(2,1)} %param.5, bf16[]{:T(256)} %constant.72.clone.1), dimensions={0,2}, to_apply=%region_0.1 | reduce | flops 1048512 | bytes 2097282 | tf_op jit(solution)/shard_map/reduce_max | solution.py:32
  18.8 3.1 %collective-permute-done.3.refs_1_ = bf16[64,2048]{1,0:T(8,128)(2,1)S(1)} collective-permute-done((bf16[64,2048]{1,0:T(8,128)(2,1)S(1)}, bf16[64,2048]{1,0:T(8,128)(2,1)S(1)}, u32[]{:S(2)}, u32[]{:S(2)}) %collective-permute-start.3) | collective-permute-done | bytes 262176 | tf_op jit(solution)/shard_map/ppermute | solution.py:247
  21.9 4.1 %collective-permute-done.4.refs_2_ = bf16[64,2048]{1,0:T(8,128)(2,1)S(1)} collective-permute-done((bf16[64,2048]{1,0:T(8,128)(2,1)S(1)}, bf16[64,2048]{1,0:T(8,128)(2,1)S(1)}, u32[]{:S(2)}, u32[]{:S(2)}) %collective-permute-start.4) | collective-permute-done | bytes 262176 | tf_op jit(solution)/shard_map/ppermute | solution.py:247
  26.5 2.4 %fusion.1 = f32[64]{0:T(128)S(1)} fusion(bf16[1,64,16384]{2,1,0:T(8,128)(2,1)} %param.5, f32[64]{0:T(128)S(1)} %get-tuple-element.61), kind=kLoop, calls=%fused_computation.2 | loop fusion | flops 3145664 | bytes 2097664 | tf_op jit(solution)/shard_map/reduce_sum | solution.py:33
  29.0 2.5 %collective-permute-start.18 = (bf16[64,2048]{1,0:T(8,128)(2,1)}, bf16[64,2048]{1,0:T(8,128)(2,1)S(1)}, u32[]{:S(2)}, u32[]{:S(2)}) collective-permute-start(bf16[64,2048]{1,0:T(8,128)(2,1)} %get-tuple-element.23), channel_id=1, source_target_pairs={{0,6},{1,7},{2,4},{3,5},{4,2},{5,3},{6,0},{7,1},{8,14},{9,15},{10,... | collective-permute-start | bytes 786440 | tf_op jit(solution)/shard_map/ppermute | solution.py:281
  31.5 1.8 %collective-permute-start.21 = (bf16[64,2048]{1,0:T(8,128)(2,1)}, bf16[64,2048]{1,0:T(8,128)(2,1)S(1)}, u32[]{:S(2)}, u32[]{:S(2)}) collective-permute-start(bf16[64,2048]{1,0:T(8,128)(2,1)} %get-tuple-element.25), channel_id=1, source_target_pairs={{0,4},{1,5},{2,0},{3,1},{4,6},{5,7},{6,2},{7,3},{8,12},{9,13},{10,... | collective-permute-start | bytes 786440 | tf_op jit(solution)/shard_map/ppermute | solution.py:281
  33.8 3.4 %copy-done = bf16[1,2048,2048]{2,1,0:T(8,128)(2,1)S(1)} copy-done((bf16[1,2048,2048]{2,1,0:T(8,128)(2,1)S(1)}, bf16[1,2048,2048]{2,1,0:T(8,128)(2,1)}, u32[]{:S(2)}) %copy-start) | copy-done | bytes 8388632
  40.9 13.1 %student.1 = (f32[512,2048]{1,0:T(8,128)S(1)}, bf16[512,2048]{1,0:T(8,128)(2,1)S(1)}, f32[8,512]{1,0:T(8,128)S(1)}) custom-call(bf16[64,2048]{1,0:T(8,128)(2,1)S(1)} %copy-done.7, bf16[64,2048]{1,0:T(8,128)(2,1)S(1)} %copy-done.10, bf16[64,2048]{1,0:T(8,128)(2,1)S(1)} %copy-done.12, bf16[64,2048]{1,0:T(8,128)(2,1)S(1)} %copy-done.14, ...), custom_call_target="tpu_custom_call" | custom-call | flops 4294967296 | bytes 12582912 | tf_op jit(solution)/shard_map/student/pallas_call | solution.py:88
  54.0 2.0 %copy-done.2 = f32[512,2048]{1,0:T(8,128)} copy-done((f32[512,2048]{1,0:T(8,128)}, f32[512,2048]{1,0:T(8,128)S(1)}, u32[]{:S(2)}) %copy-start.2) | copy-done | bytes 4194328
  57.6 2.2 %collective-permute-start.23 = (bf16[64,2048]{1,0:T(8,128)(2,1)}, bf16[64,2048]{1,0:T(8,128)(2,1)}, u32[]{:S(2)}, u32[]{:S(2)}) collective-permute-start(bf16[64,2048]{1,0:T(8,128)(2,1)} %collective-permute-done.22), channel_id=1, source_target_pairs={{0,4},{1,5},{2,0},{3,1},{4,6},{5,7},{6,2},{7,3},{8,12},{9,13},{10,... | collective-permute-start | bytes 786440 | tf_op jit(solution)/shard_map/ppermute | solution.py:281
  59.9 2.4 %collective-permute-start.12 = (f32[16,512]{1,0:T(8,128)S(1)}, f32[16,512]{1,0:T(8,128)S(1)}, u32[]{:S(2)}, u32[]{:S(2)}) collective-permute-start(f32[16,512]{1,0:T(8,128)S(1)} %shard_map.51.refs_0_), channel_id=1, source_target_pairs={{0,4},{1,5},{2,6},{3,7},{4,0},{5,1},{6,2},{7,3},{8,12},{9,13},{10,... | collective-permute-start | bytes 98312 | tf_op jit(solution)/shard_map/ppermute | solution.py:247
  63.0 2.0 %collective-permute-start.13 = (f32[16,512]{1,0:T(8,128)S(1)}, f32[16,512]{1,0:T(8,128)S(1)}, u32[]{:S(2)}, u32[]{:S(2)}) collective-permute-start(f32[16,512]{1,0:T(8,128)S(1)} %shard_map.51.refs_0_), channel_id=1, source_target_pairs={{0,6},{1,7},{2,4},{3,5},{4,2},{5,3},{6,0},{7,1},{8,14},{9,15},{10,... | collective-permute-start | bytes 98312 | tf_op jit(solution)/shard_map/ppermute | solution.py:247
  65.0 2.5 %collective-permute-done.20.refs_9_ = bf16[64,2048]{1,0:T(8,128)(2,1)} collective-permute-done((bf16[64,2048]{1,0:T(8,128)(2,1)}, bf16[64,2048]{1,0:T(8,128)(2,1)}, u32[]{:S(2)}, u32[]{:S(2)}) %collective-permute-start.20) | collective-permute-done | bytes 262176 | tf_op jit(solution)/shard_map/ppermute | solution.py:281
  67.5 4.8 %collective-permute-done.23.refs_11_ = bf16[64,2048]{1,0:T(8,128)(2,1)} collective-permute-done((bf16[64,2048]{1,0:T(8,128)(2,1)}, bf16[64,2048]{1,0:T(8,128)(2,1)}, u32[]{:S(2)}, u32[]{:S(2)}) %collective-permute-start.23) | collective-permute-done | bytes 262176 | tf_op jit(solution)/shard_map/ppermute | solution.py:281
  72.5 7.0 %collective-permute-done.12.refs_2_ = f32[16,512]{1,0:T(8,128)S(1)} collective-permute-done((f32[16,512]{1,0:T(8,128)S(1)}, f32[16,512]{1,0:T(8,128)S(1)}, u32[]{:S(2)}, u32[]{:S(2)}) %collective-permute-start.12) | collective-permute-done | bytes 32800 | tf_op jit(solution)/shard_map/ppermute | solution.py:247
  79.6 2.2 %copy-done.3 = f32[512,2048]{1,0:T(8,128)S(1)} copy-done((f32[512,2048]{1,0:T(8,128)S(1)}, f32[512,2048]{1,0:T(8,128)}, u32[]{:S(2)}) %copy-start.3) | copy-done | bytes 4194328
  82.7 2.8 %logit_grad.1.g_ref = bf16[512,2048]{1,0:T(8,128)(2,1)S(1)} custom-call(s32[6]{0:T(128)S(1)} %stack.36.ids, f32[16,512]{1,0:T(8,128)S(1)} %shard_map.51.refs_0_, f32[16,512]{1,0:T(8,128)S(1)} %collective-permute-done.11.refs_1_, f32[16,512]{1,0:T(8,128)S(1)} %collective-permute-done.12.refs_2_, f32[16,512]{1,0:T(8,128)S(1)} %collective-permute-done.13.refs_3_, ...), custom_call_target="tpu_custom_call" | custom-call | flops 8388608 | bytes 8388608 | tf_op jit(solution)/shard_map/logit_grad/pallas_call | solution.py:162
  86.2 2.6 %input_grad.3 = (f32[256,1024]{1,0:T(8,128)S(1)}, bf16[256,1024]{1,0:T(8,128)(2,1)S(1)}) custom-call(bf16[512,2048]{1,0:T(8,128)(2,1)S(1)} %logit_grad.1.g_ref, bf16[2048,2048]{1,0:T(8,128)(2,1)S(1)} %bitcast.30), custom_call_target="tpu_custom_call" | custom-call | flops 2147483648 | bytes 6291456 | tf_op jit(solution)/shard_map/input_grad/pallas_call | solution.py:189
  88.9 2.6 %input_grad.2 = (f32[256,1024]{1,0:T(8,128)S(1)}, bf16[256,1024]{1,0:T(8,128)(2,1)S(1)}) custom-call(bf16[512,2048]{1,0:T(8,128)(2,1)S(1)} %logit_grad.1.g_ref, bf16[2048,2048]{1,0:T(8,128)(2,1)S(1)} %bitcast.31), custom_call_target="tpu_custom_call" | custom-call | flops 2147483648 | bytes 6291456 | tf_op jit(solution)/shard_map/input_grad/pallas_call | solution.py:189
  92.0 2.6 %weight_grad.4.refs_0_ = bf16[1,2048,2048]{2,1,0:T(8,128)(2,1)} custom-call(bf16[512,2048]{1,0:T(8,128)(2,1)S(1)} %get-tuple-element.17.h_ref, bf16[512,2048]{1,0:T(8,128)(2,1)S(1)} %logit_grad.1.g_ref), custom_call_target="tpu_custom_call" | custom-call | flops 1073741824 | bytes 2097152 | tf_op jit(solution)/shard_map/weight_grad/pallas_call | solution.py:214
  94.6 2.6 %weight_grad.5.refs_0_ = bf16[1,2048,2048]{2,1,0:T(8,128)(2,1)} custom-call(bf16[512,2048]{1,0:T(8,128)(2,1)S(1)} %get-tuple-element.17.h_ref, bf16[512,2048]{1,0:T(8,128)(2,1)S(1)} %logit_grad.1.g_ref, bf16[1,2048,2048]{2,1,0:T(8,128)(2,1)} %weight_grad.4.refs_0_), custom_call_target="tpu_custom_call", output_to_operand_aliasing={{}: (2, {})} | custom-call | flops 1073741824 | bytes 2097152 | tf_op jit(solution)/shard_map/weight_grad/pallas_call | solution.py:214
  97.3 2.6 %weight_grad.6.refs_0_ = bf16[1,2048,2048]{2,1,0:T(8,128)(2,1)} custom-call(bf16[512,2048]{1,0:T(8,128)(2,1)S(1)} %get-tuple-element.17.h_ref, bf16[512,2048]{1,0:T(8,128)(2,1)S(1)} %logit_grad.1.g_ref, bf16[1,2048,2048]{2,1,0:T(8,128)(2,1)} %weight_grad.5.refs_0_), custom_call_target="tpu_custom_call", output_to_operand_aliasing={{}: (2, {})} | custom-call | flops 1073741824 | bytes 2097152 | tf_op jit(solution)/shard_map/weight_grad/pallas_call | solution.py:214
  99.9 2.6 %weight_grad.7 = bf16[1,2048,2048]{2,1,0:T(8,128)(2,1)} custom-call(bf16[512,2048]{1,0:T(8,128)(2,1)S(1)} %get-tuple-element.17.h_ref, bf16[512,2048]{1,0:T(8,128)(2,1)S(1)} %logit_grad.1.g_ref, bf16[1,2048,2048]{2,1,0:T(8,128)(2,1)} %weight_grad.6.refs_0_), custom_call_target="tpu_custom_call", output_to_operand_aliasing={{}: (2, {})} | custom-call | flops 1073741824 | bytes 2097152 | tf_op jit(solution)/shard_map/weight_grad/pallas_call | solution.py:214
  102.7 1.6 %collective-permute-start.34 = (bf16[64,1024]{1,0:T(8,128)(2,1)S(1)}, bf16[64,1024]{1,0:T(8,128)(2,1)S(1)}, u32[]{:S(2)}, u32[]{:S(2)}) collective-permute-start(bf16[64,1024]{1,0:T(8,128)(2,1)S(1)} %get-tuple-element.52), channel_id=1, source_target_pairs={{0,24},{8,16},{16,8},{24,0},{1,25},{9,17},{17,9},{25,1},{2,26},{10... | collective-permute-start | bytes 393224 | tf_op jit(solution)/shard_map/ppermute | solution.py:247
  110.7 2.3 %collective-permute-done.33 = bf16[64,1024]{1,0:T(8,128)(2,1)S(1)} collective-permute-done((bf16[64,1024]{1,0:T(8,128)(2,1)S(1)}, bf16[64,1024]{1,0:T(8,128)(2,1)S(1)}, u32[]{:S(2)}, u32[]{:S(2)}) %collective-permute-start.33) | collective-permute-done | bytes 131104 | tf_op jit(solution)/shard_map/ppermute | solution.py:247
  113.1 2.2 %collective-permute-start.37 = (bf16[16,1024]{1,0:T(8,128)(2,1)S(1)}, bf16[16,1024]{1,0:T(8,128)(2,1)S(1)}, u32[]{:S(2)}, u32[]{:S(2)}) collective-permute-start(bf16[16,1024]{1,0:T(8,128)(2,1)S(1)} %get-tuple-element.58), channel_id=1, source_target_pairs={{0,6},{1,7},{2,4},{3,5},{4,2},{5,3},{6,0},{7,1},{8,14},{9,15},{10,... | collective-permute-start | bytes 98312 | tf_op jit(solution)/shard_map/ppermute | solution.py:247
  115.7 1.8 %collective-permute-start.35 = (bf16[16,1024]{1,0:T(8,128)(2,1)S(1)}, bf16[16,1024]{1,0:T(8,128)(2,1)S(1)}, u32[]{:S(2)}, u32[]{:S(2)}) collective-permute-start(bf16[16,1024]{1,0:T(8,128)(2,1)S(1)} %get-tuple-element.57), channel_id=1, source_target_pairs={{0,2},{1,3},{2,0},{3,1},{4,6},{5,7},{6,4},{7,5},{8,10},{9,11},{10,... | collective-permute-start | bytes 98312 | tf_op jit(solution)/shard_map/ppermute | solution.py:247
  117.7 2.2 %collective-permute-start.30 = (bf16[16,1024]{1,0:T(8,128)(2,1)S(1)}, bf16[16,1024]{1,0:T(8,128)(2,1)S(1)}, u32[]{:S(2)}, u32[]{:S(2)}) collective-permute-start(bf16[16,1024]{1,0:T(8,128)(2,1)S(1)} %get-tuple-element.55), channel_id=1, source_target_pairs={{0,6},{1,7},{2,4},{3,5},{4,2},{5,3},{6,0},{7,1},{8,14},{9,15},{10,... | collective-permute-start | bytes 98312 | tf_op jit(solution)/shard_map/ppermute | solution.py:247
  120.2 2.0 %collective-permute-start.28 = (bf16[16,1024]{1,0:T(8,128)(2,1)S(1)}, bf16[16,1024]{1,0:T(8,128)(2,1)S(1)}, u32[]{:S(2)}, u32[]{:S(2)}) collective-permute-start(bf16[16,1024]{1,0:T(8,128)(2,1)S(1)} %get-tuple-element.54), channel_id=1, source_target_pairs={{0,2},{1,3},{2,0},{3,1},{4,6},{5,7},{6,4},{7,5},{8,10},{9,11},{10,... | collective-permute-start | bytes 98312 | tf_op jit(solution)/shard_map/ppermute | solution.py:247
  (101 shorter events, 28.8 us)
Async XLA Ops:
  0.6 9.2 %collective-permute-start = (bf16[16,2048]{1,0:T(8,128)(2,1)}, bf16[16,2048]{1,0:T(8,128)(2,1)S(1)}, u32[]{:S(2)}, u32[]{:S(2)}) collective-permute-start(bf16[16,2048]{1,0:T(8,128)(2,1)} %refs_0_.1), channel_id=1, source_target_pairs={{0,2},{1,3},{2,0},{3,1},{4,6},{5,7},{6,4},{7,5},{8,10},{9,11},{10,... | collective-permute-start | bytes 196616 | tf_op jit(solution)/shard_map/ppermute | solution.py:247
  3.8 7.5 %collective-permute-start.1 = (bf16[16,2048]{1,0:T(8,128)(2,1)}, bf16[16,2048]{1,0:T(8,128)(2,1)S(1)}, u32[]{:S(2)}, u32[]{:S(2)}) collective-permute-start(bf16[16,2048]{1,0:T(8,128)(2,1)} %refs_0_.1), channel_id=1, source_target_pairs={{0,4},{1,5},{2,6},{3,7},{4,0},{5,1},{6,2},{7,3},{8,12},{9,13},{10,... | collective-permute-start | bytes 196616 | tf_op jit(solution)/shard_map/ppermute | solution.py:247
  8.9 9.3 %collective-permute-start.14 = (bf16[64,2048]{1,0:T(8,128)(2,1)S(1)}, bf16[64,2048]{1,0:T(8,128)(2,1)S(1)}, u32[]{:S(2)}, u32[]{:S(2)}) collective-permute-start(bf16[64,2048]{1,0:T(8,128)(2,1)S(1)} %get-tuple-element.20), channel_id=1, source_target_pairs={{0,1},{1,0},{2,3},{3,2},{4,5},{5,4},{6,7},{7,6},{8,9},{9,8},{10,11... | collective-permute-start | bytes 786440 | tf_op jit(solution)/shard_map/ppermute | solution.py:247
  8.9 9.6 %collective-permute-start.15 = (bf16[64,2048]{1,0:T(8,128)(2,1)S(1)}, bf16[64,2048]{1,0:T(8,128)(2,1)S(1)}, u32[]{:S(2)}, u32[]{:S(2)}) collective-permute-start(bf16[64,2048]{1,0:T(8,128)(2,1)S(1)} %get-tuple-element.21), channel_id=1, source_target_pairs={{0,2},{1,3},{2,6},{3,7},{4,0},{5,1},{6,4},{7,5},{8,10},{9,11},{10,... | collective-permute-start | bytes 786440 | tf_op jit(solution)/shard_map/ppermute | solution.py:281
  12.7 9.2 %collective-permute-start.3 = (bf16[64,2048]{1,0:T(8,128)(2,1)S(1)}, bf16[64,2048]{1,0:T(8,128)(2,1)S(1)}, u32[]{:S(2)}, u32[]{:S(2)}) collective-permute-start(bf16[64,2048]{1,0:T(8,128)(2,1)S(1)} %shard_map.50.refs_0_), channel_id=1, source_target_pairs={{0,8},{8,0},{16,24},{24,16},{1,9},{9,1},{17,25},{25,17},{2,10},{10... | collective-permute-start | bytes 786440 | tf_op jit(solution)/shard_map/ppermute | solution.py:247
  14.2 11.8 %collective-permute-start.4 = (bf16[64,2048]{1,0:T(8,128)(2,1)S(1)}, bf16[64,2048]{1,0:T(8,128)(2,1)S(1)}, u32[]{:S(2)}, u32[]{:S(2)}) collective-permute-start(bf16[64,2048]{1,0:T(8,128)(2,1)S(1)} %shard_map.50.refs_0_), channel_id=1, source_target_pairs={{0,16},{8,24},{16,0},{24,8},{1,17},{9,25},{17,1},{25,9},{2,18},{10... | collective-permute-start | bytes 786440 | tf_op jit(solution)/shard_map/ppermute | solution.py:247
  15.8 10.2 %collective-permute-start.5 = (bf16[64,2048]{1,0:T(8,128)(2,1)S(1)}, bf16[64,2048]{1,0:T(8,128)(2,1)S(1)}, u32[]{:S(2)}, u32[]{:S(2)}) collective-permute-start(bf16[64,2048]{1,0:T(8,128)(2,1)S(1)} %shard_map.50.refs_0_), channel_id=1, source_target_pairs={{0,24},{8,16},{16,8},{24,0},{1,25},{9,17},{17,9},{25,1},{2,26},{10... | collective-permute-start | bytes 786440 | tf_op jit(solution)/shard_map/ppermute | solution.py:247
  18.2 10.7 %collective-permute-start.16 = (bf16[64,2048]{1,0:T(8,128)(2,1)S(1)}, bf16[64,2048]{1,0:T(8,128)(2,1)S(1)}, u32[]{:S(2)}, u32[]{:S(2)}) collective-permute-start(bf16[64,2048]{1,0:T(8,128)(2,1)S(1)} %get-tuple-element.22), channel_id=1, source_target_pairs={{0,1},{1,0},{2,3},{3,2},{4,5},{5,4},{6,7},{7,6},{8,9},{9,8},{10,11... | collective-permute-start | bytes 786440 | tf_op jit(solution)/shard_map/ppermute | solution.py:247
  18.5 12.9 %collective-permute-start.6 = (bf16[64,2048]{1,0:T(8,128)(2,1)S(1)}, bf16[64,2048]{1,0:T(8,128)(2,1)S(1)}, u32[]{:S(2)}, u32[]{:S(2)}) collective-permute-start(bf16[64,2048]{1,0:T(8,128)(2,1)S(1)} %shard_map.50.refs_0_), channel_id=1, source_target_pairs={{0,1},{1,0},{2,3},{3,2},{4,5},{5,4},{6,7},{7,6},{8,9},{9,8},{10,11... | collective-permute-start | bytes 786440 | tf_op jit(solution)/shard_map/ppermute | solution.py:247
  21.9 9.5 %collective-permute-start.7 = (bf16[64,2048]{1,0:T(8,128)(2,1)S(1)}, bf16[64,2048]{1,0:T(8,128)(2,1)S(1)}, u32[]{:S(2)}, u32[]{:S(2)}) collective-permute-start(bf16[64,2048]{1,0:T(8,128)(2,1)S(1)} %collective-permute-done.3.refs_1_), channel_id=1, source_target_pairs={{0,1},{1,0},{2,3},{3,2},{4,5},{5,4},{6,7},{7,6},{8,9},{9,8},{10,11... | collective-permute-start | bytes 786440 | tf_op jit(solution)/shard_map/ppermute | solution.py:247
  26.0 7.3 %collective-permute-start.8 = (bf16[64,2048]{1,0:T(8,128)(2,1)S(1)}, bf16[64,2048]{1,0:T(8,128)(2,1)S(1)}, u32[]{:S(2)}, u32[]{:S(2)}) collective-permute-start(bf16[64,2048]{1,0:T(8,128)(2,1)S(1)} %collective-permute-done.4.refs_2_), channel_id=1, source_target_pairs={{0,1},{1,0},{2,3},{3,2},{4,5},{5,4},{6,7},{7,6},{8,9},{9,8},{10,11... | collective-permute-start | bytes 786440 | tf_op jit(solution)/shard_map/ppermute | solution.py:247
  26.0 7.4 %collective-permute-start.9 = (bf16[64,2048]{1,0:T(8,128)(2,1)S(1)}, bf16[64,2048]{1,0:T(8,128)(2,1)S(1)}, u32[]{:S(2)}, u32[]{:S(2)}) collective-permute-start(bf16[64,2048]{1,0:T(8,128)(2,1)S(1)} %collective-permute-done.5.refs_3_), channel_id=1, source_target_pairs={{0,1},{1,0},{2,3},{3,2},{4,5},{5,4},{6,7},{7,6},{8,9},{9,8},{10,11... | collective-permute-start | bytes 786440 | tf_op jit(solution)/shard_map/ppermute | solution.py:247
  29.0 30.9 %collective-permute-start.18 = (bf16[64,2048]{1,0:T(8,128)(2,1)}, bf16[64,2048]{1,0:T(8,128)(2,1)S(1)}, u32[]{:S(2)}, u32[]{:S(2)}) collective-permute-start(bf16[64,2048]{1,0:T(8,128)(2,1)} %get-tuple-element.23), channel_id=1, source_target_pairs={{0,6},{1,7},{2,4},{3,5},{4,2},{5,3},{6,0},{7,1},{8,14},{9,15},{10,... | collective-permute-start | bytes 786440 | tf_op jit(solution)/shard_map/ppermute | solution.py:281
  31.5 24.6 %collective-permute-start.19 = (bf16[64,2048]{1,0:T(8,128)(2,1)}, bf16[64,2048]{1,0:T(8,128)(2,1)}, u32[]{:S(2)}, u32[]{:S(2)}) collective-permute-start(bf16[64,2048]{1,0:T(8,128)(2,1)} %get-tuple-element.24), channel_id=1, source_target_pairs={{0,1},{1,0},{2,3},{3,2},{4,5},{5,4},{6,7},{7,6},{8,9},{9,8},{10,11... | collective-permute-start | bytes 786440 | tf_op jit(solution)/shard_map/ppermute | solution.py:247
  31.5 28.4 %collective-permute-start.21 = (bf16[64,2048]{1,0:T(8,128)(2,1)}, bf16[64,2048]{1,0:T(8,128)(2,1)S(1)}, u32[]{:S(2)}, u32[]{:S(2)}) collective-permute-start(bf16[64,2048]{1,0:T(8,128)(2,1)} %get-tuple-element.25), channel_id=1, source_target_pairs={{0,4},{1,5},{2,0},{3,1},{4,6},{5,7},{6,2},{7,3},{8,12},{9,13},{10,... | collective-permute-start | bytes 786440 | tf_op jit(solution)/shard_map/ppermute | solution.py:281
  33.3 22.8 %collective-permute-start.22 = (bf16[64,2048]{1,0:T(8,128)(2,1)}, bf16[64,2048]{1,0:T(8,128)(2,1)}, u32[]{:S(2)}, u32[]{:S(2)}) collective-permute-start(bf16[64,2048]{1,0:T(8,128)(2,1)} %get-tuple-element.26), channel_id=1, source_target_pairs={{0,1},{1,0},{2,3},{3,2},{4,5},{5,4},{6,7},{7,6},{8,9},{9,8},{10,11... | collective-permute-start | bytes 786440 | tf_op jit(solution)/shard_map/ppermute | solution.py:247
  33.4 28.8 %collective-permute-start.17 = (bf16[64,2048]{1,0:T(8,128)(2,1)S(1)}, bf16[64,2048]{1,0:T(8,128)(2,1)S(1)}, u32[]{:S(2)}, u32[]{:S(2)}) collective-permute-start(bf16[64,2048]{1,0:T(8,128)(2,1)S(1)} %collective-permute-done.16), channel_id=1, source_target_pairs={{0,2},{1,3},{2,6},{3,7},{4,0},{5,1},{6,4},{7,5},{8,10},{9,11},{10,... | collective-permute-start | bytes 786440 | tf_op jit(solution)/shard_map/ppermute | solution.py:281
  56.1 11.4 %collective-permute-start.20 = (bf16[64,2048]{1,0:T(8,128)(2,1)}, bf16[64,2048]{1,0:T(8,128)(2,1)}, u32[]{:S(2)}, u32[]{:S(2)}) collective-permute-start(bf16[64,2048]{1,0:T(8,128)(2,1)} %collective-permute-done.19), channel_id=1, source_target_pairs={{0,6},{1,7},{2,4},{3,5},{4,2},{5,3},{6,0},{7,1},{8,14},{9,15},{10,... | collective-permute-start | bytes 786440 | tf_op jit(solution)/shard_map/ppermute | solution.py:281
  57.6 14.7 %collective-permute-start.23 = (bf16[64,2048]{1,0:T(8,128)(2,1)}, bf16[64,2048]{1,0:T(8,128)(2,1)}, u32[]{:S(2)}, u32[]{:S(2)}) collective-permute-start(bf16[64,2048]{1,0:T(8,128)(2,1)} %collective-permute-done.22), channel_id=1, source_target_pairs={{0,4},{1,5},{2,0},{3,1},{4,6},{5,7},{6,2},{7,3},{8,12},{9,13},{10,... | collective-permute-start | bytes 786440 | tf_op jit(solution)/shard_map/ppermute | solution.py:281
  59.9 12.7 %collective-permute-start.11 = (f32[16,512]{1,0:T(8,128)S(1)}, f32[16,512]{1,0:T(8,128)S(1)}, u32[]{:S(2)}, u32[]{:S(2)}) collective-permute-start(f32[16,512]{1,0:T(8,128)S(1)} %shard_map.51.refs_0_), channel_id=1, source_target_pairs={{0,2},{1,3},{2,0},{3,1},{4,6},{5,7},{6,4},{7,5},{8,10},{9,11},{10,... | collective-permute-start | bytes 98312 | tf_op jit(solution)/shard_map/ppermute | solution.py:247
  59.9 19.7 %collective-permute-start.12 = (f32[16,512]{1,0:T(8,128)S(1)}, f32[16,512]{1,0:T(8,128)S(1)}, u32[]{:S(2)}, u32[]{:S(2)}) collective-permute-start(f32[16,512]{1,0:T(8,128)S(1)} %shard_map.51.refs_0_), channel_id=1, source_target_pairs={{0,4},{1,5},{2,6},{3,7},{4,0},{5,1},{6,2},{7,3},{8,12},{9,13},{10,... | collective-permute-start | bytes 98312 | tf_op jit(solution)/shard_map/ppermute | solution.py:247
  63.0 16.6 %collective-permute-start.13 = (f32[16,512]{1,0:T(8,128)S(1)}, f32[16,512]{1,0:T(8,128)S(1)}, u32[]{:S(2)}, u32[]{:S(2)}) collective-permute-start(f32[16,512]{1,0:T(8,128)S(1)} %shard_map.51.refs_0_), channel_id=1, source_target_pairs={{0,6},{1,7},{2,4},{3,5},{4,2},{5,3},{6,0},{7,1},{8,14},{9,15},{10,... | collective-permute-start | bytes 98312 | tf_op jit(solution)/shard_map/ppermute | solution.py:247
  88.8 13.7 %collective-permute-start.31 = (bf16[256,1024]{1,0:T(8,128)(2,1)S(1)}, bf16[256,1024]{1,0:T(8,128)(2,1)S(1)}, u32[]{:S(2)}, u32[]{:S(2)}) collective-permute-start(bf16[256,1024]{1,0:T(8,128)(2,1)S(1)} %get-tuple-element.31), channel_id=1, source_target_pairs={{0,1},{1,0},{2,3},{3,2},{4,5},{5,4},{6,7},{7,6},{8,9},{9,8},{10,11... | collective-permute-start | bytes 1572872 | tf_op jit(solution)/shard_map/ppermute | solution.py:247
  91.5 14.8 %collective-permute-start.24 = (bf16[256,1024]{1,0:T(8,128)(2,1)S(1)}, bf16[256,1024]{1,0:T(8,128)(2,1)S(1)}, u32[]{:S(2)}, u32[]{:S(2)}) collective-permute-start(bf16[256,1024]{1,0:T(8,128)(2,1)S(1)} %get-tuple-element.29), channel_id=1, source_target_pairs={{0,1},{1,0},{2,3},{3,2},{4,5},{5,4},{6,7},{7,6},{8,9},{9,8},{10,11... | collective-permute-start | bytes 1572872 | tf_op jit(solution)/shard_map/ppermute | solution.py:247
  102.7 7.3 %collective-permute-start.34 = (bf16[64,1024]{1,0:T(8,128)(2,1)S(1)}, bf16[64,1024]{1,0:T(8,128)(2,1)S(1)}, u32[]{:S(2)}, u32[]{:S(2)}) collective-permute-start(bf16[64,1024]{1,0:T(8,128)(2,1)S(1)} %get-tuple-element.52), channel_id=1, source_target_pairs={{0,24},{8,16},{16,8},{24,0},{1,25},{9,17},{17,9},{25,1},{2,26},{10... | collective-permute-start | bytes 393224 | tf_op jit(solution)/shard_map/ppermute | solution.py:247
  104.3 8.7 %collective-permute-start.33 = (bf16[64,1024]{1,0:T(8,128)(2,1)S(1)}, bf16[64,1024]{1,0:T(8,128)(2,1)S(1)}, u32[]{:S(2)}, u32[]{:S(2)}) collective-permute-start(bf16[64,1024]{1,0:T(8,128)(2,1)S(1)} %get-tuple-element.53), channel_id=1, source_target_pairs={{0,16},{8,24},{16,0},{24,8},{1,17},{9,25},{17,1},{25,9},{2,18},{10... | collective-permute-start | bytes 393224 | tf_op jit(solution)/shard_map/ppermute | solution.py:247
  105.1 7.9 %collective-permute-start.32 = (bf16[64,1024]{1,0:T(8,128)(2,1)S(1)}, bf16[64,1024]{1,0:T(8,128)(2,1)S(1)}, u32[]{:S(2)}, u32[]{:S(2)}) collective-permute-start(bf16[64,1024]{1,0:T(8,128)(2,1)S(1)} %get-tuple-element.51), channel_id=1, source_target_pairs={{0,8},{8,0},{16,24},{24,16},{1,9},{9,1},{17,25},{25,17},{2,10},{10... | collective-permute-start | bytes 393224 | tf_op jit(solution)/shard_map/ppermute | solution.py:247
  106.5 9.2 %collective-permute-start.27 = (bf16[64,1024]{1,0:T(8,128)(2,1)S(1)}, bf16[64,1024]{1,0:T(8,128)(2,1)S(1)}, u32[]{:S(2)}, u32[]{:S(2)}) collective-permute-start(bf16[64,1024]{1,0:T(8,128)(2,1)S(1)} %get-tuple-element.49), channel_id=1, source_target_pairs={{0,24},{8,16},{16,8},{24,0},{1,25},{9,17},{17,9},{25,1},{2,26},{10... | collective-permute-start | bytes 393224 | tf_op jit(solution)/shard_map/ppermute | solution.py:247
  108.1 9.5 %collective-permute-start.26 = (bf16[64,1024]{1,0:T(8,128)(2,1)S(1)}, bf16[64,1024]{1,0:T(8,128)(2,1)S(1)}, u32[]{:S(2)}, u32[]{:S(2)}) collective-permute-start(bf16[64,1024]{1,0:T(8,128)(2,1)S(1)} %get-tuple-element.50), channel_id=1, source_target_pairs={{0,16},{8,24},{16,0},{24,8},{1,17},{9,25},{17,1},{25,9},{2,18},{10... | collective-permute-start | bytes 393224 | tf_op jit(solution)/shard_map/ppermute | solution.py:247
  110.1 7.6 %collective-permute-start.25 = (bf16[64,1024]{1,0:T(8,128)(2,1)S(1)}, bf16[64,1024]{1,0:T(8,128)(2,1)S(1)}, u32[]{:S(2)}, u32[]{:S(2)}) collective-permute-start(bf16[64,1024]{1,0:T(8,128)(2,1)S(1)} %get-tuple-element.48), channel_id=1, source_target_pairs={{0,8},{8,0},{16,24},{24,16},{1,9},{9,1},{17,25},{25,17},{2,10},{10... | collective-permute-start | bytes 393224 | tf_op jit(solution)/shard_map/ppermute | solution.py:247
  113.1 7.1 %collective-permute-start.37 = (bf16[16,1024]{1,0:T(8,128)(2,1)S(1)}, bf16[16,1024]{1,0:T(8,128)(2,1)S(1)}, u32[]{:S(2)}, u32[]{:S(2)}) collective-permute-start(bf16[16,1024]{1,0:T(8,128)(2,1)S(1)} %get-tuple-element.58), channel_id=1, source_target_pairs={{0,6},{1,7},{2,4},{3,5},{4,2},{5,3},{6,0},{7,1},{8,14},{9,15},{10,... | collective-permute-start | bytes 98312 | tf_op jit(solution)/shard_map/ppermute | solution.py:247
  115.3 6.9 %collective-permute-start.36 = (bf16[16,1024]{1,0:T(8,128)(2,1)S(1)}, bf16[16,1024]{1,0:T(8,128)(2,1)S(1)}, u32[]{:S(2)}, u32[]{:S(2)}) collective-permute-start(bf16[16,1024]{1,0:T(8,128)(2,1)S(1)} %get-tuple-element.59), channel_id=1, source_target_pairs={{0,4},{1,5},{2,6},{3,7},{4,0},{5,1},{6,2},{7,3},{8,12},{9,13},{10,... | collective-permute-start | bytes 98312 | tf_op jit(solution)/shard_map/ppermute | solution.py:247
  (21 other events, 107.1 us)

commit v2 on v1

--- a/solution.py
+++ b/solution.py
@@ -27,10 +27,46 @@
 WHOLE = pl.BlockSpec(memory_space=pltpu.VMEM)
 
 
+def teacher_stats_kernel(t_hbm, o_ref, x_ref, cols_sc, sem):
+    copy = pltpu.make_async_copy(t_hbm.at[0], x_ref, sem)
+    copy.start()
+    rows, cols = x_ref.shape
+    cols_sc[...] = jnp.zeros_like(cols_sc)
+    step = 16
+    lane = lax.broadcasted_iota(jnp.int32, (step, LANES), 1)
+    copy.wait()
+    for at in range(0, rows, step):
+        pieces = [slice(c, c + LANES) for c in range(0, cols, LANES)]
+        top = [jnp.full((step, LANES), -jnp.inf, F32)] * 4
+        for i, c in enumerate(pieces):
+            top[i % 4] = jnp.maximum(top[i % 4], x_ref[at : at + step, c].astype(F32))
+        top = functools.reduce(jnp.maximum, top)
+        top = jnp.max(top, axis=1, keepdims=True)
+        wide = jnp.broadcast_to(top, (step, LANES))
+        total = [jnp.zeros((step, LANES), F32)] * 4
+        for i, c in enumerate(pieces):
+            total[i % 4] = total[i % 4] + jnp.exp(x_ref[at : at + step, c].astype(F32) - wide)
+        total = jnp.sum(sum(total), axis=1, keepdims=True)
+        cols_sc[at : at + step, :] = jnp.where(lane == 0, wide, jnp.where(lane == 1, total, 0.0))
+    o_ref[...] = cols_sc[...].T[:8, :]
+
+
 def teacher_stats(teacher):
-    x = teacher[0].astype(F32)
-    top = jnp.max(x, axis=1)
-    return jnp.stack([top, jnp.sum(jnp.exp(x - top[:, None]), axis=1)])
+    _, rows, cols = teacher.shape
+    return pl.pallas_call(
+        teacher_stats_kernel,
+        in_specs=[pl.BlockSpec(memory_space=pl.ANY)],
+        out_specs=WHOLE,
+        out_shape=jax.ShapeDtypeStruct((8, LANES), F32),
+        scratch_shapes=[
+            pltpu.VMEM((rows, cols), BF16),
+            pltpu.VMEM((LANES, LANES), F32),
+            pltpu.SemaphoreType.DMA,
+        ],
+        compiler_params=params(2 * rows * cols + 4 * LANES * LANES),
+        cost_estimate=cost(8 * rows * cols, 2 * rows * cols),
+        name="teacher_stats",
+    )(teacher)
 
 
 def stack_kernel(*refs):
@@ -48,28 +84,26 @@
         in_specs=[WHOLE] * len(parts),
         out_specs=WHOLE,
         out_shape=shape,
-        compiler_params=params(2 * nbytes),
+        compiler_params=params(0),
         cost_estimate=cost(0, 2 * nbytes),
     )(*parts)
 
 
-def student_kernel(pieces, tile, *refs):
-    parts, (w_ref, t_ref, e_ref, h_ref, stat_ref, cols_sc) = refs[:pieces], refs[pieces:]
+def student_kernel(pieces, tile, own, *refs):
+    parts, (w_ref, t_ref, e_ref, h_ref, stat_ref, s_ref, cols_sc) = refs[:pieces], refs[pieces:]
     rows = parts[0].shape[0]
     for i, part in enumerate(parts):
         h_ref[i * rows : (i + 1) * rows, :] = part[...]
-
-    @pl.loop(0, w_ref.shape[1] // tile)
-    def _(j):
-        at = pl.ds(pl.multiple_of(j * tile, tile), tile)
-        e_ref[:, at] = jnp.dot(h_ref[...], w_ref[:, at], preferred_element_type=F32)
+    for at in range(0, w_ref.shape[1], tile):
+        w = w_ref[:, at : at + tile]
+        s_ref[:, at : at + tile] = jnp.dot(h_ref[...], w, preferred_element_type=F32)
 
     step = 8
     lane = lax.broadcasted_iota(jnp.int32, (step, LANES), 1)
 
     def body(i, _):
         at = pl.ds(pl.multiple_of(i * step, step), step)
-        x = e_ref[at, :]
+        x = s_ref[at, :]
         top = jnp.max(x, axis=1, keepdims=True)
         e = jnp.exp(x - top)
         e_ref[at, :] = e
@@ -77,16 +111,16 @@
         cols_sc[at, :] = jnp.where(lane == 0, top, jnp.where(lane == 1, total, 0.0))
         return _
 
-    lax.fori_loop(0, e_ref.shape[0] // step, body, 0, unroll=4)
+    lax.fori_loop(0, e_ref.shape[0] // step, body, 0, unroll=8)
     stat_ref[...] = cols_sc[...].T[:8, :]
-    stat_ref[2:4, : t_ref.shape[1]] = t_ref[...]
-
-
-def student(parts, weight, tstat, tile):
+    stat_ref[2:4, :own] = t_ref[:2, :own]
+
+
+def student(parts, weight, tstat, own, tile):
     depth, cols = weight.shape
     rows = sum(p.shape[0] for p in parts)
     return pl.pallas_call(
-        functools.partial(student_kernel, len(parts), tile),
+        functools.partial(student_kernel, len(parts), tile, own),
         in_specs=[WHOLE] * (len(parts) + 2),
         out_specs=[WHOLE] * 3,
         out_shape=[
@@ -94,8 +128,8 @@
             jax.ShapeDtypeStruct((rows, depth), BF16),
             jax.ShapeDtypeStruct((8, rows), F32),
         ],
-        scratch_shapes=[pltpu.VMEM((rows, LANES), F32)],
-        compiler_params=params(2 * depth * cols + 8 * rows * cols + 4 * rows * depth),
+        scratch_shapes=[pltpu.VMEM((rows, cols), F32), pltpu.VMEM((rows, LANES), F32)],
+        compiler_params=params(4 * rows * (cols + LANES)),
         cost_estimate=cost(2 * rows * cols * depth, 2 * depth * cols + 4 * rows * cols),
         name="student",
     )(*parts, weight, tstat)
@@ -106,13 +140,14 @@
     return jnp.where((lane // size) % 2 == 0, pltpu.roll(x, lanes - size, 1), pltpu.roll(x, size, 1))
 
 
-def logit_grad_kernel(place, n_stats, tile, ids, *refs):
+def logit_grad_kernel(place, n_stats, tile, *refs):
     stats = refs[:n_stats]
     teachers = refs[n_stats : n_stats + place.nv]
     e_ref, g_ref, cols_sc = refs[n_stats + place.nv :]
     rows = g_ref.shape[0]
     half = rows // 2
-    me = ids[0] * place.nv + ids[1]
+    v = lax.axis_index("vocab")
+    me = lax.axis_index("head") * place.nv + v
 
     tops, totals, teacher = [], [], []
     for zk, ref in enumerate(stats):
@@ -143,8 +178,8 @@
         for i, t_ref in enumerate(teachers):
             step, ck = divmod(i, 2)
             per = t_ref.shape[0] // place.group
-            source = ids[2 + step] * 2 + jnp.bitwise_xor(jnp.bitwise_and(ids[1], 1), ck)
-            vk = jnp.bitwise_xor(source, ids[1])
+            source = shifted(v >> 1, place.nz, place.nz - step) * 2 + jnp.bitwise_xor(v & 1, ck)
+            vk = jnp.bitwise_xor(source, v)
             for sub in range(per):
                 can = source * per + sub
                 to = place.position(jnp.bitwise_xor(me, can)) * place.group
@@ -157,19 +192,18 @@
                 g_ref[to, across] = (e_ref[to, across] * c[:, 0:1] - q).astype(BF16)
 
 
-def logit_grad(place, ids, stats, teachers, e, tile):
+def logit_grad(place, stats, teachers, e, tile):
     rows, cols = e.shape
     return pl.pallas_call(
         functools.partial(logit_grad_kernel, place, len(stats), tile),
-        in_specs=[pl.BlockSpec(memory_space=pltpu.SMEM)]
-        + [WHOLE] * (len(stats) + len(teachers) + 1),
+        in_specs=[WHOLE] * (len(stats) + len(teachers) + 1),
         out_specs=WHOLE,
         out_shape=jax.ShapeDtypeStruct((rows, cols), BF16),
         scratch_shapes=[pltpu.VMEM((rows, LANES), F32)],
-        compiler_params=params(8 * rows * cols + 4 * LANES * rows),
+        compiler_params=params(4 * rows * LANES),
         cost_estimate=cost(8 * rows * cols, 8 * rows * cols),
         name="logit_grad",
-    )(ids, *stats, *teachers, e)
+    )(*stats, *teachers, e)
 
 
 def input_grad_kernel(start, tile, g_ref, w_ref, keep_ref, send_ref):
@@ -194,38 +228,59 @@
             jax.ShapeDtypeStruct((rows // 2, width), F32),
             jax.ShapeDtypeStruct((rows // 2, width), BF16),
         ],
-        compiler_params=params(2 * rows * cols + 2 * weight.size + 3 * rows * width),
+        compiler_params=params(4 * rows * tile),
         cost_estimate=cost(2 * rows * cols * width, 2 * cols * (rows + width)),
         name="input_grad",
     )(g, weight)
 
 
-def weight_grad_kernel(h_ref, g_ref, *refs):
-    o_ref = refs[-1]
-    o_ref[0] = lax.dot_general(h_ref[...], g_ref[...], TN, preferred_element_type=F32).astype(BF16)
-
-
-def weight_grad_part(h, g, before, part, parts, tile):
+def turn_kernel(h_ref, w_hbm, o_ref, w_ref, sem):
+    copy = pltpu.make_async_copy(w_hbm, w_ref, sem)
+    copy.start()
+    o_ref[...] = h_ref[...].T
+    copy.wait()
+
+
+def turned(h, weight):
     rows, depth = h.shape
+    return pl.pallas_call(
+        turn_kernel,
+        in_specs=[WHOLE, pl.BlockSpec(memory_space=pl.ANY)],
+        out_specs=[WHOLE] * 2,
+        out_shape=[
+            jax.ShapeDtypeStruct((depth, rows), BF16),
+            jax.ShapeDtypeStruct(weight.shape, BF16),
+        ],
+        scratch_shapes=[pltpu.SemaphoreType.DMA],
+        compiler_params=params(0),
+        cost_estimate=cost(0, 4 * rows * depth + 4 * weight.size),
+        name="turn",
+    )(h, weight)
+
+
+def weight_grad_kernel(start, tile, ht_ref, g_ref, *refs):
+    at = pl.multiple_of((start + pl.program_id(0)) * tile, tile)
+    g = g_ref[:, pl.ds(at, tile)]
+    refs[-1][0] = jnp.dot(ht_ref[...], g, preferred_element_type=F32).astype(BF16)
+
+
+def weight_grad_part(ht, g, before, part, parts, tile):
+    depth, rows = ht.shape
     cols = g.shape[1]
     steps = cols // parts // tile
     start = part * steps
     extra = [] if before is None else [before]
     return pl.pallas_call(
-        weight_grad_kernel,
+        functools.partial(weight_grad_kernel, start, tile),
         grid=(steps,),
-        in_specs=[
-            pl.BlockSpec((rows, depth), lambda j: (0, 0)),
-            pl.BlockSpec((rows, tile), lambda j: (0, start + j)),
-        ]
-        + [pl.BlockSpec(memory_space=pl.ANY)] * len(extra),
+        in_specs=[WHOLE] * 2 + [pl.BlockSpec(memory_space=pl.ANY)] * len(extra),
         out_specs=pl.BlockSpec((1, depth, tile), lambda j: (0, 0, start + j)),
         out_shape=jax.ShapeDtypeStruct((1, depth, cols), BF16),
         input_output_aliases={2: 0} if extra else {},
-        compiler_params=params(4 * depth * rows + 4 * rows * tile + 8 * depth * tile),
+        compiler_params=params(8 * depth * tile),
         cost_estimate=cost(2 * rows * cols * depth // parts, 2 * depth * cols // parts),
         name="weight_grad",
-    )(h, g, *extra)
+    )(ht, g, *extra)
 
 
 class Place:
@@ -256,16 +311,14 @@
     bits = nz
     while bits > 2:
         place, rest, bits = place ^ rest, rest >> 1, bits // 2
-    return coded((place + step) % nz)
+    return coded((place + step) & (nz - 1))
 
 
 def relative(nh, nv, hidden, weight, teacher):
     place = Place(nh, nv, hidden.shape[0])
     nz = place.nz
     v = lax.axis_index("vocab")
-    z, core = v // 2, v % 2
-    sources = [shifted(z, nz, nz - step) for step in range(nz)]
-    ids = jnp.stack([lax.axis_index("head"), v] + sources).astype(jnp.int32)
+    z, core = v >> 1, v & 1
     cols = weight.shape[2]
 
     near = [hidden] + [None] * (nz - 1)
@@ -276,8 +329,10 @@
         to = shifted(z, nz, step) * 2 + (core ^ ck)
         return lax.dynamic_slice(teacher, (0, 0, to * cols), (1, teacher.shape[1], cols))[0]
 
-    def move(x, step):
-        pairs = [(2 * i + c, 2 * shifted(i, nz, step) + c) for i in range(nz) for c in range(2)]
+    def move(x, step, ck):
+        pairs = [
+            (2 * i + c, 2 * shifted(i, nz, step) + (c ^ ck)) for i in range(nz) for c in range(2)
+        ]
         return lax.ppermute(x, "vocab", pairs)
 
     blocks = []
@@ -286,10 +341,9 @@
     )
     for step in range(nz):
         mine, cross = pieces[step]
-        cross = swap(cross, "vocab", nv, 1)
         if step:
-            mine = move(mine, step)
-            cross = move(cross, step)
+            mine = move(mine, step, 0)
+        cross = move(cross, step, 1)
         blocks += [mine, cross]
 
     block = stacked(near)
@@ -300,38 +354,42 @@
     for k in range(nh):
         other.append(swap(own[k], "vocab", nv, 1))
 
-    e, h, stat = student(own + other, weight[0], teacher_stats(teacher), 512)
+    tstat = teacher_stats(teacher)
+    e, h, stat = student(own + other, weight[0], tstat, teacher.shape[1], 512)
     pair = swap(stat, "vocab", nv, 1)
     pair = stacked([stat, pair])
     stats = [pair]
     for k in range(1, nz):
         stats.append(swap(pair, "vocab", nv, 2 * k))
-    g = logit_grad(place, ids, stats, blocks, e, 1024)
+    ht, near_weight = turned(h, weight[0])
+    g = logit_grad(place, stats, blocks, e, 1024)
 
     depth = weight.shape[1]
     chunks = 2
     width = depth // chunks
     rows = place.group * nz
-    sums = []
+    keeps, sums = [], []
     for c in range(chunks):
-        keep, send = input_grad_part(g, weight[0], c * width, width, 512)
+        keep, send = input_grad_part(g, near_weight, c * width, width, 512)
         send = swap(send, "vocab", nv, 1)
-        keep = keep + send.astype(F32)
+        keeps.append(keep + send.astype(F32))
+    for keep in keeps:
         part = [keep[k * rows : (k + 1) * rows] for k in range(nh)]
         total = part[0]
         for k in range(1, nh):
             part[k] = swap(part[k].astype(BF16), "head", nh, k)
             total = total + part[k].astype(F32)
-        part = [total[k * place.group : (k + 1) * place.group] for k in range(nz)]
-        total = part[0]
-        for k in range(1, nz):
-            part[k] = swap(part[k].astype(BF16), "vocab", nv, 2 * k)
-            total = total + part[k].astype(F32)
         sums.append(total)
+    total = jnp.concatenate(sums, axis=1)
+    part = [total[k * place.group : (k + 1) * place.group] for k in range(nz)]
+    total = part[0]
+    for k in range(1, nz):
+        part[k] = swap(part[k].astype(BF16), "vocab", nv, 2 * k)
+        total = total + part[k].astype(F32)
     grad = None
     for part in range(PARTS):
-        grad = weight_grad_part(h, g, grad, part, PARTS, 512)
-    return (grad, jnp.concatenate(sums, axis=1))
+        grad = weight_grad_part(ht, g, grad, part, PARTS, 256)
+    return (grad, total)
 
 
 PARTS = 4

time: 126 us -> 127 us (level)
  starting transfers between devices: 39.9 us -> 58.9 us
  local copies, waits for them, and re-layouts: 16.5 us -> 7.63 us
  Pallas kernels: 31.5 us -> 25.3 us
  other arithmetic: 5.63 us -> 1.22 us
  waiting for transfers between devices: 31.3 us -> 32.6 us
    ppermute x32 -> x25, starting transfers between devices: 30.7 us -> 51.7 us  [swap(): return lax.ppermute(x, axis, [(i, i ^ k) for i in range(size)])]
    unnamed x30 -> x8, local copies, waits for them, and re-layouts: 13.8 us -> 5.81 us
    ppermute x32 -> x25, waiting for transfers between devices: 23.9 us -> 29.8 us  [swap(): return lax.ppermute(x, axis, [(i, i ^ k) for i in range(size)])]
    pallas_call x5 -> x7, Pallas kernels: 23.5 us -> 18.5 us  [the longest x4 9.66 us: weight_grad_part(): pl.pallas_call(functools.partial(weight_grad_kernel, start, tile), grid=(...]
    ppermute x6 -> x7, waiting for transfers between devices: 7.47 us -> 2.76 us  [move(): return lax.ppermute(x, 'vocab', pairs)]
    reduce_sum x1 -> x0, other arithmetic: 2.43 us -> none  [teacher_stats(): return jnp.stack([top, jnp.sum(jnp.exp(x - top[:, None]), axis=1)])]
    ppermute x6 -> x7, starting transfers between devices: 9.21 us -> 7.19 us  [move(): return lax.ppermute(x, 'vocab', pairs)]
    reduce_max x2 -> x0, other arithmetic: 1.97 us -> none  [teacher_stats(): top = jnp.max(x, axis=1)]
  transfers between devices with their start and end apart: 38 -> 32, of which waited for: 15 -> 16; matrix products, arithmetic and copies ran while one was open for 6% -> 2% of each run, Pallas kernels for 21% -> 17%
where the time goes in v2:
time: 127 us; the launch traced here: 126 us
  starting transfers between devices  58.9 us (46%)
  waiting for transfers between devices  32.6 us (26%)
  Pallas kernels  25.3 us (20%)
  local copies, waits for them, and re-layouts  7.63 us (6%)
    ppermute x25, starting transfers between devices, swap(): return lax.ppermute(x, axis, [(i, i ^ k) for i in range(size)])  51.7 us
    ppermute x25, waiting for transfers between devices, swap(): return lax.ppermute(x, axis, [(i, i ^ k) for i in range(size)])  29.8 us
    pallas_call x4, Pallas kernels, weight_grad_part(): pl.pallas_call(functools.partial(weight_grad_kernel, start, tile), grid=(...  9.66 us
    ppermute x7, starting transfers between devices, move(): return lax.ppermute(x, 'vocab', pairs)  7.19 us
    pallas_call x1, Pallas kernels, student(): pl.pallas_call(functools.partial(student_kernel, len(parts), tile, own),...  6.6 us
    unnamed x8, local copies, waits for them, and re-layouts  5.81 us
    pallas_call x2, Pallas kernels, input_grad_part(): pl.pallas_call(functools.partial(input_grad_kernel, start, tile), in_spec...  5.14 us
    ppermute x7, waiting for transfers between devices, move(): return lax.ppermute(x, 'vocab', pairs)  2.76 us
  transfers between devices with their start and end apart: 32, of which 16 were waited for; matrix products, arithmetic and copies ran while one was open for 2% of the time, Pallas kernels for 17%

profile of v2, /device:TPU:0, one launch (start us, length us, event | category | flops | bytes accessed | tf_op | source)
XLA Modules:
  0.0 126.5 jit_solution(14909466857089207761)
XLA Ops:
  0.6 4.1 %collective-permute-start.1 = (bf16[16,2048]{1,0:T(8,128)(2,1)}, bf16[16,2048]{1,0:T(8,128)(2,1)S(1)}, u32[]{:S(2)}, u32[]{:S(2)}) collective-permute-start(bf16[16,2048]{1,0:T(8,128)(2,1)} %refs_0_.1), channel_id=1, source_target_pairs={{0,4},{1,5},{2,6},{3,7},{4,0},{5,1},{6,2},{7,3},{8,12},{9,13},{10,... | collective-permute-start | bytes 196616 | tf_op jit(solution)/shard_map/ppermute | solution.py:302
  4.8 1.6 %collective-permute-start = (bf16[16,2048]{1,0:T(8,128)(2,1)}, bf16[16,2048]{1,0:T(8,128)(2,1)S(1)}, u32[]{:S(2)}, u32[]{:S(2)}) collective-permute-start(bf16[16,2048]{1,0:T(8,128)(2,1)} %refs_0_.1), channel_id=1, source_target_pairs={{0,2},{1,3},{2,0},{3,1},{4,6},{5,7},{6,4},{7,5},{8,10},{9,11},{10,... | collective-permute-start | bytes 196616 | tf_op jit(solution)/shard_map/ppermute | solution.py:302
  6.3 1.7 %collective-permute-done.1.refs_2_ = bf16[16,2048]{1,0:T(8,128)(2,1)S(1)} collective-permute-done((bf16[16,2048]{1,0:T(8,128)(2,1)}, bf16[16,2048]{1,0:T(8,128)(2,1)S(1)}, u32[]{:S(2)}, u32[]{:S(2)}) %collective-permute-start.1) | collective-permute-done | bytes 65568 | tf_op jit(solution)/shard_map/ppermute | solution.py:302
  9.2 3.4 %collective-permute-done.2.refs_3_ = bf16[16,2048]{1,0:T(8,128)(2,1)S(1)} collective-permute-done((bf16[16,2048]{1,0:T(8,128)(2,1)}, bf16[16,2048]{1,0:T(8,128)(2,1)S(1)}, u32[]{:S(2)}, u32[]{:S(2)}) %collective-permute-start.2) | collective-permute-done | bytes 65568 | tf_op jit(solution)/shard_map/ppermute | solution.py:302
  13.5 2.5 %collective-permute-start.5 = (bf16[64,2048]{1,0:T(8,128)(2,1)S(1)}, bf16[64,2048]{1,0:T(8,128)(2,1)S(1)}, u32[]{:S(2)}, u32[]{:S(2)}) collective-permute-start(bf16[64,2048]{1,0:T(8,128)(2,1)S(1)} %shard_map.50.refs_0_), channel_id=1, source_target_pairs={{0,24},{8,16},{16,8},{24,0},{1,25},{9,17},{17,9},{25,1},{2,26},{10... | collective-permute-start | bytes 786440 | tf_op jit(solution)/shard_map/ppermute | solution.py:302
  17.0 6.6 %collective-permute-done.5.refs_3_ = bf16[64,2048]{1,0:T(8,128)(2,1)S(1)} collective-permute-done((bf16[64,2048]{1,0:T(8,128)(2,1)S(1)}, bf16[64,2048]{1,0:T(8,128)(2,1)S(1)}, u32[]{:S(2)}, u32[]{:S(2)}) %collective-permute-start.5) | collective-permute-done | bytes 262176 | tf_op jit(solution)/shard_map/ppermute | solution.py:302
  23.6 2.9 %collective-permute-done.4.refs_2_ = bf16[64,2048]{1,0:T(8,128)(2,1)S(1)} collective-permute-done((bf16[64,2048]{1,0:T(8,128)(2,1)S(1)}, bf16[64,2048]{1,0:T(8,128)(2,1)S(1)}, u32[]{:S(2)}, u32[]{:S(2)}) %collective-permute-start.4) | collective-permute-done | bytes 262176 | tf_op jit(solution)/shard_map/ppermute | solution.py:302
  27.0 1.7 %dynamic-slice_bitcast_fusion = (bf16[64,2048]{1,0:T(8,128)(2,1)S(1)}, bf16[64,2048]{1,0:T(8,128)(2,1)S(1)}, bf16[64,2048]{1,0:T(8,128)(2,1)S(1)}, bf16[64,2048]...) fusion(bf16[1,64,16384]{2,1,0:T(8,128)(2,1)} %t_hbm.1, ...), kind=kLoop, calls=%fused_computation.12 | loop fusion | bytes 4194336 | tf_op jit(solution)/shard_map/squeeze | solution.py:330
  28.9 1.6 %copy-done.2 = bf16[1,64,16384]{2,1,0:T(8,128)(2,1)S(1)} copy-done((bf16[1,64,16384]{2,1,0:T(8,128)(2,1)S(1)}, bf16[1,64,16384]{2,1,0:T(8,128)(2,1)}, u32[]{:S(2)}) %copy-start.2) | copy-done | bytes 2097176
  33.9 2.1 %collective-permute-start.17 = (bf16[64,2048]{1,0:T(8,128)(2,1)S(1)}, bf16[64,2048]{1,0:T(8,128)(2,1)S(1)}, u32[]{:S(2)}, u32[]{:S(2)}) collective-permute-start(bf16[64,2048]{1,0:T(8,128)(2,1)S(1)} %get-tuple-element.26), channel_id=1, source_target_pairs={{0,6},{1,7},{2,4},{3,5},{4,2},{5,3},{6,0},{7,1},{8,14},{9,15},{10,... | collective-permute-start | bytes 786440 | tf_op jit(solution)/shard_map/ppermute | solution.py:336
  37.5 3.4 %copy-done = bf16[1,2048,2048]{2,1,0:T(8,128)(2,1)S(1)} copy-done((bf16[1,2048,2048]{2,1,0:T(8,128)(2,1)S(1)}, bf16[1,2048,2048]{2,1,0:T(8,128)(2,1)}, u32[]{:S(2)}) %copy-start) | copy-done | bytes 8388632
  40.9 6.6 %student.1 = (f32[512,2048]{1,0:T(8,128)S(1)}, bf16[512,2048]{1,0:T(8,128)(2,1)S(1)}, f32[8,512]{1,0:T(8,128)S(1)}) custom-call(bf16[64,2048]{1,0:T(8,128)(2,1)S(1)} %shard_map.50.refs_0_, bf16[64,2048]{1,0:T(8,128)(2,1)S(1)} %collective-permute-done.3.refs_1_, bf16[64,2048]{1,0:T(8,128)(2,1)S(1)} %collective-permute-done.4.refs_2_, ...), custom_call_target="tpu_custom_call" | custom-call | flops 4294967296 | bytes 12582912 | tf_op jit(solution)/shard_map/student/pallas_call | solution.py:122
  50.0 1.8 %collective-permute-start.13 = (f32[16,512]{1,0:T(8,128)S(1)}, f32[16,512]{1,0:T(8,128)S(1)}, u32[]{:S(2)}, u32[]{:S(2)}) collective-permute-start(f32[16,512]{1,0:T(8,128)S(1)} %shard_map.51.refs_0_), channel_id=1, source_target_pairs={{0,6},{1,7},{2,4},{3,5},{4,2},{5,3},{6,0},{7,1},{8,14},{9,15},{10,... | collective-permute-start | bytes 98312 | tf_op jit(solution)/shard_map/ppermute | solution.py:302
  51.7 2.7 %collective-permute-done.17.refs_8_ = bf16[64,2048]{1,0:T(8,128)(2,1)S(1)} collective-permute-done((bf16[64,2048]{1,0:T(8,128)(2,1)S(1)}, bf16[64,2048]{1,0:T(8,128)(2,1)S(1)}, u32[]{:S(2)}, u32[]{:S(2)}) %collective-permute-start.17) | collective-permute-done | bytes 262176 | tf_op jit(solution)/shard_map/ppermute | solution.py:336
  54.5 22.8 %collective-permute-start.12 = (f32[16,512]{1,0:T(8,128)S(1)}, f32[16,512]{1,0:T(8,128)S(1)}, u32[]{:S(2)}, u32[]{:S(2)}) collective-permute-start(f32[16,512]{1,0:T(8,128)S(1)} %shard_map.51.refs_0_), channel_id=1, source_target_pairs={{0,4},{1,5},{2,6},{3,7},{4,0},{5,1},{6,2},{7,3},{8,12},{9,13},{10,... | collective-permute-start | bytes 98312 | tf_op jit(solution)/shard_map/ppermute | solution.py:302
  77.3 4.9 %collective-permute-start.11 = (f32[16,512]{1,0:T(8,128)S(1)}, f32[16,512]{1,0:T(8,128)S(1)}, u32[]{:S(2)}, u32[]{:S(2)}) collective-permute-start(f32[16,512]{1,0:T(8,128)S(1)} %shard_map.51.refs_0_), channel_id=1, source_target_pairs={{0,2},{1,3},{2,0},{3,1},{4,6},{5,7},{6,4},{7,5},{8,10},{9,11},{10,... | collective-permute-start | bytes 98312 | tf_op jit(solution)/shard_map/ppermute | solution.py:302
  84.4 1.6 %logit_grad.1.g_ref = bf16[512,2048]{1,0:T(8,128)(2,1)S(1)} custom-call(f32[16,512]{1,0:T(8,128)S(1)} %shard_map.51.refs_0_, f32[16,512]{1,0:T(8,128)S(1)} %collective-permute-done.11.refs_1_, f32[16,512]{1,0:T(8,128)S(1)} %collective-permute-done.12.refs_2_, f32[16,512]{1,0:T(8,128)S(1)} %collective-permute-done.13.refs_3_, ...), custom_call_target="tpu_custom_call" | custom-call | flops 8388608 | bytes 8388608 | tf_op jit(solution)/shard_map/logit_grad/pallas_call | solution.py:197
  86.0 2.6 %input_grad.3 = (f32[256,1024]{1,0:T(8,128)S(1)}, bf16[256,1024]{1,0:T(8,128)(2,1)S(1)}) custom-call(bf16[512,2048]{1,0:T(8,128)(2,1)S(1)} %logit_grad.1.g_ref, bf16[2048,2048]{1,0:T(8,128)(2,1)S(1)} %get-tuple-element.31.w_ref), custom_call_target="tpu_custom_call" | custom-call | flops 2147483648 | bytes 6291456 | tf_op jit(solution)/shard_map/input_grad/pallas_call | solution.py:223
  88.8 2.6 %input_grad.2 = (f32[256,1024]{1,0:T(8,128)S(1)}, bf16[256,1024]{1,0:T(8,128)(2,1)S(1)}) custom-call(bf16[512,2048]{1,0:T(8,128)(2,1)S(1)} %logit_grad.1.g_ref, bf16[2048,2048]{1,0:T(8,128)(2,1)S(1)} %get-tuple-element.31.w_ref), custom_call_target="tpu_custom_call" | custom-call | flops 2147483648 | bytes 6291456 | tf_op jit(solution)/shard_map/input_grad/pallas_call | solution.py:223
  91.8 2.4 %weight_grad.4.refs_0_ = bf16[1,2048,2048]{2,1,0:T(8,128)(2,1)} custom-call(bf16[2048,512]{1,0:T(8,128)(2,1)S(1)} %get-tuple-element.20.ht_ref, bf16[512,2048]{1,0:T(8,128)(2,1)S(1)} %logit_grad.1.g_ref), custom_call_target="tpu_custom_call" | custom-call | flops 1073741824 | bytes 2097152 | tf_op jit(solution)/shard_map/weight_grad/pallas_call | solution.py:273
  94.3 2.4 %weight_grad.5.refs_0_ = bf16[1,2048,2048]{2,1,0:T(8,128)(2,1)} custom-call(bf16[2048,512]{1,0:T(8,128)(2,1)S(1)} %get-tuple-element.20.ht_ref, bf16[512,2048]{1,0:T(8,128)(2,1)S(1)} %logit_grad.1.g_ref, bf16[1,2048,2048]{2,1,0:T(8,128)(2,1)} %weight_grad.4.refs_0_), custom_call_target="tpu_custom_call", output_to_operand_aliasing={{}: (2, {})} | custom-call | flops 1073741824 | bytes 2097152 | tf_op jit(solution)/shard_map/weight_grad/pallas_call | solution.py:273
  96.7 2.4 %weight_grad.6.refs_0_ = bf16[1,2048,2048]{2,1,0:T(8,128)(2,1)} custom-call(bf16[2048,512]{1,0:T(8,128)(2,1)S(1)} %get-tuple-element.20.ht_ref, bf16[512,2048]{1,0:T(8,128)(2,1)S(1)} %logit_grad.1.g_ref, bf16[1,2048,2048]{2,1,0:T(8,128)(2,1)} %weight_grad.5.refs_0_), custom_call_target="tpu_custom_call", output_to_operand_aliasing={{}: (2, {})} | custom-call | flops 1073741824 | bytes 2097152 | tf_op jit(solution)/shard_map/weight_grad/pallas_call | solution.py:273
  99.4 1.6 %collective-permute-start.26 = (bf16[64,1024]{1,0:T(8,128)(2,1)S(1)}, bf16[64,1024]{1,0:T(8,128)(2,1)S(1)}, u32[]{:S(2)}, u32[]{:S(2)}) collective-permute-start(bf16[64,1024]{1,0:T(8,128)(2,1)S(1)} %get-tuple-element.48), channel_id=1, source_target_pairs={{0,8},{8,0},{16,24},{24,16},{1,9},{9,1},{17,25},{25,17},{2,10},{10... | collective-permute-start | bytes 393224 | tf_op jit(solution)/shard_map/ppermute | solution.py:302
  103.1 1.6 %collective-permute-start.22 = (bf16[64,1024]{1,0:T(8,128)(2,1)S(1)}, bf16[64,1024]{1,0:T(8,128)(2,1)S(1)}, u32[]{:S(2)}, u32[]{:S(2)}) collective-permute-start(bf16[64,1024]{1,0:T(8,128)(2,1)S(1)} %get-tuple-element.51), channel_id=1, source_target_pairs={{0,8},{8,0},{16,24},{24,16},{1,9},{9,1},{17,25},{25,17},{2,10},{10... | collective-permute-start | bytes 393224 | tf_op jit(solution)/shard_map/ppermute | solution.py:302
  107.2 2.3 %collective-permute-done.28 = bf16[64,1024]{1,0:T(8,128)(2,1)S(1)} collective-permute-done((bf16[64,1024]{1,0:T(8,128)(2,1)S(1)}, bf16[64,1024]{1,0:T(8,128)(2,1)S(1)}, u32[]{:S(2)}, u32[]{:S(2)}) %collective-permute-start.28) | collective-permute-done | bytes 131104 | tf_op jit(solution)/shard_map/ppermute | solution.py:302
  109.5 2.0 %collective-permute-done.27 = bf16[64,1024]{1,0:T(8,128)(2,1)S(1)} collective-permute-done((bf16[64,1024]{1,0:T(8,128)(2,1)S(1)}, bf16[64,1024]{1,0:T(8,128)(2,1)S(1)}, u32[]{:S(2)}, u32[]{:S(2)}) %collective-permute-start.27) | collective-permute-done | bytes 131104 | tf_op jit(solution)/shard_map/ppermute | solution.py:302
  111.5 2.8 %collective-permute-done.24 = bf16[64,1024]{1,0:T(8,128)(2,1)S(1)} collective-permute-done((bf16[64,1024]{1,0:T(8,128)(2,1)S(1)}, bf16[64,1024]{1,0:T(8,128)(2,1)S(1)}, u32[]{:S(2)}, u32[]{:S(2)}) %collective-permute-start.24) | collective-permute-done | bytes 131104 | tf_op jit(solution)/shard_map/ppermute | solution.py:302
  115.8 1.9 %collective-permute-start.29 = (bf16[16,2048]{1,0:T(8,128)(2,1)S(1)}, bf16[16,2048]{1,0:T(8,128)(2,1)S(1)}, u32[]{:S(2)}, u32[]{:S(2)}) collective-permute-start(bf16[16,2048]{1,0:T(8,128)(2,1)S(1)} %get-tuple-element.54), channel_id=1, source_target_pairs={{0,2},{1,3},{2,0},{3,1},{4,6},{5,7},{6,4},{7,5},{8,10},{9,11},{10,... | collective-permute-start | bytes 196616 | tf_op jit(solution)/shard_map/ppermute | solution.py:302
  117.6 1.9 %collective-permute-start.31 = (bf16[16,2048]{1,0:T(8,128)(2,1)S(1)}, bf16[16,2048]{1,0:T(8,128)(2,1)S(1)}, u32[]{:S(2)}, u32[]{:S(2)}) collective-permute-start(bf16[16,2048]{1,0:T(8,128)(2,1)S(1)} %get-tuple-element.55), channel_id=1, source_target_pairs={{0,6},{1,7},{2,4},{3,5},{4,2},{5,3},{6,0},{7,1},{8,14},{9,15},{10,... | collective-permute-start | bytes 196616 | tf_op jit(solution)/shard_map/ppermute | solution.py:302
  119.5 2.4 %weight_grad.7 = bf16[1,2048,2048]{2,1,0:T(8,128)(2,1)} custom-call(bf16[2048,512]{1,0:T(8,128)(2,1)S(1)} %get-tuple-element.20.ht_ref, bf16[512,2048]{1,0:T(8,128)(2,1)S(1)} %logit_grad.1.g_ref, bf16[1,2048,2048]{2,1,0:T(8,128)(2,1)} %weight_grad.6.refs_0_), custom_call_target="tpu_custom_call", output_to_operand_aliasing={{}: (2, {})} | custom-call | flops 1073741824 | bytes 2097152 | tf_op jit(solution)/shard_map/weight_grad/pallas_call | solution.py:273
  122.0 1.8 %collective-permute-done.31 = bf16[16,2048]{1,0:T(8,128)(2,1)S(1)} collective-permute-done((bf16[16,2048]{1,0:T(8,128)(2,1)S(1)}, bf16[16,2048]{1,0:T(8,128)(2,1)S(1)}, u32[]{:S(2)}, u32[]{:S(2)}) %collective-permute-start.31) | collective-permute-done | bytes 65568 | tf_op jit(solution)/shard_map/ppermute | solution.py:302
  123.7 2.0 %collective-permute-done.30 = bf16[16,2048]{1,0:T(8,128)(2,1)S(1)} collective-permute-done((bf16[16,2048]{1,0:T(8,128)(2,1)S(1)}, bf16[16,2048]{1,0:T(8,128)(2,1)S(1)}, u32[]{:S(2)}, u32[]{:S(2)}) %collective-permute-start.30) | collective-permute-done | bytes 65568 | tf_op jit(solution)/shard_map/ppermute | solution.py:302
  (62 shorter events, 21.2 us)
Async XLA Ops:
  0.6 7.4 %collective-permute-start.1 = (bf16[16,2048]{1,0:T(8,128)(2,1)}, bf16[16,2048]{1,0:T(8,128)(2,1)S(1)}, u32[]{:S(2)}, u32[]{:S(2)}) collective-permute-start(bf16[16,2048]{1,0:T(8,128)(2,1)} %refs_0_.1), channel_id=1, source_target_pairs={{0,4},{1,5},{2,6},{3,7},{4,0},{5,1},{6,2},{7,3},{8,12},{9,13},{10,... | collective-permute-start | bytes 196616 | tf_op jit(solution)/shard_map/ppermute | solution.py:302
  4.8 4.5 %collective-permute-start = (bf16[16,2048]{1,0:T(8,128)(2,1)}, bf16[16,2048]{1,0:T(8,128)(2,1)S(1)}, u32[]{:S(2)}, u32[]{:S(2)}) collective-permute-start(bf16[16,2048]{1,0:T(8,128)(2,1)} %refs_0_.1), channel_id=1, source_target_pairs={{0,2},{1,3},{2,0},{3,1},{4,6},{5,7},{6,4},{7,5},{8,10},{9,11},{10,... | collective-permute-start | bytes 196616 | tf_op jit(solution)/shard_map/ppermute | solution.py:302
  6.3 6.3 %collective-permute-start.2 = (bf16[16,2048]{1,0:T(8,128)(2,1)}, bf16[16,2048]{1,0:T(8,128)(2,1)S(1)}, u32[]{:S(2)}, u32[]{:S(2)}) collective-permute-start(bf16[16,2048]{1,0:T(8,128)(2,1)} %refs_0_.1), channel_id=1, source_target_pairs={{0,6},{1,7},{2,4},{3,5},{4,2},{5,3},{6,0},{7,1},{8,14},{9,15},{10,... | collective-permute-start | bytes 196616 | tf_op jit(solution)/shard_map/ppermute | solution.py:302
  13.5 10.2 %collective-permute-start.5 = (bf16[64,2048]{1,0:T(8,128)(2,1)S(1)}, bf16[64,2048]{1,0:T(8,128)(2,1)S(1)}, u32[]{:S(2)}, u32[]{:S(2)}) collective-permute-start(bf16[64,2048]{1,0:T(8,128)(2,1)S(1)} %shard_map.50.refs_0_), channel_id=1, source_target_pairs={{0,24},{8,16},{16,8},{24,0},{1,25},{9,17},{17,9},{25,1},{2,26},{10... | collective-permute-start | bytes 786440 | tf_op jit(solution)/shard_map/ppermute | solution.py:302
  16.0 10.5 %collective-permute-start.4 = (bf16[64,2048]{1,0:T(8,128)(2,1)S(1)}, bf16[64,2048]{1,0:T(8,128)(2,1)S(1)}, u32[]{:S(2)}, u32[]{:S(2)}) collective-permute-start(bf16[64,2048]{1,0:T(8,128)(2,1)S(1)} %shard_map.50.refs_0_), channel_id=1, source_target_pairs={{0,16},{8,24},{16,0},{24,8},{1,17},{9,25},{17,1},{25,9},{2,18},{10... | collective-permute-start | bytes 786440 | tf_op jit(solution)/shard_map/ppermute | solution.py:302
  16.5 10.1 %collective-permute-start.3 = (bf16[64,2048]{1,0:T(8,128)(2,1)S(1)}, bf16[64,2048]{1,0:T(8,128)(2,1)S(1)}, u32[]{:S(2)}, u32[]{:S(2)}) collective-permute-start(bf16[64,2048]{1,0:T(8,128)(2,1)S(1)} %shard_map.50.refs_0_), channel_id=1, source_target_pairs={{0,8},{8,0},{16,24},{24,16},{1,9},{9,1},{17,25},{25,17},{2,10},{10... | collective-permute-start | bytes 786440 | tf_op jit(solution)/shard_map/ppermute | solution.py:302
  17.0 14.6 %collective-permute-start.6 = (bf16[64,2048]{1,0:T(8,128)(2,1)S(1)}, bf16[64,2048]{1,0:T(8,128)(2,1)S(1)}, u32[]{:S(2)}, u32[]{:S(2)}) collective-permute-start(bf16[64,2048]{1,0:T(8,128)(2,1)S(1)} %shard_map.50.refs_0_), channel_id=1, source_target_pairs={{0,1},{1,0},{2,3},{3,2},{4,5},{5,4},{6,7},{7,6},{8,9},{9,8},{10,11... | collective-permute-start | bytes 786440 | tf_op jit(solution)/shard_map/ppermute | solution.py:302
  23.6 8.9 %collective-permute-start.9 = (bf16[64,2048]{1,0:T(8,128)(2,1)S(1)}, bf16[64,2048]{1,0:T(8,128)(2,1)S(1)}, u32[]{:S(2)}, u32[]{:S(2)}) collective-permute-start(bf16[64,2048]{1,0:T(8,128)(2,1)S(1)} %collective-permute-done.5.refs_3_), channel_id=1, source_target_pairs={{0,1},{1,0},{2,3},{3,2},{4,5},{5,4},{6,7},{7,6},{8,9},{9,8},{10,11... | collective-permute-start | bytes 786440 | tf_op jit(solution)/shard_map/ppermute | solution.py:302
  26.5 7.5 %collective-permute-start.8 = (bf16[64,2048]{1,0:T(8,128)(2,1)S(1)}, bf16[64,2048]{1,0:T(8,128)(2,1)S(1)}, u32[]{:S(2)}, u32[]{:S(2)}) collective-permute-start(bf16[64,2048]{1,0:T(8,128)(2,1)S(1)} %collective-permute-done.4.refs_2_), channel_id=1, source_target_pairs={{0,1},{1,0},{2,3},{3,2},{4,5},{5,4},{6,7},{7,6},{8,9},{9,8},{10,11... | collective-permute-start | bytes 786440 | tf_op jit(solution)/shard_map/ppermute | solution.py:302
  26.6 9.4 %collective-permute-start.7 = (bf16[64,2048]{1,0:T(8,128)(2,1)S(1)}, bf16[64,2048]{1,0:T(8,128)(2,1)S(1)}, u32[]{:S(2)}, u32[]{:S(2)}) collective-permute-start(bf16[64,2048]{1,0:T(8,128)(2,1)S(1)} %collective-permute-done.3.refs_1_), channel_id=1, source_target_pairs={{0,1},{1,0},{2,3},{3,2},{4,5},{5,4},{6,7},{7,6},{8,9},{9,8},{10,11... | collective-permute-start | bytes 786440 | tf_op jit(solution)/shard_map/ppermute | solution.py:302
  28.8 18.7 %collective-permute-start.14 = (bf16[64,2048]{1,0:T(8,128)(2,1)S(1)}, bf16[64,2048]{1,0:T(8,128)(2,1)S(1)}, u32[]{:S(2)}, u32[]{:S(2)}) collective-permute-start(bf16[64,2048]{1,0:T(8,128)(2,1)S(1)} %get-tuple-element.23), channel_id=1, source_target_pairs={{0,1},{1,0},{2,3},{3,2},{4,5},{5,4},{6,7},{7,6},{8,9},{9,8},{10,11... | collective-permute-start | bytes 786440 | tf_op jit(solution)/shard_map/ppermute | solution.py:336
  31.6 16.3 %collective-permute-start.15 = (bf16[64,2048]{1,0:T(8,128)(2,1)S(1)}, bf16[64,2048]{1,0:T(8,128)(2,1)S(1)}, u32[]{:S(2)}, u32[]{:S(2)}) collective-permute-start(bf16[64,2048]{1,0:T(8,128)(2,1)S(1)} %get-tuple-element.24), channel_id=1, source_target_pairs={{0,2},{1,3},{2,6},{3,7},{4,0},{5,1},{6,4},{7,5},{8,10},{9,11},{10,... | collective-permute-start | bytes 786440 | tf_op jit(solution)/shard_map/ppermute | solution.py:336
  32.5 17.5 %collective-permute-start.16 = (bf16[64,2048]{1,0:T(8,128)(2,1)S(1)}, bf16[64,2048]{1,0:T(8,128)(2,1)S(1)}, u32[]{:S(2)}, u32[]{:S(2)}) collective-permute-start(bf16[64,2048]{1,0:T(8,128)(2,1)S(1)} %get-tuple-element.25), channel_id=1, source_target_pairs={{0,3},{1,2},{2,7},{3,6},{4,1},{5,0},{6,5},{7,4},{8,11},{9,10},{10,... | collective-permute-start | bytes 786440 | tf_op jit(solution)/shard_map/ppermute | solution.py:336
  33.9 20.6 %collective-permute-start.17 = (bf16[64,2048]{1,0:T(8,128)(2,1)S(1)}, bf16[64,2048]{1,0:T(8,128)(2,1)S(1)}, u32[]{:S(2)}, u32[]{:S(2)}) collective-permute-start(bf16[64,2048]{1,0:T(8,128)(2,1)S(1)} %get-tuple-element.26), channel_id=1, source_target_pairs={{0,6},{1,7},{2,4},{3,5},{4,2},{5,3},{6,0},{7,1},{8,14},{9,15},{10,... | collective-permute-start | bytes 786440 | tf_op jit(solution)/shard_map/ppermute | solution.py:336
  36.0 41.3 %collective-permute-start.18 = (bf16[64,2048]{1,0:T(8,128)(2,1)S(1)}, bf16[64,2048]{1,0:T(8,128)(2,1)S(1)}, u32[]{:S(2)}, u32[]{:S(2)}) collective-permute-start(bf16[64,2048]{1,0:T(8,128)(2,1)S(1)} %get-tuple-element.27), channel_id=1, source_target_pairs={{0,7},{1,6},{2,5},{3,4},{4,3},{5,2},{6,1},{7,0},{8,15},{9,14},{10,... | collective-permute-start | bytes 786440 | tf_op jit(solution)/shard_map/ppermute | solution.py:336
  47.5 1.3 %collective-permute-start.10 = (f32[8,512]{1,0:T(8,128)S(1)}, f32[8,512]{1,0:T(8,128)S(1)}, u32[]{:S(2)}, u32[]{:S(2)}) collective-permute-start(f32[8,512]{1,0:T(8,128)S(1)} %get-tuple-element.21.refs_0_), channel_id=1, source_target_pairs={{0,1},{1,0},{2,3},{3,2},{4,5},{5,4},{6,7},{7,6},{8,9},{9,8},{10,11... | collective-permute-start | bytes 49160 | tf_op jit(solution)/shard_map/ppermute | solution.py:302
  47.9 35.4 %collective-permute-start.19 = (bf16[64,2048]{1,0:T(8,128)(2,1)S(1)}, bf16[64,2048]{1,0:T(8,128)(2,1)S(1)}, u32[]{:S(2)}, u32[]{:S(2)}) collective-permute-start(bf16[64,2048]{1,0:T(8,128)(2,1)S(1)} %get-tuple-element.28), channel_id=1, source_target_pairs={{0,4},{1,5},{2,0},{3,1},{4,6},{5,7},{6,2},{7,3},{8,12},{9,13},{10,... | collective-permute-start | bytes 786440 | tf_op jit(solution)/shard_map/ppermute | solution.py:336
  48.8 34.6 %collective-permute-start.20 = (bf16[64,2048]{1,0:T(8,128)(2,1)S(1)}, bf16[64,2048]{1,0:T(8,128)(2,1)S(1)}, u32[]{:S(2)}, u32[]{:S(2)}) collective-permute-start(bf16[64,2048]{1,0:T(8,128)(2,1)S(1)} %get-tuple-element.29), channel_id=1, source_target_pairs={{0,5},{1,4},{2,1},{3,0},{4,7},{5,6},{6,3},{7,2},{8,13},{9,12},{10,... | collective-permute-start | bytes 786440 | tf_op jit(solution)/shard_map/ppermute | solution.py:336
  50.0 33.4 %collective-permute-start.13 = (f32[16,512]{1,0:T(8,128)S(1)}, f32[16,512]{1,0:T(8,128)S(1)}, u32[]{:S(2)}, u32[]{:S(2)}) collective-permute-start(f32[16,512]{1,0:T(8,128)S(1)} %shard_map.51.refs_0_), channel_id=1, source_target_pairs={{0,6},{1,7},{2,4},{3,5},{4,2},{5,3},{6,0},{7,1},{8,14},{9,15},{10,... | collective-permute-start | bytes 98312 | tf_op jit(solution)/shard_map/ppermute | solution.py:302
  54.5 29.0 %collective-permute-start.12 = (f32[16,512]{1,0:T(8,128)S(1)}, f32[16,512]{1,0:T(8,128)S(1)}, u32[]{:S(2)}, u32[]{:S(2)}) collective-permute-start(f32[16,512]{1,0:T(8,128)S(1)} %shard_map.51.refs_0_), channel_id=1, source_target_pairs={{0,4},{1,5},{2,6},{3,7},{4,0},{5,1},{6,2},{7,3},{8,12},{9,13},{10,... | collective-permute-start | bytes 98312 | tf_op jit(solution)/shard_map/ppermute | solution.py:302
  77.3 7.2 %collective-permute-start.11 = (f32[16,512]{1,0:T(8,128)S(1)}, f32[16,512]{1,0:T(8,128)S(1)}, u32[]{:S(2)}, u32[]{:S(2)}) collective-permute-start(f32[16,512]{1,0:T(8,128)S(1)} %shard_map.51.refs_0_), channel_id=1, source_target_pairs={{0,2},{1,3},{2,0},{3,1},{4,6},{5,7},{6,4},{7,5},{8,10},{9,11},{10,... | collective-permute-start | bytes 98312 | tf_op jit(solution)/shard_map/ppermute | solution.py:302
  88.6 10.5 %collective-permute-start.25 = (bf16[256,1024]{1,0:T(8,128)(2,1)S(1)}, bf16[256,1024]{1,0:T(8,128)(2,1)S(1)}, u32[]{:S(2)}, u32[]{:S(2)}) collective-permute-start(bf16[256,1024]{1,0:T(8,128)(2,1)S(1)} %get-tuple-element.35), channel_id=1, source_target_pairs={{0,1},{1,0},{2,3},{3,2},{4,5},{5,4},{6,7},{7,6},{8,9},{9,8},{10,11... | collective-permute-start | bytes 1572872 | tf_op jit(solution)/shard_map/ppermute | solution.py:302
  91.4 11.5 %collective-permute-start.21 = (bf16[256,1024]{1,0:T(8,128)(2,1)S(1)}, bf16[256,1024]{1,0:T(8,128)(2,1)S(1)}, u32[]{:S(2)}, u32[]{:S(2)}) collective-permute-start(bf16[256,1024]{1,0:T(8,128)(2,1)S(1)} %get-tuple-element.33), channel_id=1, source_target_pairs={{0,1},{1,0},{2,3},{3,2},{4,5},{5,4},{6,7},{7,6},{8,9},{9,8},{10,11... | collective-permute-start | bytes 1572872 | tf_op jit(solution)/shard_map/ppermute | solution.py:302
  99.4 6.7 %collective-permute-start.26 = (bf16[64,1024]{1,0:T(8,128)(2,1)S(1)}, bf16[64,1024]{1,0:T(8,128)(2,1)S(1)}, u32[]{:S(2)}, u32[]{:S(2)}) collective-permute-start(bf16[64,1024]{1,0:T(8,128)(2,1)S(1)} %get-tuple-element.48), channel_id=1, source_target_pairs={{0,8},{8,0},{16,24},{24,16},{1,9},{9,1},{17,25},{25,17},{2,10},{10... | collective-permute-start | bytes 393224 | tf_op jit(solution)/shard_map/ppermute | solution.py:302
  100.9 8.6 %collective-permute-start.28 = (bf16[64,1024]{1,0:T(8,128)(2,1)S(1)}, bf16[64,1024]{1,0:T(8,128)(2,1)S(1)}, u32[]{:S(2)}, u32[]{:S(2)}) collective-permute-start(bf16[64,1024]{1,0:T(8,128)(2,1)S(1)} %get-tuple-element.49), channel_id=1, source_target_pairs={{0,24},{8,16},{16,8},{24,0},{1,25},{9,17},{17,9},{25,1},{2,26},{10... | collective-permute-start | bytes 393224 | tf_op jit(solution)/shard_map/ppermute | solution.py:302
  102.3 9.1 %collective-permute-start.27 = (bf16[64,1024]{1,0:T(8,128)(2,1)S(1)}, bf16[64,1024]{1,0:T(8,128)(2,1)S(1)}, u32[]{:S(2)}, u32[]{:S(2)}) collective-permute-start(bf16[64,1024]{1,0:T(8,128)(2,1)S(1)} %get-tuple-element.50), channel_id=1, source_target_pairs={{0,16},{8,24},{16,0},{24,8},{1,17},{9,25},{17,1},{25,9},{2,18},{10... | collective-permute-start | bytes 393224 | tf_op jit(solution)/shard_map/ppermute | solution.py:302
  103.1 8.4 %collective-permute-start.22 = (bf16[64,1024]{1,0:T(8,128)(2,1)S(1)}, bf16[64,1024]{1,0:T(8,128)(2,1)S(1)}, u32[]{:S(2)}, u32[]{:S(2)}) collective-permute-start(bf16[64,1024]{1,0:T(8,128)(2,1)S(1)} %get-tuple-element.51), channel_id=1, source_target_pairs={{0,8},{8,0},{16,24},{24,16},{1,9},{9,1},{17,25},{25,17},{2,10},{10... | collective-permute-start | bytes 393224 | tf_op jit(solution)/shard_map/ppermute | solution.py:302
  104.7 9.6 %collective-permute-start.24 = (bf16[64,1024]{1,0:T(8,128)(2,1)S(1)}, bf16[64,1024]{1,0:T(8,128)(2,1)S(1)}, u32[]{:S(2)}, u32[]{:S(2)}) collective-permute-start(bf16[64,1024]{1,0:T(8,128)(2,1)S(1)} %get-tuple-element.52), channel_id=1, source_target_pairs={{0,24},{8,16},{16,8},{24,0},{1,25},{9,17},{17,9},{25,1},{2,26},{10... | collective-permute-start | bytes 393224 | tf_op jit(solution)/shard_map/ppermute | solution.py:302
  106.1 9.5 %collective-permute-start.23 = (bf16[64,1024]{1,0:T(8,128)(2,1)S(1)}, bf16[64,1024]{1,0:T(8,128)(2,1)S(1)}, u32[]{:S(2)}, u32[]{:S(2)}) collective-permute-start(bf16[64,1024]{1,0:T(8,128)(2,1)S(1)} %get-tuple-element.53), channel_id=1, source_target_pairs={{0,16},{8,24},{16,0},{24,8},{1,17},{9,25},{17,1},{25,9},{2,18},{10... | collective-permute-start | bytes 393224 | tf_op jit(solution)/shard_map/ppermute | solution.py:302
  115.8 6.2 %collective-permute-start.29 = (bf16[16,2048]{1,0:T(8,128)(2,1)S(1)}, bf16[16,2048]{1,0:T(8,128)(2,1)S(1)}, u32[]{:S(2)}, u32[]{:S(2)}) collective-permute-start(bf16[16,2048]{1,0:T(8,128)(2,1)S(1)} %get-tuple-element.54), channel_id=1, source_target_pairs={{0,2},{1,3},{2,0},{3,1},{4,6},{5,7},{6,4},{7,5},{8,10},{9,11},{10,... | collective-permute-start | bytes 196616 | tf_op jit(solution)/shard_map/ppermute | solution.py:302
  117.6 6.1 %collective-permute-start.31 = (bf16[16,2048]{1,0:T(8,128)(2,1)S(1)}, bf16[16,2048]{1,0:T(8,128)(2,1)S(1)}, u32[]{:S(2)}, u32[]{:S(2)}) collective-permute-start(bf16[16,2048]{1,0:T(8,128)(2,1)S(1)} %get-tuple-element.55), channel_id=1, source_target_pairs={{0,6},{1,7},{2,4},{3,5},{4,2},{5,3},{6,0},{7,1},{8,14},{9,15},{10,... | collective-permute-start | bytes 196616 | tf_op jit(solution)/shard_map/ppermute | solution.py:302
  119.5 6.2 %collective-permute-start.30 = (bf16[16,2048]{1,0:T(8,128)(2,1)S(1)}, bf16[16,2048]{1,0:T(8,128)(2,1)S(1)}, u32[]{:S(2)}, u32[]{:S(2)}) collective-permute-start(bf16[16,2048]{1,0:T(8,128)(2,1)S(1)} %get-tuple-element.56), channel_id=1, source_target_pairs={{0,4},{1,5},{2,6},{3,7},{4,0},{5,1},{6,2},{7,3},{8,12},{9,13},{10,... | collective-permute-start | bytes 196616 | tf_op jit(solution)/shard_map/ppermute | solution.py:302
  (4 other events, 47.1 us)

commit v3 on v2

--- a/solution.py
+++ b/solution.py
@@ -14,6 +14,7 @@
 NT = (((1,), (1,)), ((), ()))
 TN = (((0,), (0,)), ((), ()))
 MIB = 1024 * 1024
+ROOM = 42 * MIB
 
 
 def params(nbytes):
@@ -25,11 +26,14 @@
 
 
 WHOLE = pl.BlockSpec(memory_space=pltpu.VMEM)
-
-
-def teacher_stats_kernel(t_hbm, o_ref, x_ref, cols_sc, sem):
-    copy = pltpu.make_async_copy(t_hbm.at[0], x_ref, sem)
+STORED = pl.BlockSpec(memory_space=pltpu.HBM)
+
+
+def prepare_kernel(t_hbm, w_hbm, o_ref, w_ref, x_ref, cols_sc, sem):
+    copy = pltpu.make_async_copy(t_hbm.at[0], x_ref, sem.at[0])
     copy.start()
+    weight = pltpu.make_async_copy(w_hbm, w_ref, sem.at[1])
+    weight.start()
     rows, cols = x_ref.shape
     cols_sc[...] = jnp.zeros_like(cols_sc)
     step = 16
@@ -49,24 +53,28 @@
         total = jnp.sum(sum(total), axis=1, keepdims=True)
         cols_sc[at : at + step, :] = jnp.where(lane == 0, wide, jnp.where(lane == 1, total, 0.0))
     o_ref[...] = cols_sc[...].T[:8, :]
-
-
-def teacher_stats(teacher):
+    weight.wait()
+
+
+def prepared(teacher, weight):
     _, rows, cols = teacher.shape
     return pl.pallas_call(
-        teacher_stats_kernel,
-        in_specs=[pl.BlockSpec(memory_space=pl.ANY)],
-        out_specs=WHOLE,
-        out_shape=jax.ShapeDtypeStruct((8, LANES), F32),
+        prepare_kernel,
+        in_specs=[STORED] * 2,
+        out_specs=[WHOLE] * 2,
+        out_shape=[
+            jax.ShapeDtypeStruct((8, LANES), F32),
+            jax.ShapeDtypeStruct(weight.shape, BF16),
+        ],
         scratch_shapes=[
             pltpu.VMEM((rows, cols), BF16),
             pltpu.VMEM((LANES, LANES), F32),
-            pltpu.SemaphoreType.DMA,
+            pltpu.SemaphoreType.DMA((2,)),
         ],
-        compiler_params=params(2 * rows * cols + 4 * LANES * LANES),
-        cost_estimate=cost(8 * rows * cols, 2 * rows * cols),
-        name="teacher_stats",
-    )(teacher)
+        compiler_params=pltpu.CompilerParams(vmem_limit_bytes=ROOM),
+        cost_estimate=cost(8 * rows * cols, 2 * rows * cols + 4 * weight.size),
+        name="prepare",
+    )(teacher, weight)
 
 
 def stack_kernel(*refs):
@@ -140,12 +148,14 @@
     return jnp.where((lane // size) % 2 == 0, pltpu.roll(x, lanes - size, 1), pltpu.roll(x, size, 1))
 
 
-def logit_grad_kernel(place, n_stats, tile, *refs):
+def logit_grad_kernel(place, part, n_stats, tile, *refs):
     stats = refs[:n_stats]
     teachers = refs[n_stats : n_stats + place.nv]
-    e_ref, g_ref, cols_sc = refs[n_stats + place.nv :]
-    rows = g_ref.shape[0]
+    e_ref, *before, g_ref, cols_sc = refs[n_stats + place.nv :]
+    rows = e_ref.shape[0]
     half = rows // 2
+    if part:
+        g_ref[:half, :] = before[0][...]
     v = lax.axis_index("vocab")
     me = lax.axis_index("head") * place.nv + v
 
@@ -181,81 +191,137 @@
             source = shifted(v >> 1, place.nz, place.nz - step) * 2 + jnp.bitwise_xor(v & 1, ck)
             vk = jnp.bitwise_xor(source, v)
             for sub in range(per):
-                can = source * per + sub
-                to = place.position(jnp.bitwise_xor(me, can)) * place.group
-                to = pl.ds(pl.multiple_of(to, place.group), place.group)
-                c = cols_sc[to, :]
-                at = pl.multiple_of((vk * per + sub) * place.group, place.group)
-                d = cols_sc[pl.ds(at, place.group), :]
+                can = (source * 2 + part) * per + sub
+                d = jnp.bitwise_xor(me, can)
+                at = pl.multiple_of(place.position(d) * place.group, place.group)
+                at = pl.ds(at, place.group)
+                to = pl.multiple_of(place.half_position(d) * place.group, place.group)
+                to = pl.ds(part * half + to, place.group)
+                c = cols_sc[at, :]
+                own = pl.multiple_of(((vk * 2 + part) * per + sub) * place.group, place.group)
+                own = cols_sc[pl.ds(own, place.group), :]
                 t = t_ref[sub * place.group : (sub + 1) * place.group, across].astype(F32)
-                q = jnp.exp(t - d[:, 1:2]) * d[:, 2:3]
-                g_ref[to, across] = (e_ref[to, across] * c[:, 0:1] - q).astype(BF16)
-
-
-def logit_grad(place, stats, teachers, e, tile):
+                q = jnp.exp(t - own[:, 1:2]) * own[:, 2:3]
+                g_ref[to, across] = (e_ref[at, across] * c[:, 0:1] - q).astype(BF16)
+
+
+def logit_grad(place, part, stats, teachers, e, before, tile):
     rows, cols = e.shape
-    return pl.pallas_call(
-        functools.partial(logit_grad_kernel, place, len(stats), tile),
-        in_specs=[WHOLE] * (len(stats) + len(teachers) + 1),
+    if not part:
+        rows //= 2
+    return pl.pallas_call(
+        functools.partial(logit_grad_kernel, place, part, len(stats), tile),
+        in_specs=[WHOLE] * (len(stats) + len(teachers) + 1 + len(before)),
         out_specs=WHOLE,
         out_shape=jax.ShapeDtypeStruct((rows, cols), BF16),
-        scratch_shapes=[pltpu.VMEM((rows, LANES), F32)],
-        compiler_params=params(4 * rows * LANES),
+        scratch_shapes=[pltpu.VMEM((e.shape[0], LANES), F32)],
+        compiler_params=params(4 * e.shape[0] * LANES),
         cost_estimate=cost(8 * rows * cols, 8 * rows * cols),
         name="logit_grad",
-    )(*stats, *teachers, e)
+    )(*stats, *teachers, e, *before)
 
 
 def input_grad_kernel(start, tile, g_ref, w_ref, keep_ref, send_ref):
-    half = g_ref.shape[0] // 2
+    half = keep_ref.shape[0]
+    g = g_ref.at[start : start + 2 * half]
 
     @pl.loop(0, keep_ref.shape[1] // tile)
     def _(j):
         at = pl.ds(pl.multiple_of(j * tile, tile), tile)
-        w = w_ref[pl.ds(pl.multiple_of(start + j * tile, tile), tile), :]
-        out = lax.dot_general(g_ref[...], w, NT, preferred_element_type=F32)
+        out = lax.dot_general(g[...], w_ref[at, :], NT, preferred_element_type=F32)
         keep_ref[:, at] = out[:half]
         send_ref[:, at] = out[half:].astype(BF16)
 
 
-def input_grad_part(g, weight, start, width, tile):
-    rows, cols = g.shape
+def input_grad_rows(g, weight, start, rows, tile):
+    depth, cols = weight.shape
     return pl.pallas_call(
         functools.partial(input_grad_kernel, start, tile),
         in_specs=[WHOLE] * 2,
         out_specs=[WHOLE] * 2,
         out_shape=[
-            jax.ShapeDtypeStruct((rows // 2, width), F32),
-            jax.ShapeDtypeStruct((rows // 2, width), BF16),
+            jax.ShapeDtypeStruct((rows // 2, depth), F32),
+            jax.ShapeDtypeStruct((rows // 2, depth), BF16),
         ],
-        compiler_params=params(4 * rows * tile),
-        cost_estimate=cost(2 * rows * cols * width, 2 * cols * (rows + width)),
+        compiler_params=params(8 * rows * tile),
+        cost_estimate=cost(2 * rows * cols * depth, 2 * cols * (rows + depth)),
         name="input_grad",
     )(g, weight)
 
 
-def turn_kernel(h_ref, w_hbm, o_ref, w_ref, sem):
-    copy = pltpu.make_async_copy(w_hbm, w_ref, sem)
-    copy.start()
-    o_ref[...] = h_ref[...].T
-    copy.wait()
-
-
-def turned(h, weight):
+def share(total, own_ref, sends):
+    rows = own_ref.shape[0]
+    own_ref[...] = total(0, rows)
+    for k, ref in enumerate(sends):
+        ref[...] = total((k + 1) * rows, (k + 2) * rows).astype(BF16)
+
+
+def core_kernel(keep_ref, got_ref, own_ref, *sends):
+    share(lambda a, b: keep_ref[a:b, :] + got_ref[a:b, :].astype(F32), own_ref, sends)
+
+
+def add_kernel(own_ref, *refs):
+    refs[-1][...] = own_ref[...] + sum(ref[...].astype(F32) for ref in refs[:-1])
+
+
+def chip_kernel(place, first_ref, second_ref, own_ref, *sends):
+    bit = (lax.axis_index("vocab") >> 1) & place.bit
+    group = place.group
+    for zk, ref in enumerate((own_ref, *sends)):
+        at = place.half_of(zk) * group
+        at = slice(at, at + group)
+
+        def put(source, ref=ref, at=at):
+            ref[...] = source[at, :].astype(ref.dtype)
+
+        pl.when(bit == zk & place.bit)(functools.partial(put, first_ref))
+        pl.when(bit != zk & place.bit)(functools.partial(put, second_ref))
+
+
+def small(kernel, args, shapes):
+    nbytes = sum(x.size * x.dtype.itemsize for x in (*args, *shapes))
+    return pl.pallas_call(
+        kernel,
+        in_specs=[WHOLE] * len(args),
+        out_specs=[WHOLE] * len(shapes),
+        out_shape=shapes,
+        compiler_params=params(0),
+        cost_estimate=cost(0, nbytes),
+    )(*args)
+
+
+def shares(rows, cols, count):
+    return [jax.ShapeDtypeStruct((rows, cols), BF16 if k else F32) for k in range(count)]
+
+
+def turn_kernel(place, h_ref, o_ref, h_sc):
+    bit = (lax.axis_index("vocab") >> 1) & place.bit
+    to = 0
+    for part in range(2):
+        for outer in range(place.nh * 2):
+            for zk in range(place.nz):
+                if zk & place.bit:
+                    continue
+                at = jnp.bitwise_xor(bit, zk | (part * place.bit)) & place.bit
+                at = (outer * place.nz + (zk | at)) * place.group
+                at = pl.ds(pl.multiple_of(at, place.group), place.group)
+                h_sc[to : to + place.group, :] = h_ref[at, :]
+                to += place.group
+    o_ref[...] = h_sc[...].T
+
+
+def turned(place, h):
     rows, depth = h.shape
     return pl.pallas_call(
-        turn_kernel,
-        in_specs=[WHOLE, pl.BlockSpec(memory_space=pl.ANY)],
-        out_specs=[WHOLE] * 2,
-        out_shape=[
-            jax.ShapeDtypeStruct((depth, rows), BF16),
-            jax.ShapeDtypeStruct(weight.shape, BF16),
-        ],
-        scratch_shapes=[pltpu.SemaphoreType.DMA],
-        compiler_params=params(0),
-        cost_estimate=cost(0, 4 * rows * depth + 4 * weight.size),
+        functools.partial(turn_kernel, place),
+        in_specs=[WHOLE],
+        out_specs=WHOLE,
+        out_shape=jax.ShapeDtypeStruct((depth, rows), BF16),
+        scratch_shapes=[pltpu.VMEM((rows, depth), BF16)],
+        compiler_params=params(2 * rows * depth),
+        cost_estimate=cost(0, 4 * rows * depth),
         name="turn",
-    )(h, weight)
+    )(h)
 
 
 def weight_grad_kernel(start, tile, ht_ref, g_ref, *refs):
@@ -286,16 +352,20 @@
 class Place:
     def __init__(self, nh, nv, group):
         self.nh, self.nv, self.nz, self.group = nh, nv, nv // 2, group
-
-    def bits(self, r):
-        ck, rest = divmod(r, self.nh * self.nz)
-        hk, zk = divmod(rest, self.nz)
-        return hk * self.nv + zk * 2 + ck
+        self.bit = nh // 4
 
     def position(self, d):
         hk, vk = d // self.nv, d % self.nv
         zk, ck = vk // 2, vk % 2
         return (ck * self.nh + hk) * self.nz + zk
+
+    def half_of(self, zk):
+        return ((zk >> 1) & ~(self.bit - 1)) | (zk & (self.bit - 1))
+
+    def half_position(self, d):
+        hk, vk = d // self.nv, d % self.nv
+        zk, ck = vk // 2, vk % 2
+        return (ck * self.nh + hk) * (self.nz // 2) + self.half_of(zk)
 
 
 def swap(x, axis, size, k):
@@ -325,9 +395,11 @@
     for k in range(nz - 1, 0, -1):
         near[k] = swap(hidden, "vocab", nv, 2 * k)
 
-    def piece(step, ck):
+    rows = teacher.shape[1] // 2
+
+    def piece(step, ck, part):
         to = shifted(z, nz, step) * 2 + (core ^ ck)
-        return lax.dynamic_slice(teacher, (0, 0, to * cols), (1, teacher.shape[1], cols))[0]
+        return lax.dynamic_slice(teacher, (0, part * rows, to * cols), (1, rows, cols))[0]
 
     def move(x, step, ck):
         pairs = [
@@ -337,14 +409,20 @@
 
     blocks = []
     pieces = lax.optimization_barrier(
-        tuple((piece(step, 0), piece(step, 1)) for step in range(nz))
+        tuple(
+            tuple((piece(step, 0, part), piece(step, 1, part)) for step in range(nz))
+            for part in range(2)
+        )
     )
-    for step in range(nz):
-        mine, cross = pieces[step]
-        if step:
-            mine = move(mine, step, 0)
-        cross = move(cross, step, 1)
-        blocks += [mine, cross]
+    for part in range(2):
+        half = []
+        for step in range(nz):
+            mine, cross = pieces[part][step]
+            if step:
+                mine = move(mine, step, 0)
+            cross = move(cross, step, 1)
+            half += [mine, cross]
+        blocks.append(half)
 
     block = stacked(near)
     own = [block]
@@ -354,38 +432,32 @@
     for k in range(nh):
         other.append(swap(own[k], "vocab", nv, 1))
 
-    tstat = teacher_stats(teacher)
-    e, h, stat = student(own + other, weight[0], tstat, teacher.shape[1], 512)
+    tstat, near_weight = prepared(teacher, weight[0])
+    e, h, stat = student(own + other, near_weight, tstat, teacher.shape[1], 512)
     pair = swap(stat, "vocab", nv, 1)
     pair = stacked([stat, pair])
     stats = [pair]
     for k in range(1, nz):
         stats.append(swap(pair, "vocab", nv, 2 * k))
-    ht, near_weight = turned(h, weight[0])
-    g = logit_grad(place, stats, blocks, e, 1024)
-
-    depth = weight.shape[1]
-    chunks = 2
-    width = depth // chunks
-    rows = place.group * nz
-    keeps, sums = [], []
-    for c in range(chunks):
-        keep, send = input_grad_part(g, near_weight, c * width, width, 512)
+    ht = turned(place, h)
+
+    rows, depth = place.group * nz // 2, weight.shape[1]
+    g, sums = (), []
+    for part in range(2):
+        g = (logit_grad(place, part, stats, blocks[part], e, g, 1024),)
+        start = part * e.shape[0] // 2
+        keep, send = input_grad_rows(g[0], near_weight, start, e.shape[0] // 2, 512)
         send = swap(send, "vocab", nv, 1)
-        keeps.append(keep + send.astype(F32))
-    for keep in keeps:
-        part = [keep[k * rows : (k + 1) * rows] for k in range(nh)]
-        total = part[0]
+        own, *piece = small(core_kernel, (keep, send), shares(rows, depth, nh))
         for k in range(1, nh):
-            part[k] = swap(part[k].astype(BF16), "head", nh, k)
-            total = total + part[k].astype(F32)
-        sums.append(total)
-    total = jnp.concatenate(sums, axis=1)
-    part = [total[k * place.group : (k + 1) * place.group] for k in range(nz)]
-    total = part[0]
+            piece[k - 1] = swap(piece[k - 1], "head", nh, k)
+        sums += small(add_kernel, (own, *piece), shares(rows, depth, 1))
+    kernel = functools.partial(chip_kernel, place)
+    own, *piece = small(kernel, sums, shares(place.group, depth, nz))
     for k in range(1, nz):
-        part[k] = swap(part[k].astype(BF16), "vocab", nv, 2 * k)
-        total = total + part[k].astype(F32)
+        piece[k - 1] = swap(piece[k - 1], "vocab", nv, 2 * k)
+    (total,) = small(add_kernel, (own, *piece), shares(place.group, depth, 1))
+    g = g[0]
     grad = None
     for part in range(PARTS):
         grad = weight_grad_part(ht, g, grad, part, PARTS, 256)
@@ -426,7 +498,7 @@
 
     def step(hidden, weight, teacher):
         group = hidden.shape[0] // (nh * nv)
-        plain = nh & (nh - 1) or nv & (nv - 1) or group % 16
+        plain = nh & (nh - 1) or nv & (nv - 1) or group % 16 or not 4 <= nh < 2 * nv
         run = jax.shard_map(
             functools.partial(per_device, nh, nv, plain),
             mesh=mesh,

time: 127 us -> 117 us (0.921)
  starting transfers between devices: 58.9 us -> 51.8 us
  Pallas kernels: 25.3 us -> 29.6 us
  local copies, waits for them, and re-layouts: 7.63 us -> 4.28 us
  waiting for transfers between devices: 32.6 us -> 30.6 us
    ppermute x25, starting transfers between devices: 51.7 us -> 31.1 us  [swap(): return lax.ppermute(x, axis, [(i, i ^ k) for i in range(size)])]
    ppermute x7 -> x14, starting transfers between devices: 7.19 us -> 20.7 us  [move(): return lax.ppermute(x, 'vocab', pairs)]
    ppermute x25, waiting for transfers between devices: 29.8 us -> 23.2 us  [swap(): return lax.ppermute(x, axis, [(i, i ^ k) for i in range(size)])]
    ppermute x7 -> x14, waiting for transfers between devices: 2.76 us -> 7.32 us  [move(): return lax.ppermute(x, 'vocab', pairs)]
    pallas_call x5 -> x12, Pallas kernels: 9.02 us -> 13.3 us  [the longest x2 5.93 us: input_grad_rows(): pl.pallas_call(functools.partial(input_grad_kernel, start, tile), in_spec...]
    unnamed x8 -> x4, local copies, waits for them, and re-layouts: 5.81 us -> 2.43 us
  transfers between devices with their start and end apart: 32 -> 39, of which waited for: 16 -> 16; matrix products, arithmetic and copies ran while one was open for 2% -> 2% of each run, Pallas kernels for 17% -> 25%
where the time goes in v3:
time: 117 us
  starting transfers between devices  51.8 us (44%)
  waiting for transfers between devices  30.6 us (26%)
  Pallas kernels  29.6 us (25%)
  local copies, waits for them, and re-layouts  4.28 us (4%)
    ppermute x25, starting transfers between devices, swap(): return lax.ppermute(x, axis, [(i, i ^ k) for i in range(size)])  31.1 us
    ppermute x25, waiting for transfers between devices, swap(): return lax.ppermute(x, axis, [(i, i ^ k) for i in range(size)])  23.2 us
    ppermute x14, starting transfers between devices, move(): return lax.ppermute(x, 'vocab', pairs)  20.7 us
    pallas_call x4, Pallas kernels, weight_grad_part(): pl.pallas_call(functools.partial(weight_grad_kernel, start, tile), grid=(...  9.68 us
    ppermute x14, waiting for transfers between devices, move(): return lax.ppermute(x, 'vocab', pairs)  7.32 us
    pallas_call x1, Pallas kernels, student(): pl.pallas_call(functools.partial(student_kernel, len(parts), tile, own),...  6.55 us
    pallas_call x2, Pallas kernels, input_grad_rows(): pl.pallas_call(functools.partial(input_grad_kernel, start, tile), in_spec...  5.93 us
    pallas_call x1, Pallas kernels, prepared(): pl.pallas_call(prepare_kernel, in_specs=[STORED] * 2, out_specs=[WHOLE] *...  3.54 us
  transfers between devices with their start and end apart: 39, of which 16 were waited for; matrix products, arithmetic and copies ran while one was open for 2% of the time, Pallas kernels for 25%

profile of v3, /device:TPU:0, one launch (start us, length us, event | category | flops | bytes accessed | tf_op | source)
XLA Modules:
  0.0 117.0 jit_solution(4029705610479028077)
XLA Ops:
  0.6 4.1 %collective-permute-start.1 = (bf16[16,2048]{1,0:T(8,128)(2,1)}, bf16[16,2048]{1,0:T(8,128)(2,1)S(1)}, u32[]{:S(2)}, u32[]{:S(2)}) collective-permute-start(bf16[16,2048]{1,0:T(8,128)(2,1)} %refs_0_.1), channel_id=1, source_target_pairs={{0,4},{1,5},{2,6},{3,7},{4,0},{5,1},{6,2},{7,3},{8,12},{9,13},{10,... | collective-permute-start | bytes 196616 | tf_op jit(solution)/shard_map/ppermute | solution.py:372
  4.8 1.6 %collective-permute-start = (bf16[16,2048]{1,0:T(8,128)(2,1)}, bf16[16,2048]{1,0:T(8,128)(2,1)S(1)}, u32[]{:S(2)}, u32[]{:S(2)}) collective-permute-start(bf16[16,2048]{1,0:T(8,128)(2,1)} %refs_0_.1), channel_id=1, source_target_pairs={{0,2},{1,3},{2,0},{3,1},{4,6},{5,7},{6,4},{7,5},{8,10},{9,11},{10,... | collective-permute-start | bytes 196616 | tf_op jit(solution)/shard_map/ppermute | solution.py:372
  6.3 1.7 %collective-permute-done.1.refs_2_ = bf16[16,2048]{1,0:T(8,128)(2,1)S(1)} collective-permute-done((bf16[16,2048]{1,0:T(8,128)(2,1)}, bf16[16,2048]{1,0:T(8,128)(2,1)S(1)}, u32[]{:S(2)}, u32[]{:S(2)}) %collective-permute-start.1) | collective-permute-done | bytes 65568 | tf_op jit(solution)/shard_map/ppermute | solution.py:372
  9.2 3.4 %collective-permute-done.2.refs_3_ = bf16[16,2048]{1,0:T(8,128)(2,1)S(1)} collective-permute-done((bf16[16,2048]{1,0:T(8,128)(2,1)}, bf16[16,2048]{1,0:T(8,128)(2,1)S(1)}, u32[]{:S(2)}, u32[]{:S(2)}) %collective-permute-start.2) | collective-permute-done | bytes 65568 | tf_op jit(solution)/shard_map/ppermute | solution.py:372
  13.5 2.5 %collective-permute-start.5 = (bf16[64,2048]{1,0:T(8,128)(2,1)S(1)}, bf16[64,2048]{1,0:T(8,128)(2,1)S(1)}, u32[]{:S(2)}, u32[]{:S(2)}) collective-permute-start(bf16[64,2048]{1,0:T(8,128)(2,1)S(1)} %shard_map.50.refs_0_), channel_id=1, source_target_pairs={{0,24},{8,16},{16,8},{24,0},{1,25},{9,17},{17,9},{25,1},{2,26},{10... | collective-permute-start | bytes 786440 | tf_op jit(solution)/shard_map/ppermute | solution.py:372
  17.0 1.8 %dynamic-slice_bitcast_fusion = (bf16[32,2048]{1,0:T(8,128)(2,1)S(1)}, bf16[32,2048]{1,0:T(8,128)(2,1)S(1)}, bf16[32,2048]{1,0:T(8,128)(2,1)S(1)}, bf16[32,2048]...) fusion(bf16[1,64,16384]{2,1,0:T(8,128)(2,1)} %t_hbm.1, ...), kind=kLoop, calls=%fused_computation | loop fusion | bytes 4194336 | tf_op jit(solution)/shard_map/squeeze | solution.py:402
  19.5 4.2 %collective-permute-done.5.refs_3_ = bf16[64,2048]{1,0:T(8,128)(2,1)S(1)} collective-permute-done((bf16[64,2048]{1,0:T(8,128)(2,1)S(1)}, bf16[64,2048]{1,0:T(8,128)(2,1)S(1)}, u32[]{:S(2)}, u32[]{:S(2)}) %collective-permute-start.5) | collective-permute-done | bytes 262176 | tf_op jit(solution)/shard_map/ppermute | solution.py:372
  23.6 2.9 %collective-permute-done.4.refs_2_ = bf16[64,2048]{1,0:T(8,128)(2,1)S(1)} collective-permute-done((bf16[64,2048]{1,0:T(8,128)(2,1)S(1)}, bf16[64,2048]{1,0:T(8,128)(2,1)S(1)}, u32[]{:S(2)}, u32[]{:S(2)}) %collective-permute-start.4) | collective-permute-done | bytes 262176 | tf_op jit(solution)/shard_map/ppermute | solution.py:372
  27.8 1.6 %copy-done = bf16[1,64,16384]{2,1,0:T(8,128)(2,1)S(1)} copy-done((bf16[1,64,16384]{2,1,0:T(8,128)(2,1)S(1)}, bf16[1,64,16384]{2,1,0:T(8,128)(2,1)}, u32[]{:S(2)}) %copy-start) | copy-done | bytes 2097176
  29.4 3.5 %prepare.1 = (f32[8,128]{1,0:T(8,128)S(1)}, bf16[2048,2048]{1,0:T(8,128)(2,1)S(1)}) custom-call(bf16[1,64,16384]{2,1,0:T(8,128)(2,1)S(1)} %copy-done, bf16[2048,2048]{1,0:T(8,128)(2,1)} %bitcast.33), custom_call_target="tpu_custom_call" | custom-call | flops 8388608 | bytes 18874368 | tf_op jit(solution)/shard_map/prepare/pallas_call | solution.py:61
  34.1 2.4 %collective-permute-start.24 = (bf16[32,2048]{1,0:T(8,128)(2,1)S(1)}, bf16[32,2048]{1,0:T(8,128)(2,1)S(1)}, u32[]{:S(2)}, u32[]{:S(2)}) collective-permute-start(bf16[32,2048]{1,0:T(8,128)(2,1)S(1)} %get-tuple-element.56), channel_id=1, source_target_pairs={{0,6},{1,7},{2,4},{3,5},{4,2},{5,3},{6,0},{7,1},{8,14},{9,15},{10,... | collective-permute-start | bytes 393224 | tf_op jit(solution)/shard_map/ppermute | solution.py:408
  38.3 2.1 %collective-permute-start.27 = (bf16[32,2048]{1,0:T(8,128)(2,1)S(1)}, bf16[32,2048]{1,0:T(8,128)(2,1)S(1)}, u32[]{:S(2)}, u32[]{:S(2)}) collective-permute-start(bf16[32,2048]{1,0:T(8,128)(2,1)S(1)} %get-tuple-element.59), channel_id=1, source_target_pairs={{0,5},{1,4},{2,1},{3,0},{4,7},{5,6},{6,3},{7,2},{8,13},{9,12},{10,... | collective-permute-start | bytes 393224 | tf_op jit(solution)/shard_map/ppermute | solution.py:408
  40.4 6.5 %student.1 = (f32[512,2048]{1,0:T(8,128)S(1)}, bf16[512,2048]{1,0:T(8,128)(2,1)S(1)}, f32[8,512]{1,0:T(8,128)S(1)}) custom-call(bf16[64,2048]{1,0:T(8,128)(2,1)S(1)} %shard_map.50.refs_0_, bf16[64,2048]{1,0:T(8,128)(2,1)S(1)} %collective-permute-done.3.refs_1_, bf16[64,2048]{1,0:T(8,128)(2,1)S(1)} %collective-permute-done.4.refs_2_, ...), custom_call_target="tpu_custom_call" | custom-call | flops 4294967296 | bytes 12582912 | tf_op jit(solution)/shard_map/student/pallas_call | solution.py:130
  48.1 6.4 %collective-permute-start.15 = (bf16[32,2048]{1,0:T(8,128)(2,1)S(1)}, bf16[32,2048]{1,0:T(8,128)(2,1)S(1)}, u32[]{:S(2)}, u32[]{:S(2)}) collective-permute-start(bf16[32,2048]{1,0:T(8,128)(2,1)S(1)} %get-tuple-element.45), channel_id=1, source_target_pairs={{0,2},{1,3},{2,6},{3,7},{4,0},{5,1},{6,4},{7,5},{8,10},{9,11},{10,... | collective-permute-start | bytes 393224 | tf_op jit(solution)/shard_map/ppermute | solution.py:408
  54.5 3.4 %collective-permute-start.13 = (f32[16,512]{1,0:T(8,128)S(1)}, f32[16,512]{1,0:T(8,128)S(1)}, u32[]{:S(2)}, u32[]{:S(2)}) collective-permute-start(f32[16,512]{1,0:T(8,128)S(1)} %shard_map.51.refs_0_), channel_id=1, source_target_pairs={{0,6},{1,7},{2,4},{3,5},{4,2},{5,3},{6,0},{7,1},{8,14},{9,15},{10,... | collective-permute-start | bytes 98312 | tf_op jit(solution)/shard_map/ppermute | solution.py:372
  59.8 2.6 %collective-permute-done.13.refs_3_ = f32[16,512]{1,0:T(8,128)S(1)} collective-permute-done((f32[16,512]{1,0:T(8,128)S(1)}, f32[16,512]{1,0:T(8,128)S(1)}, u32[]{:S(2)}, u32[]{:S(2)}) %collective-permute-start.13) | collective-permute-done | bytes 32800 | tf_op jit(solution)/shard_map/ppermute | solution.py:372
  63.1 2.6 %collective-permute-start.17 = (bf16[32,2048]{1,0:T(8,128)(2,1)S(1)}, bf16[32,2048]{1,0:T(8,128)(2,1)S(1)}, u32[]{:S(2)}, u32[]{:S(2)}) collective-permute-start(bf16[32,2048]{1,0:T(8,128)(2,1)S(1)} %get-tuple-element.47), channel_id=1, source_target_pairs={{0,6},{1,7},{2,4},{3,5},{4,2},{5,3},{6,0},{7,1},{8,14},{9,15},{10,... | collective-permute-start | bytes 393224 | tf_op jit(solution)/shard_map/ppermute | solution.py:408
  67.9 2.7 %collective-permute-start.20 = (bf16[32,2048]{1,0:T(8,128)(2,1)S(1)}, bf16[32,2048]{1,0:T(8,128)(2,1)S(1)}, u32[]{:S(2)}, u32[]{:S(2)}) collective-permute-start(bf16[32,2048]{1,0:T(8,128)(2,1)S(1)} %get-tuple-element.50), channel_id=1, source_target_pairs={{0,5},{1,4},{2,1},{3,0},{4,7},{5,6},{6,3},{7,2},{8,13},{9,12},{10,... | collective-permute-start | bytes 393224 | tf_op jit(solution)/shard_map/ppermute | solution.py:408
  70.7 3.0 %input_grad.2 = (f32[128,2048]{1,0:T(8,128)S(1)}, bf16[128,2048]{1,0:T(8,128)(2,1)S(1)}) custom-call(bf16[256,2048]{1,0:T(8,128)(2,1)S(1)} %logit_grad.2.refs_13_.g_ref, bf16[2048,2048]{1,0:T(8,128)(2,1)S(1)} %get-tuple-element.39.refs_8_.w_ref), custom_call_target="tpu_custom_call" | custom-call | flops 2147483648 | bytes 9437184 | tf_op jit(solution)/shard_map/input_grad/pallas_call | solution.py:238
  75.1 2.5 %collective-permute-done.19.refs_10_ = bf16[32,2048]{1,0:T(8,128)(2,1)S(1)} collective-permute-done((bf16[32,2048]{1,0:T(8,128)(2,1)S(1)}, bf16[32,2048]{1,0:T(8,128)(2,1)S(1)}, u32[]{:S(2)}, u32[]{:S(2)}) %collective-permute-start.19) | collective-permute-done | bytes 131104 | tf_op jit(solution)/shard_map/ppermute | solution.py:408
  77.6 2.8 %collective-permute-done.20.refs_11_ = bf16[32,2048]{1,0:T(8,128)(2,1)S(1)} collective-permute-done((bf16[32,2048]{1,0:T(8,128)(2,1)S(1)}, bf16[32,2048]{1,0:T(8,128)(2,1)S(1)}, u32[]{:S(2)}, u32[]{:S(2)}) %collective-permute-start.20) | collective-permute-done | bytes 131104 | tf_op jit(solution)/shard_map/ppermute | solution.py:408
  81.6 3.0 %input_grad.3 = (f32[128,2048]{1,0:T(8,128)S(1)}, bf16[128,2048]{1,0:T(8,128)(2,1)S(1)}) custom-call(bf16[512,2048]{1,0:T(8,128)(2,1)S(1)} %logit_grad.3.g_ref, bf16[2048,2048]{1,0:T(8,128)(2,1)S(1)} %get-tuple-element.39.refs_8_.w_ref), custom_call_target="tpu_custom_call" | custom-call | flops 2147483648 | bytes 9437184 | tf_op jit(solution)/shard_map/input_grad/pallas_call | solution.py:238
  84.8 1.6 %collective-permute-start.29 = (bf16[32,2048]{1,0:T(8,128)(2,1)S(1)}, bf16[32,2048]{1,0:T(8,128)(2,1)S(1)}, u32[]{:S(2)}, u32[]{:S(2)}) collective-permute-start(bf16[32,2048]{1,0:T(8,128)(2,1)S(1)} %get-tuple-element.63), channel_id=1, source_target_pairs={{0,8},{8,0},{16,24},{24,16},{1,9},{9,1},{17,25},{25,17},{2,10},{10... | collective-permute-start | bytes 393224 | tf_op jit(solution)/shard_map/ppermute | solution.py:372
  87.0 2.4 %weight_grad.4.refs_0_ = bf16[1,2048,2048]{2,1,0:T(8,128)(2,1)} custom-call(bf16[2048,512]{1,0:T(8,128)(2,1)S(1)} %turn.1.ht_ref, bf16[512,2048]{1,0:T(8,128)(2,1)S(1)} %logit_grad.3.g_ref), custom_call_target="tpu_custom_call" | custom-call | flops 1073741824 | bytes 2097152 | tf_op jit(solution)/shard_map/weight_grad/pallas_call | solution.py:339
  91.5 1.6 %collective-permute-start.33 = (bf16[32,2048]{1,0:T(8,128)(2,1)S(1)}, bf16[32,2048]{1,0:T(8,128)(2,1)S(1)}, u32[]{:S(2)}, u32[]{:S(2)}) collective-permute-start(bf16[32,2048]{1,0:T(8,128)(2,1)S(1)} %get-tuple-element.69), channel_id=1, source_target_pairs={{0,8},{8,0},{16,24},{24,16},{1,9},{9,1},{17,25},{25,17},{2,10},{10... | collective-permute-start | bytes 393224 | tf_op jit(solution)/shard_map/ppermute | solution.py:372
  95.1 2.4 %weight_grad.5.refs_0_ = bf16[1,2048,2048]{2,1,0:T(8,128)(2,1)} custom-call(bf16[2048,512]{1,0:T(8,128)(2,1)S(1)} %turn.1.ht_ref, bf16[512,2048]{1,0:T(8,128)(2,1)S(1)} %logit_grad.3.g_ref, bf16[1,2048,2048]{2,1,0:T(8,128)(2,1)} %weight_grad.4.refs_0_), custom_call_target="tpu_custom_call", output_to_operand_aliasing={{}: (2, {})} | custom-call | flops 1073741824 | bytes 2097152 | tf_op jit(solution)/shard_map/weight_grad/pallas_call | solution.py:339
  97.5 2.4 %weight_grad.6.refs_0_ = bf16[1,2048,2048]{2,1,0:T(8,128)(2,1)} custom-call(bf16[2048,512]{1,0:T(8,128)(2,1)S(1)} %turn.1.ht_ref, bf16[512,2048]{1,0:T(8,128)(2,1)S(1)} %logit_grad.3.g_ref, bf16[1,2048,2048]{2,1,0:T(8,128)(2,1)} %weight_grad.5.refs_0_), custom_call_target="tpu_custom_call", output_to_operand_aliasing={{}: (2, {})} | custom-call | flops 1073741824 | bytes 2097152 | tf_op jit(solution)/shard_map/weight_grad/pallas_call | solution.py:339
  100.1 3.3 %collective-permute-done.34.refs_1_ = bf16[32,2048]{1,0:T(8,128)(2,1)S(1)} collective-permute-done((bf16[32,2048]{1,0:T(8,128)(2,1)S(1)}, bf16[32,2048]{1,0:T(8,128)(2,1)S(1)}, u32[]{:S(2)}, u32[]{:S(2)}) %collective-permute-start.34) | collective-permute-done | bytes 131104 | tf_op jit(solution)/shard_map/ppermute | solution.py:372
  103.5 5.5 %collective-permute-start.36 = (bf16[16,2048]{1,0:T(8,128)(2,1)S(1)}, bf16[16,2048]{1,0:T(8,128)(2,1)S(1)}, u32[]{:S(2)}, u32[]{:S(2)}) collective-permute-start(bf16[16,2048]{1,0:T(8,128)(2,1)S(1)} %get-tuple-element.73), channel_id=1, source_target_pairs={{0,2},{1,3},{2,0},{3,1},{4,6},{5,7},{6,4},{7,5},{8,10},{9,11},{10,... | collective-permute-start | bytes 196616 | tf_op jit(solution)/shard_map/ppermute | solution.py:372
  109.1 2.4 %collective-permute-start.38 = (bf16[16,2048]{1,0:T(8,128)(2,1)S(1)}, bf16[16,2048]{1,0:T(8,128)(2,1)S(1)}, u32[]{:S(2)}, u32[]{:S(2)}) collective-permute-start(bf16[16,2048]{1,0:T(8,128)(2,1)S(1)} %get-tuple-element.75), channel_id=1, source_target_pairs={{0,6},{1,7},{2,4},{3,5},{4,2},{5,3},{6,0},{7,1},{8,14},{9,15},{10,... | collective-permute-start | bytes 196616 | tf_op jit(solution)/shard_map/ppermute | solution.py:372
  111.5 2.4 %weight_grad.7 = bf16[1,2048,2048]{2,1,0:T(8,128)(2,1)} custom-call(bf16[2048,512]{1,0:T(8,128)(2,1)S(1)} %turn.1.ht_ref, bf16[512,2048]{1,0:T(8,128)(2,1)S(1)} %logit_grad.3.g_ref, bf16[1,2048,2048]{2,1,0:T(8,128)(2,1)} %weight_grad.6.refs_0_), custom_call_target="tpu_custom_call", output_to_operand_aliasing={{}: (2, {})} | custom-call | flops 1073741824 | bytes 2097152 | tf_op jit(solution)/shard_map/weight_grad/pallas_call | solution.py:339
  113.9 2.4 %collective-permute-done.37.refs_1_ = bf16[16,2048]{1,0:T(8,128)(2,1)S(1)} collective-permute-done((bf16[16,2048]{1,0:T(8,128)(2,1)S(1)}, bf16[16,2048]{1,0:T(8,128)(2,1)S(1)}, u32[]{:S(2)}, u32[]{:S(2)}) %collective-permute-start.37) | collective-permute-done | bytes 65568 | tf_op jit(solution)/shard_map/ppermute | solution.py:372
  (70 shorter events, 22.5 us)
Async XLA Ops:
  0.6 7.4 %collective-permute-start.1 = (bf16[16,2048]{1,0:T(8,128)(2,1)}, bf16[16,2048]{1,0:T(8,128)(2,1)S(1)}, u32[]{:S(2)}, u32[]{:S(2)}) collective-permute-start(bf16[16,2048]{1,0:T(8,128)(2,1)} %refs_0_.1), channel_id=1, source_target_pairs={{0,4},{1,5},{2,6},{3,7},{4,0},{5,1},{6,2},{7,3},{8,12},{9,13},{10,... | collective-permute-start | bytes 196616 | tf_op jit(solution)/shard_map/ppermute | solution.py:372
  13.5 10.2 %collective-permute-start.5 = (bf16[64,2048]{1,0:T(8,128)(2,1)S(1)}, bf16[64,2048]{1,0:T(8,128)(2,1)S(1)}, u32[]{:S(2)}, u32[]{:S(2)}) collective-permute-start(bf16[64,2048]{1,0:T(8,128)(2,1)S(1)} %shard_map.50.refs_0_), channel_id=1, source_target_pairs={{0,24},{8,16},{16,8},{24,0},{1,25},{9,17},{17,9},{25,1},{2,26},{10... | collective-permute-start | bytes 786440 | tf_op jit(solution)/shard_map/ppermute | solution.py:372
  16.0 10.5 %collective-permute-start.4 = (bf16[64,2048]{1,0:T(8,128)(2,1)S(1)}, bf16[64,2048]{1,0:T(8,128)(2,1)S(1)}, u32[]{:S(2)}, u32[]{:S(2)}) collective-permute-start(bf16[64,2048]{1,0:T(8,128)(2,1)S(1)} %shard_map.50.refs_0_), channel_id=1, source_target_pairs={{0,16},{8,24},{16,0},{24,8},{1,17},{9,25},{17,1},{25,9},{2,18},{10... | collective-permute-start | bytes 786440 | tf_op jit(solution)/shard_map/ppermute | solution.py:372
  16.5 10.1 %collective-permute-start.3 = (bf16[64,2048]{1,0:T(8,128)(2,1)S(1)}, bf16[64,2048]{1,0:T(8,128)(2,1)S(1)}, u32[]{:S(2)}, u32[]{:S(2)}) collective-permute-start(bf16[64,2048]{1,0:T(8,128)(2,1)S(1)} %shard_map.50.refs_0_), channel_id=1, source_target_pairs={{0,8},{8,0},{16,24},{24,16},{1,9},{9,1},{17,25},{25,17},{2,10},{10... | collective-permute-start | bytes 786440 | tf_op jit(solution)/shard_map/ppermute | solution.py:372
  18.9 8.1 %collective-permute-start.21 = (bf16[32,2048]{1,0:T(8,128)(2,1)S(1)}, bf16[32,2048]{1,0:T(8,128)(2,1)S(1)}, u32[]{:S(2)}, u32[]{:S(2)}) collective-permute-start(bf16[32,2048]{1,0:T(8,128)(2,1)S(1)} %get-tuple-element.53), channel_id=1, source_target_pairs={{0,1},{1,0},{2,3},{3,2},{4,5},{5,4},{6,7},{7,6},{8,9},{9,8},{10,11... | collective-permute-start | bytes 393224 | tf_op jit(solution)/shard_map/ppermute | solution.py:408
  19.0 15.2 %collective-permute-start.6 = (bf16[64,2048]{1,0:T(8,128)(2,1)S(1)}, bf16[64,2048]{1,0:T(8,128)(2,1)S(1)}, u32[]{:S(2)}, u32[]{:S(2)}) collective-permute-start(bf16[64,2048]{1,0:T(8,128)(2,1)S(1)} %shard_map.50.refs_0_), channel_id=1, source_target_pairs={{0,1},{1,0},{2,3},{3,2},{4,5},{5,4},{6,7},{7,6},{8,9},{9,8},{10,11... | collective-permute-start | bytes 786440 | tf_op jit(solution)/shard_map/ppermute | solution.py:372
  23.6 12.9 %collective-permute-start.9 = (bf16[64,2048]{1,0:T(8,128)(2,1)S(1)}, bf16[64,2048]{1,0:T(8,128)(2,1)S(1)}, u32[]{:S(2)}, u32[]{:S(2)}) collective-permute-start(bf16[64,2048]{1,0:T(8,128)(2,1)S(1)} %collective-permute-done.5.refs_3_), channel_id=1, source_target_pairs={{0,1},{1,0},{2,3},{3,2},{4,5},{5,4},{6,7},{7,6},{8,9},{9,8},{10,11... | collective-permute-start | bytes 786440 | tf_op jit(solution)/shard_map/ppermute | solution.py:372
  26.5 11.5 %collective-permute-start.8 = (bf16[64,2048]{1,0:T(8,128)(2,1)S(1)}, bf16[64,2048]{1,0:T(8,128)(2,1)S(1)}, u32[]{:S(2)}, u32[]{:S(2)}) collective-permute-start(bf16[64,2048]{1,0:T(8,128)(2,1)S(1)} %collective-permute-done.4.refs_2_), channel_id=1, source_target_pairs={{0,1},{1,0},{2,3},{3,2},{4,5},{5,4},{6,7},{7,6},{8,9},{9,8},{10,11... | collective-permute-start | bytes 786440 | tf_op jit(solution)/shard_map/ppermute | solution.py:372
  26.6 11.7 %collective-permute-start.7 = (bf16[64,2048]{1,0:T(8,128)(2,1)S(1)}, bf16[64,2048]{1,0:T(8,128)(2,1)S(1)}, u32[]{:S(2)}, u32[]{:S(2)}) collective-permute-start(bf16[64,2048]{1,0:T(8,128)(2,1)S(1)} %collective-permute-done.3.refs_1_), channel_id=1, source_target_pairs={{0,1},{1,0},{2,3},{3,2},{4,5},{5,4},{6,7},{7,6},{8,9},{9,8},{10,11... | collective-permute-start | bytes 786440 | tf_op jit(solution)/shard_map/ppermute | solution.py:372
  33.5 13.4 %collective-permute-start.23 = (bf16[32,2048]{1,0:T(8,128)(2,1)S(1)}, bf16[32,2048]{1,0:T(8,128)(2,1)S(1)}, u32[]{:S(2)}, u32[]{:S(2)}) collective-permute-start(bf16[32,2048]{1,0:T(8,128)(2,1)S(1)} %get-tuple-element.55), channel_id=1, source_target_pairs={{0,3},{1,2},{2,7},{3,6},{4,1},{5,0},{6,5},{7,4},{8,11},{9,10},{10,... | collective-permute-start | bytes 393224 | tf_op jit(solution)/shard_map/ppermute | solution.py:408
  34.1 13.2 %collective-permute-start.24 = (bf16[32,2048]{1,0:T(8,128)(2,1)S(1)}, bf16[32,2048]{1,0:T(8,128)(2,1)S(1)}, u32[]{:S(2)}, u32[]{:S(2)}) collective-permute-start(bf16[32,2048]{1,0:T(8,128)(2,1)S(1)} %get-tuple-element.56), channel_id=1, source_target_pairs={{0,6},{1,7},{2,4},{3,5},{4,2},{5,3},{6,0},{7,1},{8,14},{9,15},{10,... | collective-permute-start | bytes 393224 | tf_op jit(solution)/shard_map/ppermute | solution.py:408
  36.5 18.0 %collective-permute-start.25 = (bf16[32,2048]{1,0:T(8,128)(2,1)S(1)}, bf16[32,2048]{1,0:T(8,128)(2,1)S(1)}, u32[]{:S(2)}, u32[]{:S(2)}) collective-permute-start(bf16[32,2048]{1,0:T(8,128)(2,1)S(1)} %get-tuple-element.57), channel_id=1, source_target_pairs={{0,7},{1,6},{2,5},{3,4},{4,3},{5,2},{6,1},{7,0},{8,15},{9,14},{10,... | collective-permute-start | bytes 393224 | tf_op jit(solution)/shard_map/ppermute | solution.py:408
  38.0 19.9 %collective-permute-start.26 = (bf16[32,2048]{1,0:T(8,128)(2,1)S(1)}, bf16[32,2048]{1,0:T(8,128)(2,1)S(1)}, u32[]{:S(2)}, u32[]{:S(2)}) collective-permute-start(bf16[32,2048]{1,0:T(8,128)(2,1)S(1)} %get-tuple-element.58), channel_id=1, source_target_pairs={{0,4},{1,5},{2,0},{3,1},{4,6},{5,7},{6,2},{7,3},{8,12},{9,13},{10,... | collective-permute-start | bytes 393224 | tf_op jit(solution)/shard_map/ppermute | solution.py:408
  38.3 20.9 %collective-permute-start.27 = (bf16[32,2048]{1,0:T(8,128)(2,1)S(1)}, bf16[32,2048]{1,0:T(8,128)(2,1)S(1)}, u32[]{:S(2)}, u32[]{:S(2)}) collective-permute-start(bf16[32,2048]{1,0:T(8,128)(2,1)S(1)} %get-tuple-element.59), channel_id=1, source_target_pairs={{0,5},{1,4},{2,1},{3,0},{4,7},{5,6},{6,3},{7,2},{8,13},{9,12},{10,... | collective-permute-start | bytes 393224 | tf_op jit(solution)/shard_map/ppermute | solution.py:408
  47.3 19.5 %collective-permute-start.14 = (bf16[32,2048]{1,0:T(8,128)(2,1)S(1)}, bf16[32,2048]{1,0:T(8,128)(2,1)S(1)}, u32[]{:S(2)}, u32[]{:S(2)}) collective-permute-start(bf16[32,2048]{1,0:T(8,128)(2,1)S(1)} %get-tuple-element.44), channel_id=1, source_target_pairs={{0,1},{1,0},{2,3},{3,2},{4,5},{5,4},{6,7},{7,6},{8,9},{9,8},{10,11... | collective-permute-start | bytes 393224 | tf_op jit(solution)/shard_map/ppermute | solution.py:408
  48.1 19.8 %collective-permute-start.15 = (bf16[32,2048]{1,0:T(8,128)(2,1)S(1)}, bf16[32,2048]{1,0:T(8,128)(2,1)S(1)}, u32[]{:S(2)}, u32[]{:S(2)}) collective-permute-start(bf16[32,2048]{1,0:T(8,128)(2,1)S(1)} %get-tuple-element.45), channel_id=1, source_target_pairs={{0,2},{1,3},{2,6},{3,7},{4,0},{5,1},{6,4},{7,5},{8,10},{9,11},{10,... | collective-permute-start | bytes 393224 | tf_op jit(solution)/shard_map/ppermute | solution.py:408
  54.5 7.8 %collective-permute-start.13 = (f32[16,512]{1,0:T(8,128)S(1)}, f32[16,512]{1,0:T(8,128)S(1)}, u32[]{:S(2)}, u32[]{:S(2)}) collective-permute-start(f32[16,512]{1,0:T(8,128)S(1)} %shard_map.51.refs_0_), channel_id=1, source_target_pairs={{0,6},{1,7},{2,4},{3,5},{4,2},{5,3},{6,0},{7,1},{8,14},{9,15},{10,... | collective-permute-start | bytes 98312 | tf_op jit(solution)/shard_map/ppermute | solution.py:372
  62.4 11.3 %collective-permute-start.16 = (bf16[32,2048]{1,0:T(8,128)(2,1)S(1)}, bf16[32,2048]{1,0:T(8,128)(2,1)S(1)}, u32[]{:S(2)}, u32[]{:S(2)}) collective-permute-start(bf16[32,2048]{1,0:T(8,128)(2,1)S(1)} %get-tuple-element.46), channel_id=1, source_target_pairs={{0,3},{1,2},{2,7},{3,6},{4,1},{5,0},{6,5},{7,4},{8,11},{9,10},{10,... | collective-permute-start | bytes 393224 | tf_op jit(solution)/shard_map/ppermute | solution.py:408
  63.1 10.7 %collective-permute-start.17 = (bf16[32,2048]{1,0:T(8,128)(2,1)S(1)}, bf16[32,2048]{1,0:T(8,128)(2,1)S(1)}, u32[]{:S(2)}, u32[]{:S(2)}) collective-permute-start(bf16[32,2048]{1,0:T(8,128)(2,1)S(1)} %get-tuple-element.47), channel_id=1, source_target_pairs={{0,6},{1,7},{2,4},{3,5},{4,2},{5,3},{6,0},{7,1},{8,14},{9,15},{10,... | collective-permute-start | bytes 393224 | tf_op jit(solution)/shard_map/ppermute | solution.py:408
  65.6 9.5 %collective-permute-start.18 = (bf16[32,2048]{1,0:T(8,128)(2,1)S(1)}, bf16[32,2048]{1,0:T(8,128)(2,1)S(1)}, u32[]{:S(2)}, u32[]{:S(2)}) collective-permute-start(bf16[32,2048]{1,0:T(8,128)(2,1)S(1)} %get-tuple-element.48), channel_id=1, source_target_pairs={{0,7},{1,6},{2,5},{3,4},{4,3},{5,2},{6,1},{7,0},{8,15},{9,14},{10,... | collective-permute-start | bytes 393224 | tf_op jit(solution)/shard_map/ppermute | solution.py:408
  66.8 10.9 %collective-permute-start.19 = (bf16[32,2048]{1,0:T(8,128)(2,1)S(1)}, bf16[32,2048]{1,0:T(8,128)(2,1)S(1)}, u32[]{:S(2)}, u32[]{:S(2)}) collective-permute-start(bf16[32,2048]{1,0:T(8,128)(2,1)S(1)} %get-tuple-element.49), channel_id=1, source_target_pairs={{0,4},{1,5},{2,0},{3,1},{4,6},{5,7},{6,2},{7,3},{8,12},{9,13},{10,... | collective-permute-start | bytes 393224 | tf_op jit(solution)/shard_map/ppermute | solution.py:408
  67.9 12.5 %collective-permute-start.20 = (bf16[32,2048]{1,0:T(8,128)(2,1)S(1)}, bf16[32,2048]{1,0:T(8,128)(2,1)S(1)}, u32[]{:S(2)}, u32[]{:S(2)}) collective-permute-start(bf16[32,2048]{1,0:T(8,128)(2,1)S(1)} %get-tuple-element.50), channel_id=1, source_target_pairs={{0,5},{1,4},{2,1},{3,0},{4,7},{5,6},{6,3},{7,2},{8,13},{9,12},{10,... | collective-permute-start | bytes 393224 | tf_op jit(solution)/shard_map/ppermute | solution.py:408
  73.6 11.1 %collective-permute-start.28 = (bf16[128,2048]{1,0:T(8,128)(2,1)S(1)}, bf16[128,2048]{1,0:T(8,128)(2,1)S(1)}, u32[]{:S(2)}, u32[]{:S(2)}) collective-permute-start(bf16[128,2048]{1,0:T(8,128)(2,1)S(1)} %get-tuple-element.61), channel_id=1, source_target_pairs={{0,1},{1,0},{2,3},{3,2},{4,5},{5,4},{6,7},{7,6},{8,9},{9,8},{10,11... | collective-permute-start | bytes 1572872 | tf_op jit(solution)/shard_map/ppermute | solution.py:372
  84.8 9.1 %collective-permute-start.29 = (bf16[32,2048]{1,0:T(8,128)(2,1)S(1)}, bf16[32,2048]{1,0:T(8,128)(2,1)S(1)}, u32[]{:S(2)}, u32[]{:S(2)}) collective-permute-start(bf16[32,2048]{1,0:T(8,128)(2,1)S(1)} %get-tuple-element.63), channel_id=1, source_target_pairs={{0,8},{8,0},{16,24},{24,16},{1,9},{9,1},{17,25},{25,17},{2,10},{10... | collective-permute-start | bytes 393224 | tf_op jit(solution)/shard_map/ppermute | solution.py:372
  89.4 10.5 %collective-permute-start.30 = (bf16[32,2048]{1,0:T(8,128)(2,1)S(1)}, bf16[32,2048]{1,0:T(8,128)(2,1)S(1)}, u32[]{:S(2)}, u32[]{:S(2)}) collective-permute-start(bf16[32,2048]{1,0:T(8,128)(2,1)S(1)} %get-tuple-element.64), channel_id=1, source_target_pairs={{0,16},{8,24},{16,0},{24,8},{1,17},{9,25},{17,1},{25,9},{2,18},{10... | collective-permute-start | bytes 393224 | tf_op jit(solution)/shard_map/ppermute | solution.py:372
  90.2 9.7 %collective-permute-start.31 = (bf16[32,2048]{1,0:T(8,128)(2,1)S(1)}, bf16[32,2048]{1,0:T(8,128)(2,1)S(1)}, u32[]{:S(2)}, u32[]{:S(2)}) collective-permute-start(bf16[32,2048]{1,0:T(8,128)(2,1)S(1)} %get-tuple-element.65), channel_id=1, source_target_pairs={{0,24},{8,16},{16,8},{24,0},{1,25},{9,17},{17,9},{25,1},{2,26},{10... | collective-permute-start | bytes 393224 | tf_op jit(solution)/shard_map/ppermute | solution.py:372
  91.5 8.6 %collective-permute-start.33 = (bf16[32,2048]{1,0:T(8,128)(2,1)S(1)}, bf16[32,2048]{1,0:T(8,128)(2,1)S(1)}, u32[]{:S(2)}, u32[]{:S(2)}) collective-permute-start(bf16[32,2048]{1,0:T(8,128)(2,1)S(1)} %get-tuple-element.69), channel_id=1, source_target_pairs={{0,8},{8,0},{16,24},{24,16},{1,9},{9,1},{17,25},{25,17},{2,10},{10... | collective-permute-start | bytes 393224 | tf_op jit(solution)/shard_map/ppermute | solution.py:372
  93.1 10.3 %collective-permute-start.34 = (bf16[32,2048]{1,0:T(8,128)(2,1)S(1)}, bf16[32,2048]{1,0:T(8,128)(2,1)S(1)}, u32[]{:S(2)}, u32[]{:S(2)}) collective-permute-start(bf16[32,2048]{1,0:T(8,128)(2,1)S(1)} %get-tuple-element.70), channel_id=1, source_target_pairs={{0,16},{8,24},{16,0},{24,8},{1,17},{9,25},{17,1},{25,9},{2,18},{10... | collective-permute-start | bytes 393224 | tf_op jit(solution)/shard_map/ppermute | solution.py:372
  93.9 9.5 %collective-permute-start.35 = (bf16[32,2048]{1,0:T(8,128)(2,1)S(1)}, bf16[32,2048]{1,0:T(8,128)(2,1)S(1)}, u32[]{:S(2)}, u32[]{:S(2)}) collective-permute-start(bf16[32,2048]{1,0:T(8,128)(2,1)S(1)} %get-tuple-element.71), channel_id=1, source_target_pairs={{0,24},{8,16},{16,8},{24,0},{1,25},{9,17},{17,9},{25,1},{2,26},{10... | collective-permute-start | bytes 393224 | tf_op jit(solution)/shard_map/ppermute | solution.py:372
  103.5 10.4 %collective-permute-start.36 = (bf16[16,2048]{1,0:T(8,128)(2,1)S(1)}, bf16[16,2048]{1,0:T(8,128)(2,1)S(1)}, u32[]{:S(2)}, u32[]{:S(2)}) collective-permute-start(bf16[16,2048]{1,0:T(8,128)(2,1)S(1)} %get-tuple-element.73), channel_id=1, source_target_pairs={{0,2},{1,3},{2,0},{3,1},{4,6},{5,7},{6,4},{7,5},{8,10},{9,11},{10,... | collective-permute-start | bytes 196616 | tf_op jit(solution)/shard_map/ppermute | solution.py:372
  109.0 7.3 %collective-permute-start.37 = (bf16[16,2048]{1,0:T(8,128)(2,1)S(1)}, bf16[16,2048]{1,0:T(8,128)(2,1)S(1)}, u32[]{:S(2)}, u32[]{:S(2)}) collective-permute-start(bf16[16,2048]{1,0:T(8,128)(2,1)S(1)} %get-tuple-element.74), channel_id=1, source_target_pairs={{0,4},{1,5},{2,6},{3,7},{4,0},{5,1},{6,2},{7,3},{8,12},{9,13},{10,... | collective-permute-start | bytes 196616 | tf_op jit(solution)/shard_map/ppermute | solution.py:372
  109.1 7.3 %collective-permute-start.38 = (bf16[16,2048]{1,0:T(8,128)(2,1)S(1)}, bf16[16,2048]{1,0:T(8,128)(2,1)S(1)}, u32[]{:S(2)}, u32[]{:S(2)}) collective-permute-start(bf16[16,2048]{1,0:T(8,128)(2,1)S(1)} %get-tuple-element.75), channel_id=1, source_target_pairs={{0,6},{1,7},{2,4},{3,5},{4,2},{5,3},{6,0},{7,1},{8,14},{9,15},{10,... | collective-permute-start | bytes 196616 | tf_op jit(solution)/shard_map/ppermute | solution.py:372
  (9 other events, 39.4 us)

commit v4 on v3

--- a/solution.py
+++ b/solution.py
@@ -29,52 +29,52 @@
 STORED = pl.BlockSpec(memory_space=pltpu.HBM)
 
 
-def prepare_kernel(t_hbm, w_hbm, o_ref, w_ref, x_ref, cols_sc, sem):
-    copy = pltpu.make_async_copy(t_hbm.at[0], x_ref, sem.at[0])
-    copy.start()
-    weight = pltpu.make_async_copy(w_hbm, w_ref, sem.at[1])
+def prepare_kernel(*refs):
+    pieces, (w_hbm, o_ref, w_ref, cols_sc, sem) = refs[:-5], refs[-5:]
+    weight = pltpu.make_async_copy(w_hbm, w_ref, sem)
     weight.start()
-    rows, cols = x_ref.shape
+    half, cols = pieces[0].shape
     cols_sc[...] = jnp.zeros_like(cols_sc)
     step = 16
     lane = lax.broadcasted_iota(jnp.int32, (step, LANES), 1)
-    copy.wait()
-    for at in range(0, rows, step):
-        pieces = [slice(c, c + LANES) for c in range(0, cols, LANES)]
+    count = len(pieces) // 2
+    for at in range(0, 2 * half, step):
+        part, row = divmod(at, half)
+        row = slice(row, row + step)
+        views = [
+            (ref, slice(c, c + LANES))
+            for ref in pieces[part * count : (part + 1) * count]
+            for c in range(0, cols, LANES)
+        ]
         top = [jnp.full((step, LANES), -jnp.inf, F32)] * 4
-        for i, c in enumerate(pieces):
-            top[i % 4] = jnp.maximum(top[i % 4], x_ref[at : at + step, c].astype(F32))
-        top = functools.reduce(jnp.maximum, top)
-        top = jnp.max(top, axis=1, keepdims=True)
+        for i, (ref, c) in enumerate(views):
+            top[i % 4] = jnp.maximum(top[i % 4], ref[row, c].astype(F32))
+        top = jnp.max(functools.reduce(jnp.maximum, top), axis=1, keepdims=True)
         wide = jnp.broadcast_to(top, (step, LANES))
         total = [jnp.zeros((step, LANES), F32)] * 4
-        for i, c in enumerate(pieces):
-            total[i % 4] = total[i % 4] + jnp.exp(x_ref[at : at + step, c].astype(F32) - wide)
+        for i, (ref, c) in enumerate(views):
+            total[i % 4] = total[i % 4] + jnp.exp(ref[row, c].astype(F32) - wide)
         total = jnp.sum(sum(total), axis=1, keepdims=True)
         cols_sc[at : at + step, :] = jnp.where(lane == 0, wide, jnp.where(lane == 1, total, 0.0))
     o_ref[...] = cols_sc[...].T[:8, :]
     weight.wait()
 
 
-def prepared(teacher, weight):
-    _, rows, cols = teacher.shape
+def prepared(pieces, weight):
+    rows, cols = pieces[0].shape
     return pl.pallas_call(
         prepare_kernel,
-        in_specs=[STORED] * 2,
+        in_specs=[WHOLE] * len(pieces) + [STORED],
         out_specs=[WHOLE] * 2,
         out_shape=[
             jax.ShapeDtypeStruct((8, LANES), F32),
             jax.ShapeDtypeStruct(weight.shape, BF16),
         ],
-        scratch_shapes=[
-            pltpu.VMEM((rows, cols), BF16),
-            pltpu.VMEM((LANES, LANES), F32),
-            pltpu.SemaphoreType.DMA((2,)),
-        ],
+        scratch_shapes=[pltpu.VMEM((LANES, LANES), F32), pltpu.SemaphoreType.DMA],
         compiler_params=pltpu.CompilerParams(vmem_limit_bytes=ROOM),
-        cost_estimate=cost(8 * rows * cols, 2 * rows * cols + 4 * weight.size),
+        cost_estimate=cost(8 * rows * cols * len(pieces), 4 * weight.size),
         name="prepare",
-    )(teacher, weight)
+    )(*pieces, weight)
 
 
 def stack_kernel(*refs):
@@ -424,6 +424,7 @@
             half += [mine, cross]
         blocks.append(half)
 
+    near[0] = stacked(near[:1])
     block = stacked(near)
     own = [block]
     for k in range(1, nh):
@@ -432,8 +433,9 @@
     for k in range(nh):
         other.append(swap(own[k], "vocab", nv, 1))
 
-    tstat, near_weight = prepared(teacher, weight[0])
-    e, h, stat = student(own + other, near_weight, tstat, teacher.shape[1], 512)
+    flat = [x for half in pieces for pair in half for x in pair]
+    tstat, near_weight = prepared(flat, weight[0])
+    e, h, stat = student(own + other, near_weight, tstat, teacher.shape[1], 1024)
     pair = swap(stat, "vocab", nv, 1)
     pair = stacked([stat, pair])
     stats = [pair]
@@ -444,9 +446,9 @@
     rows, depth = place.group * nz // 2, weight.shape[1]
     g, sums = (), []
     for part in range(2):
-        g = (logit_grad(place, part, stats, blocks[part], e, g, 1024),)
+        g = (logit_grad(place, part, stats, blocks[part], e, g, 2048),)
         start = part * e.shape[0] // 2
-        keep, send = input_grad_rows(g[0], near_weight, start, e.shape[0] // 2, 512)
+        keep, send = input_grad_rows(g[0], near_weight, start, e.shape[0] // 2, 2048)
         send = swap(send, "vocab", nv, 1)
         own, *piece = small(core_kernel, (keep, send), shares(rows, depth, nh))
         for k in range(1, nh):
@@ -460,11 +462,11 @@
     g = g[0]
     grad = None
     for part in range(PARTS):
-        grad = weight_grad_part(ht, g, grad, part, PARTS, 256)
+        grad = weight_grad_part(ht, g, grad, part, PARTS, 512)
     return (grad, total)
 
 
-PARTS = 4
+PARTS = 2
 
 
 def gathered(hidden, weight, teacher):

time: 117 us -> 113 us (0.966)
  waiting for transfers between devices: 30.6 us -> 39.7 us
  starting transfers between devices: 51.8 us -> 43.5 us
  Pallas kernels: 29.6 us -> 26.2 us
  local copies, waits for them, and re-layouts: 4.28 us -> 2.72 us
    ppermute x14, waiting for transfers between devices: 7.32 us -> 16.3 us  [move(): return lax.ppermute(x, 'vocab', pairs)]
    ppermute x14, starting transfers between devices: 20.7 us -> 13 us  [move(): return lax.ppermute(x, 'vocab', pairs)]
    pallas_call x4 -> x2, Pallas kernels: 9.68 us -> 7.68 us  [weight_grad_part(): pl.pallas_call(functools.partial(weight_grad_kernel, start, tile), grid=(...]
    unnamed x4 -> x2, local copies, waits for them, and re-layouts: 2.43 us -> 0.87 us
    pallas_call x2, Pallas kernels: 5.93 us -> 4.73 us  [input_grad_rows(): pl.pallas_call(functools.partial(input_grad_kernel, start, tile), in_spec...]
  transfers between devices with their start and end apart: 39 -> 39, of which waited for: 16 -> 14; matrix products, arithmetic and copies ran while one was open for 2% -> 2% of each run, Pallas kernels for 25% -> 22%
where the time goes in v4:
time: 113 us
  starting transfers between devices  43.5 us (38%)
  waiting for transfers between devices  39.7 us (35%)
  Pallas kernels  26.2 us (23%)
  local copies, waits for them, and re-layouts  2.72 us (2%)
    ppermute x25, starting transfers between devices, swap(): return lax.ppermute(x, axis, [(i, i ^ k) for i in range(size)])  30.5 us
    ppermute x25, waiting for transfers between devices, swap(): return lax.ppermute(x, axis, [(i, i ^ k) for i in range(size)])  23.4 us
    ppermute x14, waiting for transfers between devices, move(): return lax.ppermute(x, 'vocab', pairs)  16.3 us
    ppermute x14, starting transfers between devices, move(): return lax.ppermute(x, 'vocab', pairs)  13 us
    pallas_call x2, Pallas kernels, weight_grad_part(): pl.pallas_call(functools.partial(weight_grad_kernel, start, tile), grid=(...  7.68 us
    pallas_call x1, Pallas kernels, student(): pl.pallas_call(functools.partial(student_kernel, len(parts), tile, own),...  6.58 us
    pallas_call x2, Pallas kernels, input_grad_rows(): pl.pallas_call(functools.partial(input_grad_kernel, start, tile), in_spec...  4.73 us
    pallas_call x1, Pallas kernels, prepared(): pl.pallas_call(prepare_kernel, in_specs=[WHOLE] * len(pieces) + [STORED],...  3.51 us
  transfers between devices with their start and end apart: 39, of which 14 were waited for; matrix products, arithmetic and copies ran while one was open for 2% of the time, Pallas kernels for 22%

profile of v4, /device:TPU:0, one launch (start us, length us, event | category | flops | bytes accessed | tf_op | source)
XLA Modules:
  0.0 112.9 jit_solution(5550476976129260397)
XLA Ops:
  0.6 3.1 %collective-permute-start = (bf16[16,2048]{1,0:T(8,128)(2,1)}, bf16[16,2048]{1,0:T(8,128)(2,1)S(1)}, u32[]{:S(2)}, u32[]{:S(2)}) collective-permute-start(bf16[16,2048]{1,0:T(8,128)(2,1)} %refs_0_.1), channel_id=1, source_target_pairs={{0,2},{1,3},{2,0},{3,1},{4,6},{5,7},{6,4},{7,5},{8,10},{9,11},{10,... | collective-permute-start | bytes 196616 | tf_op jit(solution)/shard_map/ppermute | solution.py:372
  3.7 2.5 %collective-permute-start.2 = (bf16[16,2048]{1,0:T(8,128)(2,1)}, bf16[16,2048]{1,0:T(8,128)(2,1)S(1)}, u32[]{:S(2)}, u32[]{:S(2)}) collective-permute-start(bf16[16,2048]{1,0:T(8,128)(2,1)} %refs_0_.1), channel_id=1, source_target_pairs={{0,6},{1,7},{2,4},{3,5},{4,2},{5,3},{6,0},{7,1},{8,14},{9,15},{10,... | collective-permute-start | bytes 196616 | tf_op jit(solution)/shard_map/ppermute | solution.py:372
  7.2 3.6 %collective-permute-done.2.refs_3_ = bf16[16,2048]{1,0:T(8,128)(2,1)S(1)} collective-permute-done((bf16[16,2048]{1,0:T(8,128)(2,1)}, bf16[16,2048]{1,0:T(8,128)(2,1)S(1)}, u32[]{:S(2)}, u32[]{:S(2)}) %collective-permute-start.2) | collective-permute-done | bytes 65568 | tf_op jit(solution)/shard_map/ppermute | solution.py:372
  10.8 2.1 %collective-permute-done.1.refs_2_ = bf16[16,2048]{1,0:T(8,128)(2,1)S(1)} collective-permute-done((bf16[16,2048]{1,0:T(8,128)(2,1)}, bf16[16,2048]{1,0:T(8,128)(2,1)S(1)}, u32[]{:S(2)}, u32[]{:S(2)}) %collective-permute-start.1) | collective-permute-done | bytes 65568 | tf_op jit(solution)/shard_map/ppermute | solution.py:372
  12.9 2.5 %collective-permute-start.5 = (bf16[64,2048]{1,0:T(8,128)(2,1)S(1)}, bf16[64,2048]{1,0:T(8,128)(2,1)S(1)}, u32[]{:S(2)}, u32[]{:S(2)}) collective-permute-start(bf16[64,2048]{1,0:T(8,128)(2,1)S(1)} %shard_map.51.refs_0_), channel_id=1, source_target_pairs={{0,24},{8,16},{16,8},{24,0},{1,25},{9,17},{17,9},{25,1},{2,26},{10... | collective-permute-start | bytes 786440 | tf_op jit(solution)/shard_map/ppermute | solution.py:372
  16.5 1.8 %dynamic-slice_bitcast_fusion = (bf16[32,2048]{1,0:T(8,128)(2,1)S(1)}, bf16[32,2048]{1,0:T(8,128)(2,1)S(1)}, bf16[32,2048]{1,0:T(8,128)(2,1)S(1)}, bf16[32,2048]...) fusion(bf16[1,64,16384]{2,1,0:T(8,128)(2,1)} %param.5, ...), kind=kLoop, calls=%fused_computation | loop fusion | bytes 4194336 | tf_op jit(solution)/shard_map/squeeze | solution.py:402
  18.9 4.2 %collective-permute-done.5.refs_3_ = bf16[64,2048]{1,0:T(8,128)(2,1)S(1)} collective-permute-done((bf16[64,2048]{1,0:T(8,128)(2,1)S(1)}, bf16[64,2048]{1,0:T(8,128)(2,1)S(1)}, u32[]{:S(2)}, u32[]{:S(2)}) %collective-permute-start.5) | collective-permute-done | bytes 262176 | tf_op jit(solution)/shard_map/ppermute | solution.py:372
  23.1 4.6 %collective-permute-done.4.refs_2_ = bf16[64,2048]{1,0:T(8,128)(2,1)S(1)} collective-permute-done((bf16[64,2048]{1,0:T(8,128)(2,1)S(1)}, bf16[64,2048]{1,0:T(8,128)(2,1)S(1)}, u32[]{:S(2)}, u32[]{:S(2)}) %collective-permute-start.4) | collective-permute-done | bytes 262176 | tf_op jit(solution)/shard_map/ppermute | solution.py:372
  28.2 3.5 %prepare.1 = (f32[8,128]{1,0:T(8,128)S(1)}, bf16[2048,2048]{1,0:T(8,128)(2,1)S(1)}) custom-call(bf16[32,2048]{1,0:T(8,128)(2,1)S(1)} %get-tuple-element.39.refs_0_.refs_4_, bf16[32,2048]{1,0:T(8,128)(2,1)S(1)} %get-tuple-element.40.refs_1_, bf16[32,2048]{1,0:T(8,128)(2,1)S(1)} %get-tuple-element.41.refs_2_, bf16[32,2048]{1,0:T(8,128)(2,1)S(1)} %get-tuple-element.42.refs_3_, ...), custom_call_target="tpu_custom_call" | custom-call | flops 8388608 | bytes 16777216 | tf_op jit(solution)/shard_map/prepare/pallas_call | solution.py:65
  31.7 2.9 %collective-permute-done.22.refs_6_ = bf16[32,2048]{1,0:T(8,128)(2,1)S(1)} collective-permute-done((bf16[32,2048]{1,0:T(8,128)(2,1)S(1)}, bf16[32,2048]{1,0:T(8,128)(2,1)S(1)}, u32[]{:S(2)}, u32[]{:S(2)}) %collective-permute-start.22) | collective-permute-done | bytes 131104 | tf_op jit(solution)/shard_map/ppermute | solution.py:408
  34.6 1.5 %collective-permute-start.24 = (bf16[32,2048]{1,0:T(8,128)(2,1)S(1)}, bf16[32,2048]{1,0:T(8,128)(2,1)S(1)}, u32[]{:S(2)}, u32[]{:S(2)}) collective-permute-start(bf16[32,2048]{1,0:T(8,128)(2,1)S(1)} %get-tuple-element.43.refs_4_), channel_id=1, source_target_pairs={{0,6},{1,7},{2,4},{3,5},{4,2},{5,3},{6,0},{7,1},{8,14},{9,15},{10,... | collective-permute-start | bytes 393224 | tf_op jit(solution)/shard_map/ppermute | solution.py:408
  37.2 1.7 %collective-permute-start.26 = (bf16[32,2048]{1,0:T(8,128)(2,1)S(1)}, bf16[32,2048]{1,0:T(8,128)(2,1)S(1)}, u32[]{:S(2)}, u32[]{:S(2)}) collective-permute-start(bf16[32,2048]{1,0:T(8,128)(2,1)S(1)} %get-tuple-element.45.refs_6_), channel_id=1, source_target_pairs={{0,4},{1,5},{2,0},{3,1},{4,6},{5,7},{6,2},{7,3},{8,12},{9,13},{10,... | collective-permute-start | bytes 393224 | tf_op jit(solution)/shard_map/ppermute | solution.py:408
  39.9 6.6 %student.1 = (f32[512,2048]{1,0:T(8,128)S(1)}, bf16[512,2048]{1,0:T(8,128)(2,1)S(1)}, f32[8,512]{1,0:T(8,128)S(1)}) custom-call(bf16[64,2048]{1,0:T(8,128)(2,1)S(1)} %shard_map.51.refs_0_, bf16[64,2048]{1,0:T(8,128)(2,1)S(1)} %collective-permute-done.3.refs_1_, bf16[64,2048]{1,0:T(8,128)(2,1)S(1)} %collective-permute-done.4.refs_2_, ...), custom_call_target="tpu_custom_call" | custom-call | flops 4294967296 | bytes 12582912 | tf_op jit(solution)/shard_map/student/pallas_call | solution.py:130
  46.5 6.0 %collective-permute-done.23.refs_7_ = bf16[32,2048]{1,0:T(8,128)(2,1)S(1)} collective-permute-done((bf16[32,2048]{1,0:T(8,128)(2,1)S(1)}, bf16[32,2048]{1,0:T(8,128)(2,1)S(1)}, u32[]{:S(2)}, u32[]{:S(2)}) %collective-permute-start.23) | collective-permute-done | bytes 131104 | tf_op jit(solution)/shard_map/ppermute | solution.py:408
  53.7 2.0 %collective-permute-start.15 = (bf16[32,2048]{1,0:T(8,128)(2,1)S(1)}, bf16[32,2048]{1,0:T(8,128)(2,1)S(1)}, u32[]{:S(2)}, u32[]{:S(2)}) collective-permute-start(bf16[32,2048]{1,0:T(8,128)(2,1)S(1)} %get-tuple-element.49.refs_10_), channel_id=1, source_target_pairs={{0,2},{1,3},{2,6},{3,7},{4,0},{5,1},{6,4},{7,5},{8,10},{9,11},{10,... | collective-permute-start | bytes 393224 | tf_op jit(solution)/shard_map/ppermute | solution.py:408
  55.8 1.5 %collective-permute-start.13 = (f32[16,512]{1,0:T(8,128)S(1)}, f32[16,512]{1,0:T(8,128)S(1)}, u32[]{:S(2)}, u32[]{:S(2)}) collective-permute-start(f32[16,512]{1,0:T(8,128)S(1)} %shard_map.52.refs_0_), channel_id=1, source_target_pairs={{0,6},{1,7},{2,4},{3,5},{4,2},{5,3},{6,0},{7,1},{8,14},{9,15},{10,... | collective-permute-start | bytes 98312 | tf_op jit(solution)/shard_map/ppermute | solution.py:372
  57.3 2.3 %collective-permute-start.12 = (f32[16,512]{1,0:T(8,128)S(1)}, f32[16,512]{1,0:T(8,128)S(1)}, u32[]{:S(2)}, u32[]{:S(2)}) collective-permute-start(f32[16,512]{1,0:T(8,128)S(1)} %shard_map.52.refs_0_), channel_id=1, source_target_pairs={{0,4},{1,5},{2,6},{3,7},{4,0},{5,1},{6,2},{7,3},{8,12},{9,13},{10,... | collective-permute-start | bytes 98312 | tf_op jit(solution)/shard_map/ppermute | solution.py:372
  60.2 1.7 %collective-permute-done.13.refs_3_ = f32[16,512]{1,0:T(8,128)S(1)} collective-permute-done((f32[16,512]{1,0:T(8,128)S(1)}, f32[16,512]{1,0:T(8,128)S(1)}, u32[]{:S(2)}, u32[]{:S(2)}) %collective-permute-start.13) | collective-permute-done | bytes 32800 | tf_op jit(solution)/shard_map/ppermute | solution.py:372
  61.9 1.3 %collective-permute-done.12.refs_2_ = f32[16,512]{1,0:T(8,128)S(1)} collective-permute-done((f32[16,512]{1,0:T(8,128)S(1)}, f32[16,512]{1,0:T(8,128)S(1)}, u32[]{:S(2)}, u32[]{:S(2)}) %collective-permute-start.12) | collective-permute-done | bytes 32800 | tf_op jit(solution)/shard_map/ppermute | solution.py:372
  63.2 1.2 %collective-permute-start.17 = (bf16[32,2048]{1,0:T(8,128)(2,1)S(1)}, bf16[32,2048]{1,0:T(8,128)(2,1)S(1)}, u32[]{:S(2)}, u32[]{:S(2)}) collective-permute-start(bf16[32,2048]{1,0:T(8,128)(2,1)S(1)} %get-tuple-element.51.refs_12_), channel_id=1, source_target_pairs={{0,6},{1,7},{2,4},{3,5},{4,2},{5,3},{6,0},{7,1},{8,14},{9,15},{10,... | collective-permute-start | bytes 393224 | tf_op jit(solution)/shard_map/ppermute | solution.py:408
  64.4 1.9 %collective-permute-start.18 = (bf16[32,2048]{1,0:T(8,128)(2,1)S(1)}, bf16[32,2048]{1,0:T(8,128)(2,1)S(1)}, u32[]{:S(2)}, u32[]{:S(2)}) collective-permute-start(bf16[32,2048]{1,0:T(8,128)(2,1)S(1)} %get-tuple-element.52.refs_13_), channel_id=1, source_target_pairs={{0,7},{1,6},{2,5},{3,4},{4,3},{5,2},{6,1},{7,0},{8,15},{9,14},{10,... | collective-permute-start | bytes 393224 | tf_op jit(solution)/shard_map/ppermute | solution.py:408
  67.5 1.9 %collective-permute-start.20 = (bf16[32,2048]{1,0:T(8,128)(2,1)S(1)}, bf16[32,2048]{1,0:T(8,128)(2,1)S(1)}, u32[]{:S(2)}, u32[]{:S(2)}) collective-permute-start(bf16[32,2048]{1,0:T(8,128)(2,1)S(1)} %get-tuple-element.54.refs_15_), channel_id=1, source_target_pairs={{0,5},{1,4},{2,1},{3,0},{4,7},{5,6},{6,3},{7,2},{8,13},{9,12},{10,... | collective-permute-start | bytes 393224 | tf_op jit(solution)/shard_map/ppermute | solution.py:408
  69.3 2.4 %input_grad.2 = (f32[128,2048]{1,0:T(8,128)S(1)}, bf16[128,2048]{1,0:T(8,128)(2,1)S(1)}) custom-call(bf16[256,2048]{1,0:T(8,128)(2,1)S(1)} %logit_grad.2.refs_13_.g_ref, bf16[2048,2048]{1,0:T(8,128)(2,1)S(1)} %get-tuple-element.55.refs_8_.w_ref), custom_call_target="tpu_custom_call" | custom-call | flops 2147483648 | bytes 9437184 | tf_op jit(solution)/shard_map/input_grad/pallas_call | solution.py:238
  71.7 7.4 %collective-permute-done.16.refs_7_ = bf16[32,2048]{1,0:T(8,128)(2,1)S(1)} collective-permute-done((bf16[32,2048]{1,0:T(8,128)(2,1)S(1)}, bf16[32,2048]{1,0:T(8,128)(2,1)S(1)}, u32[]{:S(2)}, u32[]{:S(2)}) %collective-permute-start.16) | collective-permute-done | bytes 131104 | tf_op jit(solution)/shard_map/ppermute | solution.py:408
  80.2 2.4 %input_grad.3 = (f32[128,2048]{1,0:T(8,128)S(1)}, bf16[128,2048]{1,0:T(8,128)(2,1)S(1)}) custom-call(bf16[512,2048]{1,0:T(8,128)(2,1)S(1)} %logit_grad.3.g_ref, bf16[2048,2048]{1,0:T(8,128)(2,1)S(1)} %get-tuple-element.55.refs_8_.w_ref), custom_call_target="tpu_custom_call" | custom-call | flops 2147483648 | bytes 9437184 | tf_op jit(solution)/shard_map/input_grad/pallas_call | solution.py:238
  83.2 1.6 %collective-permute-start.29 = (bf16[32,2048]{1,0:T(8,128)(2,1)S(1)}, bf16[32,2048]{1,0:T(8,128)(2,1)S(1)}, u32[]{:S(2)}, u32[]{:S(2)}) collective-permute-start(bf16[32,2048]{1,0:T(8,128)(2,1)S(1)} %get-tuple-element.63), channel_id=1, source_target_pairs={{0,8},{8,0},{16,24},{24,16},{1,9},{9,1},{17,25},{25,17},{2,10},{10... | collective-permute-start | bytes 393224 | tf_op jit(solution)/shard_map/ppermute | solution.py:372
  87.5 1.6 %collective-permute-start.33 = (bf16[32,2048]{1,0:T(8,128)(2,1)S(1)}, bf16[32,2048]{1,0:T(8,128)(2,1)S(1)}, u32[]{:S(2)}, u32[]{:S(2)}) collective-permute-start(bf16[32,2048]{1,0:T(8,128)(2,1)S(1)} %get-tuple-element.69), channel_id=1, source_target_pairs={{0,8},{8,0},{16,24},{24,16},{1,9},{9,1},{17,25},{25,17},{2,10},{10... | collective-permute-start | bytes 393224 | tf_op jit(solution)/shard_map/ppermute | solution.py:372
  91.1 3.8 %weight_grad.2.refs_0_ = bf16[1,2048,2048]{2,1,0:T(8,128)(2,1)} custom-call(bf16[2048,512]{1,0:T(8,128)(2,1)S(1)} %turn.1.ht_ref, bf16[512,2048]{1,0:T(8,128)(2,1)S(1)} %logit_grad.3.g_ref), custom_call_target="tpu_custom_call" | custom-call | flops 2147483648 | bytes 4194304 | tf_op jit(solution)/shard_map/weight_grad/pallas_call | solution.py:339
  96.0 3.0 %collective-permute-done.34.refs_1_ = bf16[32,2048]{1,0:T(8,128)(2,1)S(1)} collective-permute-done((bf16[32,2048]{1,0:T(8,128)(2,1)S(1)}, bf16[32,2048]{1,0:T(8,128)(2,1)S(1)}, u32[]{:S(2)}, u32[]{:S(2)}) %collective-permute-start.34) | collective-permute-done | bytes 131104 | tf_op jit(solution)/shard_map/ppermute | solution.py:372
  99.1 5.6 %collective-permute-start.36 = (bf16[16,2048]{1,0:T(8,128)(2,1)S(1)}, bf16[16,2048]{1,0:T(8,128)(2,1)S(1)}, u32[]{:S(2)}, u32[]{:S(2)}) collective-permute-start(bf16[16,2048]{1,0:T(8,128)(2,1)S(1)} %get-tuple-element.73), channel_id=1, source_target_pairs={{0,2},{1,3},{2,0},{3,1},{4,6},{5,7},{6,4},{7,5},{8,10},{9,11},{10,... | collective-permute-start | bytes 196616 | tf_op jit(solution)/shard_map/ppermute | solution.py:372
  105.9 1.4 %collective-permute-start.38 = (bf16[16,2048]{1,0:T(8,128)(2,1)S(1)}, bf16[16,2048]{1,0:T(8,128)(2,1)S(1)}, u32[]{:S(2)}, u32[]{:S(2)}) collective-permute-start(bf16[16,2048]{1,0:T(8,128)(2,1)S(1)} %get-tuple-element.75), channel_id=1, source_target_pairs={{0,6},{1,7},{2,4},{3,5},{4,2},{5,3},{6,0},{7,1},{8,14},{9,15},{10,... | collective-permute-start | bytes 196616 | tf_op jit(solution)/shard_map/ppermute | solution.py:372
  107.3 3.8 %weight_grad.3 = bf16[1,2048,2048]{2,1,0:T(8,128)(2,1)} custom-call(bf16[2048,512]{1,0:T(8,128)(2,1)S(1)} %turn.1.ht_ref, bf16[512,2048]{1,0:T(8,128)(2,1)S(1)} %logit_grad.3.g_ref, bf16[1,2048,2048]{2,1,0:T(8,128)(2,1)} %weight_grad.2.refs_0_), custom_call_target="tpu_custom_call", output_to_operand_aliasing={{}: (2, {})} | custom-call | flops 2147483648 | bytes 4194304 | tf_op jit(solution)/shard_map/weight_grad/pallas_call | solution.py:339
  (67 shorter events, 18.6 us)
Async XLA Ops:
  0.6 6.6 %collective-permute-start = (bf16[16,2048]{1,0:T(8,128)(2,1)}, bf16[16,2048]{1,0:T(8,128)(2,1)S(1)}, u32[]{:S(2)}, u32[]{:S(2)}) collective-permute-start(bf16[16,2048]{1,0:T(8,128)(2,1)} %refs_0_.1), channel_id=1, source_target_pairs={{0,2},{1,3},{2,0},{3,1},{4,6},{5,7},{6,4},{7,5},{8,10},{9,11},{10,... | collective-permute-start | bytes 196616 | tf_op jit(solution)/shard_map/ppermute | solution.py:372
  3.7 7.1 %collective-permute-start.2 = (bf16[16,2048]{1,0:T(8,128)(2,1)}, bf16[16,2048]{1,0:T(8,128)(2,1)S(1)}, u32[]{:S(2)}, u32[]{:S(2)}) collective-permute-start(bf16[16,2048]{1,0:T(8,128)(2,1)} %refs_0_.1), channel_id=1, source_target_pairs={{0,6},{1,7},{2,4},{3,5},{4,2},{5,3},{6,0},{7,1},{8,14},{9,15},{10,... | collective-permute-start | bytes 196616 | tf_op jit(solution)/shard_map/ppermute | solution.py:372
  6.2 6.7 %collective-permute-start.1 = (bf16[16,2048]{1,0:T(8,128)(2,1)}, bf16[16,2048]{1,0:T(8,128)(2,1)S(1)}, u32[]{:S(2)}, u32[]{:S(2)}) collective-permute-start(bf16[16,2048]{1,0:T(8,128)(2,1)} %refs_0_.1), channel_id=1, source_target_pairs={{0,4},{1,5},{2,6},{3,7},{4,0},{5,1},{6,2},{7,3},{8,12},{9,13},{10,... | collective-permute-start | bytes 196616 | tf_op jit(solution)/shard_map/ppermute | solution.py:372
  12.9 10.2 %collective-permute-start.5 = (bf16[64,2048]{1,0:T(8,128)(2,1)S(1)}, bf16[64,2048]{1,0:T(8,128)(2,1)S(1)}, u32[]{:S(2)}, u32[]{:S(2)}) collective-permute-start(bf16[64,2048]{1,0:T(8,128)(2,1)S(1)} %shard_map.51.refs_0_), channel_id=1, source_target_pairs={{0,24},{8,16},{16,8},{24,0},{1,25},{9,17},{17,9},{25,1},{2,26},{10... | collective-permute-start | bytes 786440 | tf_op jit(solution)/shard_map/ppermute | solution.py:372
  15.4 12.2 %collective-permute-start.4 = (bf16[64,2048]{1,0:T(8,128)(2,1)S(1)}, bf16[64,2048]{1,0:T(8,128)(2,1)S(1)}, u32[]{:S(2)}, u32[]{:S(2)}) collective-permute-start(bf16[64,2048]{1,0:T(8,128)(2,1)S(1)} %shard_map.51.refs_0_), channel_id=1, source_target_pairs={{0,16},{8,24},{16,0},{24,8},{1,17},{9,25},{17,1},{25,9},{2,18},{10... | collective-permute-start | bytes 786440 | tf_op jit(solution)/shard_map/ppermute | solution.py:372
  15.9 11.8 %collective-permute-start.3 = (bf16[64,2048]{1,0:T(8,128)(2,1)S(1)}, bf16[64,2048]{1,0:T(8,128)(2,1)S(1)}, u32[]{:S(2)}, u32[]{:S(2)}) collective-permute-start(bf16[64,2048]{1,0:T(8,128)(2,1)S(1)} %shard_map.51.refs_0_), channel_id=1, source_target_pairs={{0,8},{8,0},{16,24},{24,16},{1,9},{9,1},{17,25},{25,17},{2,10},{10... | collective-permute-start | bytes 786440 | tf_op jit(solution)/shard_map/ppermute | solution.py:372
  18.3 9.9 %collective-permute-start.21 = (bf16[32,2048]{1,0:T(8,128)(2,1)S(1)}, bf16[32,2048]{1,0:T(8,128)(2,1)S(1)}, u32[]{:S(2)}, u32[]{:S(2)}) collective-permute-start(bf16[32,2048]{1,0:T(8,128)(2,1)S(1)} %get-tuple-element.40.refs_1_), channel_id=1, source_target_pairs={{0,1},{1,0},{2,3},{3,2},{4,5},{5,4},{6,7},{7,6},{8,9},{9,8},{10,11... | collective-permute-start | bytes 393224 | tf_op jit(solution)/shard_map/ppermute | solution.py:408
  18.4 16.2 %collective-permute-start.6 = (bf16[64,2048]{1,0:T(8,128)(2,1)S(1)}, bf16[64,2048]{1,0:T(8,128)(2,1)S(1)}, u32[]{:S(2)}, u32[]{:S(2)}) collective-permute-start(bf16[64,2048]{1,0:T(8,128)(2,1)S(1)} %shard_map.51.refs_0_), channel_id=1, source_target_pairs={{0,1},{1,0},{2,3},{3,2},{4,5},{5,4},{6,7},{7,6},{8,9},{9,8},{10,11... | collective-permute-start | bytes 786440 | tf_op jit(solution)/shard_map/ppermute | solution.py:372
  23.1 13.0 %collective-permute-start.9 = (bf16[64,2048]{1,0:T(8,128)(2,1)S(1)}, bf16[64,2048]{1,0:T(8,128)(2,1)S(1)}, u32[]{:S(2)}, u32[]{:S(2)}) collective-permute-start(bf16[64,2048]{1,0:T(8,128)(2,1)S(1)} %collective-permute-done.5.refs_3_), channel_id=1, source_target_pairs={{0,1},{1,0},{2,3},{3,2},{4,5},{5,4},{6,7},{7,6},{8,9},{9,8},{10,11... | collective-permute-start | bytes 786440 | tf_op jit(solution)/shard_map/ppermute | solution.py:372
  27.7 9.6 %collective-permute-start.8 = (bf16[64,2048]{1,0:T(8,128)(2,1)S(1)}, bf16[64,2048]{1,0:T(8,128)(2,1)S(1)}, u32[]{:S(2)}, u32[]{:S(2)}) collective-permute-start(bf16[64,2048]{1,0:T(8,128)(2,1)S(1)} %collective-permute-done.4.refs_2_), channel_id=1, source_target_pairs={{0,1},{1,0},{2,3},{3,2},{4,5},{5,4},{6,7},{7,6},{8,9},{9,8},{10,11... | collective-permute-start | bytes 786440 | tf_op jit(solution)/shard_map/ppermute | solution.py:372
  27.8 11.2 %collective-permute-start.7 = (bf16[64,2048]{1,0:T(8,128)(2,1)S(1)}, bf16[64,2048]{1,0:T(8,128)(2,1)S(1)}, u32[]{:S(2)}, u32[]{:S(2)}) collective-permute-start(bf16[64,2048]{1,0:T(8,128)(2,1)S(1)} %collective-permute-done.3.refs_1_), channel_id=1, source_target_pairs={{0,1},{1,0},{2,3},{3,2},{4,5},{5,4},{6,7},{7,6},{8,9},{9,8},{10,11... | collective-permute-start | bytes 786440 | tf_op jit(solution)/shard_map/ppermute | solution.py:372
  28.2 6.4 %collective-permute-start.22 = (bf16[32,2048]{1,0:T(8,128)(2,1)S(1)}, bf16[32,2048]{1,0:T(8,128)(2,1)S(1)}, u32[]{:S(2)}, u32[]{:S(2)}) collective-permute-start(bf16[32,2048]{1,0:T(8,128)(2,1)S(1)} %get-tuple-element.41.refs_2_), channel_id=1, source_target_pairs={{0,2},{1,3},{2,6},{3,7},{4,0},{5,1},{6,4},{7,5},{8,10},{9,11},{10,... | collective-permute-start | bytes 393224 | tf_op jit(solution)/shard_map/ppermute | solution.py:408
  34.6 18.0 %collective-permute-start.23 = (bf16[32,2048]{1,0:T(8,128)(2,1)S(1)}, bf16[32,2048]{1,0:T(8,128)(2,1)S(1)}, u32[]{:S(2)}, u32[]{:S(2)}) collective-permute-start(bf16[32,2048]{1,0:T(8,128)(2,1)S(1)} %get-tuple-element.42.refs_3_), channel_id=1, source_target_pairs={{0,3},{1,2},{2,7},{3,6},{4,1},{5,0},{6,5},{7,4},{8,11},{9,10},{10,... | collective-permute-start | bytes 393224 | tf_op jit(solution)/shard_map/ppermute | solution.py:408
  34.6 18.0 %collective-permute-start.24 = (bf16[32,2048]{1,0:T(8,128)(2,1)S(1)}, bf16[32,2048]{1,0:T(8,128)(2,1)S(1)}, u32[]{:S(2)}, u32[]{:S(2)}) collective-permute-start(bf16[32,2048]{1,0:T(8,128)(2,1)S(1)} %get-tuple-element.43.refs_4_), channel_id=1, source_target_pairs={{0,6},{1,7},{2,4},{3,5},{4,2},{5,3},{6,0},{7,1},{8,14},{9,15},{10,... | collective-permute-start | bytes 393224 | tf_op jit(solution)/shard_map/ppermute | solution.py:408
  36.1 19.6 %collective-permute-start.25 = (bf16[32,2048]{1,0:T(8,128)(2,1)S(1)}, bf16[32,2048]{1,0:T(8,128)(2,1)S(1)}, u32[]{:S(2)}, u32[]{:S(2)}) collective-permute-start(bf16[32,2048]{1,0:T(8,128)(2,1)S(1)} %get-tuple-element.44.refs_5_), channel_id=1, source_target_pairs={{0,7},{1,6},{2,5},{3,4},{4,3},{5,2},{6,1},{7,0},{8,15},{9,14},{10,... | collective-permute-start | bytes 393224 | tf_op jit(solution)/shard_map/ppermute | solution.py:408
  37.2 20.0 %collective-permute-start.26 = (bf16[32,2048]{1,0:T(8,128)(2,1)S(1)}, bf16[32,2048]{1,0:T(8,128)(2,1)S(1)}, u32[]{:S(2)}, u32[]{:S(2)}) collective-permute-start(bf16[32,2048]{1,0:T(8,128)(2,1)S(1)} %get-tuple-element.45.refs_6_), channel_id=1, source_target_pairs={{0,4},{1,5},{2,0},{3,1},{4,6},{5,7},{6,2},{7,3},{8,12},{9,13},{10,... | collective-permute-start | bytes 393224 | tf_op jit(solution)/shard_map/ppermute | solution.py:408
  39.0 20.6 %collective-permute-start.27 = (bf16[32,2048]{1,0:T(8,128)(2,1)S(1)}, bf16[32,2048]{1,0:T(8,128)(2,1)S(1)}, u32[]{:S(2)}, u32[]{:S(2)}) collective-permute-start(bf16[32,2048]{1,0:T(8,128)(2,1)S(1)} %get-tuple-element.46.refs_7_), channel_id=1, source_target_pairs={{0,5},{1,4},{2,1},{3,0},{4,7},{5,6},{6,3},{7,2},{8,13},{9,12},{10,... | collective-permute-start | bytes 393224 | tf_op jit(solution)/shard_map/ppermute | solution.py:408
  52.6 14.8 %collective-permute-start.14 = (bf16[32,2048]{1,0:T(8,128)(2,1)S(1)}, bf16[32,2048]{1,0:T(8,128)(2,1)S(1)}, u32[]{:S(2)}, u32[]{:S(2)}) collective-permute-start(bf16[32,2048]{1,0:T(8,128)(2,1)S(1)} %get-tuple-element.48.refs_9_), channel_id=1, source_target_pairs={{0,1},{1,0},{2,3},{3,2},{4,5},{5,4},{6,7},{7,6},{8,9},{9,8},{10,11... | collective-permute-start | bytes 393224 | tf_op jit(solution)/shard_map/ppermute | solution.py:408
  53.7 13.7 %collective-permute-start.15 = (bf16[32,2048]{1,0:T(8,128)(2,1)S(1)}, bf16[32,2048]{1,0:T(8,128)(2,1)S(1)}, u32[]{:S(2)}, u32[]{:S(2)}) collective-permute-start(bf16[32,2048]{1,0:T(8,128)(2,1)S(1)} %get-tuple-element.49.refs_10_), channel_id=1, source_target_pairs={{0,2},{1,3},{2,6},{3,7},{4,0},{5,1},{6,4},{7,5},{8,10},{9,11},{10,... | collective-permute-start | bytes 393224 | tf_op jit(solution)/shard_map/ppermute | solution.py:408
  61.9 17.2 %collective-permute-start.16 = (bf16[32,2048]{1,0:T(8,128)(2,1)S(1)}, bf16[32,2048]{1,0:T(8,128)(2,1)S(1)}, u32[]{:S(2)}, u32[]{:S(2)}) collective-permute-start(bf16[32,2048]{1,0:T(8,128)(2,1)S(1)} %get-tuple-element.50.refs_11_), channel_id=1, source_target_pairs={{0,3},{1,2},{2,7},{3,6},{4,1},{5,0},{6,5},{7,4},{8,11},{9,10},{10,... | collective-permute-start | bytes 393224 | tf_op jit(solution)/shard_map/ppermute | solution.py:408
  63.2 15.9 %collective-permute-start.17 = (bf16[32,2048]{1,0:T(8,128)(2,1)S(1)}, bf16[32,2048]{1,0:T(8,128)(2,1)S(1)}, u32[]{:S(2)}, u32[]{:S(2)}) collective-permute-start(bf16[32,2048]{1,0:T(8,128)(2,1)S(1)} %get-tuple-element.51.refs_12_), channel_id=1, source_target_pairs={{0,6},{1,7},{2,4},{3,5},{4,2},{5,3},{6,0},{7,1},{8,14},{9,15},{10,... | collective-permute-start | bytes 393224 | tf_op jit(solution)/shard_map/ppermute | solution.py:408
  64.4 14.7 %collective-permute-start.18 = (bf16[32,2048]{1,0:T(8,128)(2,1)S(1)}, bf16[32,2048]{1,0:T(8,128)(2,1)S(1)}, u32[]{:S(2)}, u32[]{:S(2)}) collective-permute-start(bf16[32,2048]{1,0:T(8,128)(2,1)S(1)} %get-tuple-element.52.refs_13_), channel_id=1, source_target_pairs={{0,7},{1,6},{2,5},{3,4},{4,3},{5,2},{6,1},{7,0},{8,15},{9,14},{10,... | collective-permute-start | bytes 393224 | tf_op jit(solution)/shard_map/ppermute | solution.py:408
  67.4 11.8 %collective-permute-start.19 = (bf16[32,2048]{1,0:T(8,128)(2,1)S(1)}, bf16[32,2048]{1,0:T(8,128)(2,1)S(1)}, u32[]{:S(2)}, u32[]{:S(2)}) collective-permute-start(bf16[32,2048]{1,0:T(8,128)(2,1)S(1)} %get-tuple-element.53.refs_14_), channel_id=1, source_target_pairs={{0,4},{1,5},{2,0},{3,1},{4,6},{5,7},{6,2},{7,3},{8,12},{9,13},{10,... | collective-permute-start | bytes 393224 | tf_op jit(solution)/shard_map/ppermute | solution.py:408
  67.5 11.7 %collective-permute-start.20 = (bf16[32,2048]{1,0:T(8,128)(2,1)S(1)}, bf16[32,2048]{1,0:T(8,128)(2,1)S(1)}, u32[]{:S(2)}, u32[]{:S(2)}) collective-permute-start(bf16[32,2048]{1,0:T(8,128)(2,1)S(1)} %get-tuple-element.54.refs_15_), channel_id=1, source_target_pairs={{0,5},{1,4},{2,1},{3,0},{4,7},{5,6},{6,3},{7,2},{8,13},{9,12},{10,... | collective-permute-start | bytes 393224 | tf_op jit(solution)/shard_map/ppermute | solution.py:408
  83.2 6.7 %collective-permute-start.29 = (bf16[32,2048]{1,0:T(8,128)(2,1)S(1)}, bf16[32,2048]{1,0:T(8,128)(2,1)S(1)}, u32[]{:S(2)}, u32[]{:S(2)}) collective-permute-start(bf16[32,2048]{1,0:T(8,128)(2,1)S(1)} %get-tuple-element.63), channel_id=1, source_target_pairs={{0,8},{8,0},{16,24},{24,16},{1,9},{9,1},{17,25},{25,17},{2,10},{10... | collective-permute-start | bytes 393224 | tf_op jit(solution)/shard_map/ppermute | solution.py:372
  85.3 9.6 %collective-permute-start.30 = (bf16[32,2048]{1,0:T(8,128)(2,1)S(1)}, bf16[32,2048]{1,0:T(8,128)(2,1)S(1)}, u32[]{:S(2)}, u32[]{:S(2)}) collective-permute-start(bf16[32,2048]{1,0:T(8,128)(2,1)S(1)} %get-tuple-element.64), channel_id=1, source_target_pairs={{0,16},{8,24},{16,0},{24,8},{1,17},{9,25},{17,1},{25,9},{2,18},{10... | collective-permute-start | bytes 393224 | tf_op jit(solution)/shard_map/ppermute | solution.py:372
  86.2 8.7 %collective-permute-start.31 = (bf16[32,2048]{1,0:T(8,128)(2,1)S(1)}, bf16[32,2048]{1,0:T(8,128)(2,1)S(1)}, u32[]{:S(2)}, u32[]{:S(2)}) collective-permute-start(bf16[32,2048]{1,0:T(8,128)(2,1)S(1)} %get-tuple-element.65), channel_id=1, source_target_pairs={{0,24},{8,16},{16,8},{24,0},{1,25},{9,17},{17,9},{25,1},{2,26},{10... | collective-permute-start | bytes 393224 | tf_op jit(solution)/shard_map/ppermute | solution.py:372
  87.5 8.5 %collective-permute-start.33 = (bf16[32,2048]{1,0:T(8,128)(2,1)S(1)}, bf16[32,2048]{1,0:T(8,128)(2,1)S(1)}, u32[]{:S(2)}, u32[]{:S(2)}) collective-permute-start(bf16[32,2048]{1,0:T(8,128)(2,1)S(1)} %get-tuple-element.69), channel_id=1, source_target_pairs={{0,8},{8,0},{16,24},{24,16},{1,9},{9,1},{17,25},{25,17},{2,10},{10... | collective-permute-start | bytes 393224 | tf_op jit(solution)/shard_map/ppermute | solution.py:372
  89.1 9.9 %collective-permute-start.34 = (bf16[32,2048]{1,0:T(8,128)(2,1)S(1)}, bf16[32,2048]{1,0:T(8,128)(2,1)S(1)}, u32[]{:S(2)}, u32[]{:S(2)}) collective-permute-start(bf16[32,2048]{1,0:T(8,128)(2,1)S(1)} %get-tuple-element.70), channel_id=1, source_target_pairs={{0,16},{8,24},{16,0},{24,8},{1,17},{9,25},{17,1},{25,9},{2,18},{10... | collective-permute-start | bytes 393224 | tf_op jit(solution)/shard_map/ppermute | solution.py:372
  89.9 9.1 %collective-permute-start.35 = (bf16[32,2048]{1,0:T(8,128)(2,1)S(1)}, bf16[32,2048]{1,0:T(8,128)(2,1)S(1)}, u32[]{:S(2)}, u32[]{:S(2)}) collective-permute-start(bf16[32,2048]{1,0:T(8,128)(2,1)S(1)} %get-tuple-element.71), channel_id=1, source_target_pairs={{0,24},{8,16},{16,8},{24,0},{1,25},{9,17},{17,9},{25,1},{2,26},{10... | collective-permute-start | bytes 393224 | tf_op jit(solution)/shard_map/ppermute | solution.py:372
  99.1 12.0 %collective-permute-start.36 = (bf16[16,2048]{1,0:T(8,128)(2,1)S(1)}, bf16[16,2048]{1,0:T(8,128)(2,1)S(1)}, u32[]{:S(2)}, u32[]{:S(2)}) collective-permute-start(bf16[16,2048]{1,0:T(8,128)(2,1)S(1)} %get-tuple-element.73), channel_id=1, source_target_pairs={{0,2},{1,3},{2,0},{3,1},{4,6},{5,7},{6,4},{7,5},{8,10},{9,11},{10,... | collective-permute-start | bytes 196616 | tf_op jit(solution)/shard_map/ppermute | solution.py:372
  104.7 7.5 %collective-permute-start.37 = (bf16[16,2048]{1,0:T(8,128)(2,1)S(1)}, bf16[16,2048]{1,0:T(8,128)(2,1)S(1)}, u32[]{:S(2)}, u32[]{:S(2)}) collective-permute-start(bf16[16,2048]{1,0:T(8,128)(2,1)S(1)} %get-tuple-element.74), channel_id=1, source_target_pairs={{0,4},{1,5},{2,6},{3,7},{4,0},{5,1},{6,2},{7,3},{8,12},{9,13},{10,... | collective-permute-start | bytes 196616 | tf_op jit(solution)/shard_map/ppermute | solution.py:372
  (8 other events, 34.1 us)
